TPU v7x, 32 devices: a whole 2x2x4 slice. The times are simulated.
32 devices in a mesh: groups: 2 (over y), chain: 4 (over z), samp: 4 (over x, core).
Axes of the slice: x: 2, y: 2, z: 4, core: 2. Of those that a mesh axis runs over, the one named last changes fastest.
Arguments:
- dosage: bfloat16 [16384, 4096], P('samp', ('groups', 'chain')), parts along dimension 1
- filter_mask: int32 [4096], P(('groups', 'chain')), parts along dimension 0, may hold values 0 or 1
- counts: int32 [8], P(('groups', 'chain')), parts along dimension 0, may hold values from 128 to 512, as said below
Outputs:
- ld_tiles: float32 [8, 512, 3, 512], P(('groups', 'chain'), 'samp'), parts along dimension 0
There are 2 independent parts, one for each index of `groups`. A program takes and returns all parts, laid end to end along the dimension named above; each array names one. Nothing has to cross between parts.
Inputs may be any that keep to these rules, and one draw needn't show every extreme that they name: `counts`: every block but the last holds 512 live variants; the last holds from 128 to 512.
All inputs are finite; a program needn't handle non-finite values. No bound on the sum of `filter_mask` on one device may be relied on, other than what follows from the above.
Results may differ from a plain program's by a relative error of at most 0.0013.
Values may be sent and summed in bfloat16 or wider, within the bound.
No kernel may reach another device: no remote copies, remote signals or barrier semaphores. Data moves between devices by JAX's collectives and lax.ppermute only.
A program may use at most 64 MiB of HBM per device.

v0:
```python
import jax
import jax.numpy as jnp
from jax import lax
from jax.sharding import PartitionSpec as P


def shifted(array, axis, by):
    devices = lax.axis_size(axis)
    pairs = [(i, i + by) for i in range(devices) if 0 <= i + by < devices]
    return lax.ppermute(array, axis, pairs)


def body(dosage, filter_mask, counts):
    local_rows, width = dosage.shape
    samples = local_rows * lax.axis_size("samp")
    values = dosage.astype(jnp.float32)
    totals, squares = lax.psum((jnp.sum(values, 0), jnp.sum(values * values, 0)), "samp")
    mean = totals / samples
    var = squares / samples - mean * mean
    live = (jnp.arange(width, dtype=jnp.int32) < counts[0]).astype(jnp.float32)
    keep = filter_mask.astype(jnp.float32) * live
    scaled = ((values - mean) * lax.rsqrt(var + 1e-05) * keep).astype(jnp.bfloat16)
    nearer = shifted(scaled, "chain", -1)
    farther = shifted(scaled, "chain", -2)
    pieces = [
        lax.dot_general(scaled, other, (((0,), (0,)), ((), ())), preferred_element_type=jnp.float32)
        for other in (scaled, nearer, farther)
    ]
    tiles = lax.psum_scatter(
        jnp.stack(pieces, 1) / samples, "samp", scatter_dimension=0, tiled=True
    )
    return tiles[None]


def solution(mesh):
    in_specs = (P("samp", ("groups", "chain")), P(("groups", "chain")), P(("groups", "chain")))
    out_specs = P(("groups", "chain"), "samp", None, None)
    return jax.shard_map(body, mesh=mesh, in_specs=in_specs, out_specs=out_specs, check_vma=False)
```

profile of v0, /device:TPU:0, one launch (start us, length us, event | category | flops | bytes accessed | tf_op | source)
XLA Modules:
  0.0 343.6 jit_solution(13362100987524406571)
XLA Ops:
  6.5 0.0 copy-start
  6.5 0.0 reduce-scatter.2.cloned.1.call-start
  6.5 3.3 convert_reduce_fusion
  10.5 8.4 %all-reduce = (f32[512]{0:T(512)S(1)}, f32[512]{0:T(512)S(1)}) all-reduce(f32[512]{0:T(512)S(1)} %get-tuple-element.6, f32[512]{0:T(512)S(1)} %get-tuple-element.5), channel_id=1, replica_groups=mesh['groups'=2,'chain'=4,'samp'=4] {'samp'}, use_global_device_ids=true, to_apply=%region_3.0 | all-reduce | flops 1024 | bytes 8192 | tf_op jit(solution)/shard_map/psum | solution.py:17
  18.9 0.0 copy-done
  18.9 3.5 %fusion.2 = bf16[4096,512]{1,0:T(8,128)(2,1)S(1)} fusion(bf16[4096,512]{1,0:T(8,128)(2,1)} %param.3, f32[512]{0:T(512)S(1)} %get-tuple-element.11, f32[512]{0:T(512)S(1)} %get-tuple-element.10, f32[512]{0:T(512)S(1)} %get-tuple-element.9), kind=kLoop, calls=%fused_computation.5 | loop fusion | flops 10485760 | bytes 8394752 | tf_op jit(solution)/shard_map/convert_element_type | solution.py:22
  22.4 1.3 collective-permute-start
  23.7 1.3 collective-permute-start.1
  25.0 2.4 convolution_bitcast_fusion.2
  27.4 88.6 %collective-permute-done = bf16[4096,512]{1,0:T(8,128)(2,1)S(1)} collective-permute-done((bf16[4096,512]{1,0:T(8,128)(2,1)S(1)}, bf16[4096,512]{1,0:T(8,128)(2,1)S(1)}, u32[]{:S(2)}, u32[]{:S(2)}) %collective-permute-start) | collective-permute-done | bytes 4194336 | tf_op jit(solution)/shard_map/ppermute | solution.py:10
  116.0 2.3 convolution_bitcast_fusion.1
  118.4 177.8 %collective-permute-done.1 = bf16[4096,512]{1,0:T(8,128)(2,1)S(1)} collective-permute-done((bf16[4096,512]{1,0:T(8,128)(2,1)S(1)}, bf16[4096,512]{1,0:T(8,128)(2,1)S(1)}, u32[]{:S(2)}, u32[]{:S(2)}) %collective-permute-start.1) | collective-permute-done | bytes 4194336 | tf_op jit(solution)/shard_map/ppermute | solution.py:10
  296.2 2.4 convolution_bitcast_fusion
  298.6 2.0 maximum_multiply_fusion
  300.6 0.0 reduce-scatter.2.cloned.1.call-update
  300.6 36.1 %reduce-scatter.2.cloned.1.call-done = f32[128,3,512]{2,0,1:T(8,128)} async-done(((f32[512,3,512]{2,0,1:T(8,128)}), f32[128,3,512]{2,0,1:T(8,128)}) %reduce-scatter.2.cloned.1.call-update) | async-done | bytes 786448 | tf_op jit(solution)/shard_map/reduce_scatter | solution.py:29
  (1 shorter events, 0.0 us)
Async XLA Ops:
  6.5 12.4 %copy-start = (s32[512]{0:T(512)S(1)}, s32[512]{0:T(512)}, u32[]{:S(2)}) copy-start(s32[512]{0:T(512)} %param.4) | copy-start | bytes 6148
  6.5 330.2 %reduce-scatter.2.cloned.1.call-start = ((), (), s32[]{:S(2)}) async-start(), calls=%async_computation.1 | async-start | bytes 3932160 | tf_op jit(solution)/shard_map/reduce_scatter | solution.py:29
  22.4 93.6 %collective-permute-start = (bf16[4096,512]{1,0:T(8,128)(2,1)S(1)}, bf16[4096,512]{1,0:T(8,128)(2,1)S(1)}, u32[]{:S(2)}, u32[]{:S(2)}) collective-permute-start(bf16[4096,512]{1,0:T(8,128)(2,1)S(1)} %fusion.2), channel_id=1, source_target_pairs={{4,0},{8,4},{12,8},{5,1},{9,5},{13,9},{6,2},{10,6},{14,10},{7,3},{... | collective-permute-start | bytes 12582920 | tf_op jit(solution)/shard_map/ppermute | solution.py:10
  23.7 272.5 %collective-permute-start.1 = (bf16[4096,512]{1,0:T(8,128)(2,1)S(1)}, bf16[4096,512]{1,0:T(8,128)(2,1)S(1)}, u32[]{:S(2)}, u32[]{:S(2)}) collective-permute-start(bf16[4096,512]{1,0:T(8,128)(2,1)S(1)} %fusion.2), channel_id=1, source_target_pairs={{8,0},{12,4},{9,1},{13,5},{10,2},{14,6},{11,3},{15,7},{24,16},{28,... | collective-permute-start | bytes 12582920 | tf_op jit(solution)/shard_map/ppermute | solution.py:10
Sparse Core Ops, SparseCore 0:
  300.8 35.9 reduce-scatter.1
where the time goes:
time: 344 us
  waiting for transfers between devices  303 us (88%)
  between operations  14.1 us (4%)
  other arithmetic  8.9 us (3%)
  blocking collectives  8.37 us (2%)
  matrix products  7.05 us (2%)
    ppermute x2, waiting for transfers between devices, shifted(): return lax.ppermute(array, axis, pairs)  266 us
    reduce_scatter x1, waiting for transfers between devices, body(): lax.psum_scatter(jnp.stack(pieces, 1) / samples, 'samp', scatter_dimensio...  36.1 us
    psum x1, blocking collectives, body(): lax.psum((jnp.sum(values, 0), jnp.sum(values * values, 0)), 'samp')  8.37 us
    dot_general x3, matrix products, body(): lax.dot_general(scaled, other, (((0,), (0,)), ((), ())), preferred_elemen...  7.05 us
  transfers between devices with their start and end apart: 3, of which 3 were waited for; matrix products, arithmetic and copies ran while one was open for 1% of the time, Pallas kernels for 0%

commit v1 on v0

v1 whole, which is shorter than its diff:
```python
import jax
import jax.numpy as jnp
from jax import lax
from jax.sharding import PartitionSpec as P


LANES = 128


def edges(devices, first):
    pairs = []
    for low in range(first, devices - 1, 2):
        pairs += [(low, low + 1), (low + 1, low)]
    return pairs


def exchange(array, devices, first):
    pairs = edges(devices, first)
    if not pairs:
        return jnp.zeros_like(array)
    return lax.ppermute(array, "chain", pairs)


def partner(devices, me, step):
    if devices & (devices - 1) == 0:
        return me ^ step, [(i, i ^ step) for i in range(devices)]
    return (me + step) % devices, [(i, (i + step) % devices) for i in range(devices)]


def scatter_sum(parts, me, devices):
    own = lax.dynamic_index_in_dim(parts, me, 0, False)
    for step in range(1, devices):
        target, pairs = partner(devices, me, step)
        own = own + lax.ppermute(lax.dynamic_index_in_dim(parts, target, 0, False), "samp", pairs)
    return own


def dot(left, right):
    return lax.dot_general(left, right, (((0,), (0,)), ((), ())), preferred_element_type=jnp.float32)


def standardize(values, mean, scale):
    return ((values.astype(jnp.float32) - mean) * scale).astype(jnp.bfloat16)


def body(dosage, filter_mask, counts):
    chain, samp = lax.axis_size("chain"), lax.axis_size("samp")
    me, block = lax.axis_index("samp"), lax.axis_index("chain")
    even = block % 2 == 0
    local_rows, width = dosage.shape
    samples = local_rows * samp
    step = LANES if width % LANES == 0 else width
    starts = list(range(0, width, step))
    part = width // samp

    raw = []
    for c in starts:
        piece = dosage[:, c : c + step]
        a = exchange(piece, chain, 0)
        b = exchange(piece, chain, 1)
        raw.append((a, b))

    values = dosage.astype(jnp.float32)
    totals, squares = lax.psum((jnp.sum(values, 0), jnp.sum(values * values, 0)), "samp")
    mean = totals / samples
    var = squares / samples - mean * mean
    live = (jnp.arange(width, dtype=jnp.int32) < counts[0]).astype(jnp.float32)
    keep = filter_mask.astype(jnp.float32) * live
    stats = jnp.stack([mean, lax.rsqrt(var + 1e-05) * keep])
    sa = exchange(stats, chain, 0)
    sb = exchange(stats, chain, 1)
    after = jnp.where(even, sa, sb)
    before = jnp.where(even, sb, sa)

    own = standardize(dosage, stats[0], stats[1])
    tile = scatter_sum(dot(own, own).reshape(samp, part, width), me, samp)
    near, far = [], []
    befores, afters = [], []
    for j, c in enumerate(starts):
        a, b = raw[j]
        cols = slice(c, c + step)
        afters.append(standardize(jnp.where(even, a, b), after[0, cols], after[1, cols]))
        befores.append(standardize(jnp.where(even, b, a), before[0, cols], before[1, cols]))
        piece = dot(own, afters[j])
        near.append(scatter_sum(piece.reshape(samp, part, step), me, samp))
    after_all = jnp.concatenate(afters, 1)
    before_all = jnp.concatenate(befores, 1)
    for j, c in enumerate(starts):
        piece = dot(before_all, afters[j])
        far.append(scatter_sum(piece.reshape(samp, part, step), me, samp))
    far = jnp.concatenate(far, 1)
    far = lax.ppermute(far, "chain", [(i + 1, i) for i in range(chain - 1)])
    out = jnp.stack([tile, jnp.concatenate(near, 1), far], 1) / samples
    return out[None]


def solution(mesh):
    in_specs = (P("samp", ("groups", "chain")), P(("groups", "chain")), P(("groups", "chain")))
    out_specs = P(("groups", "chain"), "samp", None, None)
    return jax.shard_map(body, mesh=mesh, in_specs=in_specs, out_specs=out_specs, check_vma=False)
```

time: 344 us -> 154 us (0.45)
  waiting for transfers between devices: 303 us -> 67 us
  starting transfers between devices: 2.59 us -> 49.2 us
  between operations: 14.1 us -> 1.07 us
  matrix products: 7.05 us -> 19.6 us
  local copies, waits for them, and re-layouts: 0.01 us -> 5.6 us
  other arithmetic: 8.9 us -> 4.99 us
    ppermute x2 -> x38, waiting for transfers between devices: 266 us -> 67 us  [the longest x10 43.9 us: exchange(): return lax.ppermute(array, 'chain', pairs)]
    ppermute x2 -> x38, starting transfers between devices: 2.58 us -> 49.2 us  [the longest x10 26.8 us: exchange(): return lax.ppermute(array, 'chain', pairs)]
    reduce_scatter x1 -> x0, waiting for transfers between devices: 36.1 us -> none  [body(): lax.psum_scatter(jnp.stack(pieces, 1) / samples, 'samp', scatter_dimensio...]
    dot_general x3 -> x9, matrix products: 7.05 us -> 19.6 us  [dot(): lax.dot_general(left, right, (((0,), (0,)), ((), ())), preferred_element_...]
    slice x0 -> x1, local copies, waits for them, and re-layouts: none -> 4.46 us  [body(): piece = dosage[:, c:c + step]]
  transfers between devices with their start and end apart: 3 -> 38, of which waited for: 3 -> 14; matrix products, arithmetic and copies ran while one was open for 1% -> 16% of each run, Pallas kernels for 0% -> 0%
where the time goes in v1:
time: 154 us
  waiting for transfers between devices  67 us (44%)
  starting transfers between devices  49.2 us (32%)
  matrix products  19.6 us (13%)
  blocking collectives  6.6 us (4%)
  local copies, waits for them, and re-layouts  5.6 us (4%)
  other arithmetic  4.99 us (3%)
    ppermute x10, waiting for transfers between devices, exchange(): return lax.ppermute(array, 'chain', pairs)  43.9 us
    ppermute x10, starting transfers between devices, exchange(): return lax.ppermute(array, 'chain', pairs)  26.8 us
    ppermute x27, starting transfers between devices, scatter_sum(): lax.ppermute(lax.dynamic_index_in_dim(parts, target, 0, False), 'samp', p...  21 us
    dot_general x9, matrix products, dot(): lax.dot_general(left, right, (((0,), (0,)), ((), ())), preferred_element_...  19.6 us
    ppermute x27, waiting for transfers between devices, scatter_sum(): lax.ppermute(lax.dynamic_index_in_dim(parts, target, 0, False), 'samp', p...  15.6 us
    ppermute x1, waiting for transfers between devices, body(): far = lax.ppermute(far, 'chain', [(i + 1, i) for i in range(chain - 1)])  7.52 us
    psum x1, blocking collectives, body(): lax.psum((jnp.sum(values, 0), jnp.sum(values * values, 0)), 'samp')  6.6 us
    slice x1, local copies, waits for them, and re-layouts, body(): piece = dosage[:, c:c + step]  4.46 us
  transfers between devices with their start and end apart: 38, of which 14 were waited for; matrix products, arithmetic and copies ran while one was open for 16% of the time, Pallas kernels for 0%

profile of v1, /device:TPU:0, one launch (start us, length us, event | category | flops | bytes accessed | tf_op | source)
XLA Modules:
  0.0 154.0 jit_solution(7524267937863048577)
XLA Ops:
  0.0 4.5 %fusion.36 = (bf16[4096,128]{1,0:T(8,128)(2,1)}, bf16[4096,128]{1,0:T(8,128)(2,1)}, bf16[4096,128]{1,0:T(8,128)(2,1)}, bf16[4096,128]{1,0:T(8,128)(2,1)}) fusion(bf16[4096,512]{1,0:T(8,128)(2,1)} %param.3), kind=kLoop, calls=%fused_computation.104 | loop fusion | bytes 8388608 | tf_op jit(solution)/shard_map/slice | solution.py:58
  4.5 3.1 %collective-permute-start.3 = (bf16[4096,128]{1,0:T(8,128)(2,1)}, bf16[4096,128]{1,0:T(8,128)(2,1)S(1)}, u32[]{:S(2)}, u32[]{:S(2)}) collective-permute-start(bf16[4096,128]{1,0:T(8,128)(2,1)} %get-tuple-element.9), channel_id=1, source_target_pairs={{0,4},{4,0},{8,12},{12,8},{1,5},{5,1},{9,13},{13,9},{2,6},{6,2},{1... | collective-permute-start | bytes 3145736 | tf_op jit(solution)/shard_map/ppermute | solution.py:21
  10.0 6.6 %all-reduce = (f32[512]{0:T(512)S(1)}, f32[512]{0:T(512)S(1)}) all-reduce(f32[512]{0:T(512)S(1)} %get-tuple-element.6, f32[512]{0:T(512)S(1)} %get-tuple-element.5), channel_id=1, replica_groups=mesh['groups'=2,'chain'=4,'samp'=4] {'samp'}, use_global_device_ids=true, to_apply=%region_3.4 | all-reduce | flops 1024 | bytes 8192 | tf_op jit(solution)/shard_map/psum | solution.py:64
  16.7 5.9 %fusion.14 = f32[512,512]{1,0:T(8,128)S(1)} fusion(bf16[4096,512]{1,0:T(8,128)(2,1)} %param.3, f32[512]{0:T(512)S(1)} %get-tuple-element.59, f32[512]{0:T(512)S(1)} %get-tuple-element.58), kind=kOutput, calls=%fused_computation.29 | convolution fusion | flops 2155872256 | bytes 5246976 | tf_op jit(solution)/shard_map/dot_general | solution.py:39
  24.4 4.4 %collective-permute-start.5 = (f32[2,512]{1,0:T(2,128)S(1)}, f32[2,512]{1,0:T(2,128)S(1)}, u32[]{:S(2)}, u32[]{:S(2)}) collective-permute-start(f32[2,512]{1,0:T(2,128)S(1)} %pad_maximum_fusion.2), channel_id=1, source_target_pairs={{0,4},{4,0},{8,12},{12,8},{1,5},{5,1},{9,13},{13,9},{2,6},{6,2},{1... | collective-permute-start | bytes 12296 | tf_op jit(solution)/shard_map/ppermute | solution.py:21
  28.8 2.2 %collective-permute-done.5 = f32[2,512]{1,0:T(2,128)S(1)} collective-permute-done((f32[2,512]{1,0:T(2,128)S(1)}, f32[2,512]{1,0:T(2,128)S(1)}, u32[]{:S(2)}, u32[]{:S(2)}) %collective-permute-start.5) | collective-permute-done | bytes 4128 | tf_op jit(solution)/shard_map/ppermute | solution.py:21
  32.1 6.2 %collective-permute-start.10 = (bf16[4096,128]{1,0:T(8,128)(2,1)}, bf16[4096,128]{1,0:T(8,128)(2,1)S(1)}, u32[]{:S(2)}, u32[]{:S(2)}) collective-permute-start(bf16[4096,128]{1,0:T(8,128)(2,1)} %get-tuple-element.10), channel_id=1, source_target_pairs={{0,4},{4,0},{8,12},{12,8},{1,5},{5,1},{9,13},{13,9},{2,6},{6,2},{1... | collective-permute-start | bytes 3145736 | tf_op jit(solution)/shard_map/ppermute | solution.py:21
  40.3 6.7 %collective-permute-start.15 = (bf16[4096,128]{1,0:T(8,128)(2,1)}, bf16[4096,128]{1,0:T(8,128)(2,1)S(1)}, u32[]{:S(2)}, u32[]{:S(2)}) collective-permute-start(bf16[4096,128]{1,0:T(8,128)(2,1)} %get-tuple-element.12), channel_id=1, source_target_pairs={{0,4},{4,0},{8,12},{12,8},{1,5},{5,1},{9,13},{13,9},{2,6},{6,2},{1... | collective-permute-start | bytes 3145736 | tf_op jit(solution)/shard_map/ppermute | solution.py:21
  48.8 2.8 %collective-permute-start.20 = (bf16[4096,128]{1,0:T(8,128)(2,1)}, bf16[4096,128]{1,0:T(8,128)(2,1)S(1)}, u32[]{:S(2)}, u32[]{:S(2)}) collective-permute-start(bf16[4096,128]{1,0:T(8,128)(2,1)} %get-tuple-element.11), channel_id=1, source_target_pairs={{0,4},{4,0},{8,12},{12,8},{1,5},{5,1},{9,13},{13,9},{2,6},{6,2},{1... | collective-permute-start | bytes 3145736 | tf_op jit(solution)/shard_map/ppermute | solution.py:21
  51.6 3.9 %fusion.12 = f32[512,128]{1,0:T(8,128)S(1)} fusion(bf16[4096,512]{1,0:T(8,128)(2,1)} %param.3, f32[512]{0:T(512)S(1)} %get-tuple-element.59, f32[512]{0:T(512)S(1)} %get-tuple-element.58, f32[128]{0:T(128)S(1)} %get-tuple-element.60, f32[128]{0:T(128)S(1)} %get-tuple-element.67, bf16[4096,128]{1,0:T(8,128)(2,1)S(1)} %collective-permute-done.3, ...), kind=kOutput, calls=%fused_computation.28 | convolution fusion | flops 547880960 | bytes 6558721 | tf_op jit(solution)/shard_map/dot_general | solution.py:39
  55.5 6.1 %collective-permute-done.10 = bf16[4096,128]{1,0:T(8,128)(2,1)S(1)} collective-permute-done((bf16[4096,128]{1,0:T(8,128)(2,1)}, bf16[4096,128]{1,0:T(8,128)(2,1)S(1)}, u32[]{:S(2)}, u32[]{:S(2)}) %collective-permute-start.10) | collective-permute-done | bytes 1048608 | tf_op jit(solution)/shard_map/ppermute | solution.py:21
  62.5 2.0 %collective-permute-start.7 = (f32[128,128]{1,0:T(8,128)S(1)}, f32[128,128]{1,0:T(8,128)S(1)}, u32[]{:S(2)}, u32[]{:S(2)}) collective-permute-start(f32[128,128]{1,0:T(8,128)S(1)} %get-tuple-element.16), channel_id=1, source_target_pairs={{0,1},{1,0},{2,3},{3,2},{4,5},{5,4},{6,7},{7,6},{8,9},{9,8},{10,11... | collective-permute-start | bytes 196616 | tf_op jit(solution)/shard_map/ppermute | solution.py:34
  66.1 18.0 %collective-permute-done.15 = bf16[4096,128]{1,0:T(8,128)(2,1)S(1)} collective-permute-done((bf16[4096,128]{1,0:T(8,128)(2,1)}, bf16[4096,128]{1,0:T(8,128)(2,1)S(1)}, u32[]{:S(2)}, u32[]{:S(2)}) %collective-permute-start.15) | collective-permute-done | bytes 1048608 | tf_op jit(solution)/shard_map/ppermute | solution.py:21
  84.1 2.4 %collective-permute-start.8 = (f32[128,128]{1,0:T(8,128)S(1)}, f32[128,128]{1,0:T(8,128)S(1)}, u32[]{:S(2)}, u32[]{:S(2)}) collective-permute-start(f32[128,128]{1,0:T(8,128)S(1)} %get-tuple-element.18), channel_id=1, source_target_pairs={{0,2},{1,3},{2,0},{3,1},{4,6},{5,7},{6,4},{7,5},{8,10},{9,11},{10,... | collective-permute-start | bytes 196616 | tf_op jit(solution)/shard_map/ppermute | solution.py:34
  88.9 17.6 %collective-permute-done.20 = bf16[4096,128]{1,0:T(8,128)(2,1)S(1)} collective-permute-done((bf16[4096,128]{1,0:T(8,128)(2,1)}, bf16[4096,128]{1,0:T(8,128)(2,1)S(1)}, u32[]{:S(2)}, u32[]{:S(2)}) %collective-permute-start.20) | collective-permute-done | bytes 1048608 | tf_op jit(solution)/shard_map/ppermute | solution.py:21
  107.3 1.7 %collective-permute-start.13 = (f32[128,128]{1,0:T(8,128)S(1)}, f32[128,128]{1,0:T(8,128)S(1)}, u32[]{:S(2)}, u32[]{:S(2)}) collective-permute-start(f32[128,128]{1,0:T(8,128)S(1)} %get-tuple-element.21), channel_id=1, source_target_pairs={{0,2},{1,3},{2,0},{3,1},{4,6},{5,7},{6,4},{7,5},{8,10},{9,11},{10,... | collective-permute-start | bytes 196616 | tf_op jit(solution)/shard_map/ppermute | solution.py:34
  118.1 1.7 %collective-permute-start.18 = (f32[128,128]{1,0:T(8,128)S(1)}, f32[128,128]{1,0:T(8,128)S(1)}, u32[]{:S(2)}, u32[]{:S(2)}) collective-permute-start(f32[128,128]{1,0:T(8,128)S(1)} %get-tuple-element.24), channel_id=1, source_target_pairs={{0,2},{1,3},{2,0},{3,1},{4,6},{5,7},{6,4},{7,5},{8,10},{9,11},{10,... | collective-permute-start | bytes 196616 | tf_op jit(solution)/shard_map/ppermute | solution.py:34
  122.3 2.7 %collective-permute-done.26 = f32[128,128]{1,0:T(8,128)S(1)} collective-permute-done((f32[128,128]{1,0:T(8,128)S(1)}, f32[128,128]{1,0:T(8,128)S(1)}, u32[]{:S(2)}, u32[]{:S(2)}) %collective-permute-start.26) | collective-permute-done | bytes 65568 | tf_op jit(solution)/shard_map/ppermute | solution.py:34
  127.2 2.5 %collective-permute-done.29 = f32[128,128]{1,0:T(8,128)S(1)} collective-permute-done((f32[128,128]{1,0:T(8,128)S(1)}, f32[128,128]{1,0:T(8,128)S(1)}, u32[]{:S(2)}, u32[]{:S(2)}) %collective-permute-start.29) | collective-permute-done | bytes 65568 | tf_op jit(solution)/shard_map/ppermute | solution.py:34
  132.0 2.6 %collective-permute-done.32 = f32[128,128]{1,0:T(8,128)S(1)} collective-permute-done((f32[128,128]{1,0:T(8,128)S(1)}, f32[128,128]{1,0:T(8,128)S(1)}, u32[]{:S(2)}, u32[]{:S(2)}) %collective-permute-start.32) | collective-permute-done | bytes 65568 | tf_op jit(solution)/shard_map/ppermute | solution.py:34
  136.4 2.7 %collective-permute-done.35 = f32[128,128]{1,0:T(8,128)S(1)} collective-permute-done((f32[128,128]{1,0:T(8,128)S(1)}, f32[128,128]{1,0:T(8,128)S(1)}, u32[]{:S(2)}, u32[]{:S(2)}) %collective-permute-start.35) | collective-permute-done | bytes 65568 | tf_op jit(solution)/shard_map/ppermute | solution.py:34
  139.1 1.9 %collective-permute-start.23 = (f32[128,128]{1,0:T(8,128)S(1)}, f32[128,128]{1,0:T(8,128)S(1)}, u32[]{:S(2)}, u32[]{:S(2)}) collective-permute-start(f32[128,128]{1,0:T(8,128)S(1)} %get-tuple-element.27), channel_id=1, source_target_pairs={{0,2},{1,3},{2,0},{3,1},{4,6},{5,7},{6,4},{7,5},{8,10},{9,11},{10,... | collective-permute-start | bytes 196616 | tf_op jit(solution)/shard_map/ppermute | solution.py:34
  143.8 1.7 %collective-permute-done.24 = f32[128,128]{1,0:T(8,128)S(1)} collective-permute-done((f32[128,128]{1,0:T(8,128)S(1)}, f32[128,128]{1,0:T(8,128)S(1)}, u32[]{:S(2)}, u32[]{:S(2)}) %collective-permute-start.24) | collective-permute-done | bytes 65568 | tf_op jit(solution)/shard_map/ppermute | solution.py:34
  145.5 7.5 %collective-permute-done.37 = f32[128,512]{1,0:T(8,128)S(1)} collective-permute-done((f32[128,512]{1,0:T(8,128)S(1)}, f32[128,512]{1,0:T(8,128)S(1)}, u32[]{:S(2)}, u32[]{:S(2)}) %collective-permute-start.37) | collective-permute-done | bytes 262176 | tf_op jit(solution)/shard_map/ppermute | solution.py:92
  (101 shorter events, 35.8 us)
Async XLA Ops:
  4.5 43.6 %collective-permute-start.3 = (bf16[4096,128]{1,0:T(8,128)(2,1)}, bf16[4096,128]{1,0:T(8,128)(2,1)S(1)}, u32[]{:S(2)}, u32[]{:S(2)}) collective-permute-start(bf16[4096,128]{1,0:T(8,128)(2,1)} %get-tuple-element.9), channel_id=1, source_target_pairs={{0,4},{4,0},{8,12},{12,8},{1,5},{5,1},{9,13},{13,9},{2,6},{6,2},{1... | collective-permute-start | bytes 3145736 | tf_op jit(solution)/shard_map/ppermute | solution.py:21
  7.5 41.3 %collective-permute-start.4 = (bf16[4096,128]{1,0:T(8,128)(2,1)}, bf16[4096,128]{1,0:T(8,128)(2,1)S(1)}, u32[]{:S(2)}, u32[]{:S(2)}) collective-permute-start(bf16[4096,128]{1,0:T(8,128)(2,1)} %get-tuple-element.9), channel_id=1, source_target_pairs={{4,8},{8,4},{5,9},{9,5},{6,10},{10,6},{7,11},{11,7},{20,24},{24,20... | collective-permute-start | bytes 3145736 | tf_op jit(solution)/shard_map/ppermute | solution.py:21
  23.5 8.6 %collective-permute-start = (f32[128,512]{1,0:T(8,128)}, f32[128,512]{1,0:T(8,128)S(1)}, u32[]{:S(2)}, u32[]{:S(2)}) collective-permute-start(f32[128,512]{1,0:T(8,128)} %get-tuple-element.13), channel_id=1, source_target_pairs={{0,1},{1,0},{2,3},{3,2},{4,5},{5,4},{6,7},{7,6},{8,9},{9,8},{10,11... | collective-permute-start | bytes 786440 | tf_op jit(solution)/shard_map/ppermute | solution.py:34
  23.5 14.8 %collective-permute-start.1 = (f32[128,512]{1,0:T(8,128)}, f32[128,512]{1,0:T(8,128)}, u32[]{:S(2)}, u32[]{:S(2)}) collective-permute-start(f32[128,512]{1,0:T(8,128)} %get-tuple-element.15), channel_id=1, source_target_pairs={{0,2},{1,3},{2,0},{3,1},{4,6},{5,7},{6,4},{7,5},{8,10},{9,11},{10,... | collective-permute-start | bytes 786440 | tf_op jit(solution)/shard_map/ppermute | solution.py:34
  24.4 6.6 %collective-permute-start.5 = (f32[2,512]{1,0:T(2,128)S(1)}, f32[2,512]{1,0:T(2,128)S(1)}, u32[]{:S(2)}, u32[]{:S(2)}) collective-permute-start(f32[2,512]{1,0:T(2,128)S(1)} %pad_maximum_fusion.2), channel_id=1, source_target_pairs={{0,4},{4,0},{8,12},{12,8},{1,5},{5,1},{9,13},{13,9},{2,6},{6,2},{1... | collective-permute-start | bytes 12296 | tf_op jit(solution)/shard_map/ppermute | solution.py:21
  31.7 8.7 %collective-permute-start.2 = (f32[128,512]{1,0:T(8,128)}, f32[128,512]{1,0:T(8,128)S(1)}, u32[]{:S(2)}, u32[]{:S(2)}) collective-permute-start(f32[128,512]{1,0:T(8,128)} %get-tuple-element.14), channel_id=1, source_target_pairs={{0,3},{1,2},{2,1},{3,0},{4,7},{5,6},{6,5},{7,4},{8,11},{9,10},{10,... | collective-permute-start | bytes 786440 | tf_op jit(solution)/shard_map/ppermute | solution.py:34
  32.1 29.5 %collective-permute-start.10 = (bf16[4096,128]{1,0:T(8,128)(2,1)}, bf16[4096,128]{1,0:T(8,128)(2,1)S(1)}, u32[]{:S(2)}, u32[]{:S(2)}) collective-permute-start(bf16[4096,128]{1,0:T(8,128)(2,1)} %get-tuple-element.10), channel_id=1, source_target_pairs={{0,4},{4,0},{8,12},{12,8},{1,5},{5,1},{9,13},{13,9},{2,6},{6,2},{1... | collective-permute-start | bytes 3145736 | tf_op jit(solution)/shard_map/ppermute | solution.py:21
  38.3 24.2 %collective-permute-start.11 = (bf16[4096,128]{1,0:T(8,128)(2,1)}, bf16[4096,128]{1,0:T(8,128)(2,1)S(1)}, u32[]{:S(2)}, u32[]{:S(2)}) collective-permute-start(bf16[4096,128]{1,0:T(8,128)(2,1)} %get-tuple-element.10), channel_id=1, source_target_pairs={{4,8},{8,4},{5,9},{9,5},{6,10},{10,6},{7,11},{11,7},{20,24},{24,20... | collective-permute-start | bytes 3145736 | tf_op jit(solution)/shard_map/ppermute | solution.py:21
  40.3 43.8 %collective-permute-start.15 = (bf16[4096,128]{1,0:T(8,128)(2,1)}, bf16[4096,128]{1,0:T(8,128)(2,1)S(1)}, u32[]{:S(2)}, u32[]{:S(2)}) collective-permute-start(bf16[4096,128]{1,0:T(8,128)(2,1)} %get-tuple-element.12), channel_id=1, source_target_pairs={{0,4},{4,0},{8,12},{12,8},{1,5},{5,1},{9,13},{13,9},{2,6},{6,2},{1... | collective-permute-start | bytes 3145736 | tf_op jit(solution)/shard_map/ppermute | solution.py:21
  48.0 38.4 %collective-permute-start.16 = (bf16[4096,128]{1,0:T(8,128)(2,1)}, bf16[4096,128]{1,0:T(8,128)(2,1)S(1)}, u32[]{:S(2)}, u32[]{:S(2)}) collective-permute-start(bf16[4096,128]{1,0:T(8,128)(2,1)} %get-tuple-element.12), channel_id=1, source_target_pairs={{4,8},{8,4},{5,9},{9,5},{6,10},{10,6},{7,11},{11,7},{20,24},{24,20... | collective-permute-start | bytes 3145736 | tf_op jit(solution)/shard_map/ppermute | solution.py:21
  48.8 57.8 %collective-permute-start.20 = (bf16[4096,128]{1,0:T(8,128)(2,1)}, bf16[4096,128]{1,0:T(8,128)(2,1)S(1)}, u32[]{:S(2)}, u32[]{:S(2)}) collective-permute-start(bf16[4096,128]{1,0:T(8,128)(2,1)} %get-tuple-element.11), channel_id=1, source_target_pairs={{0,4},{4,0},{8,12},{12,8},{1,5},{5,1},{9,13},{13,9},{2,6},{6,2},{1... | collective-permute-start | bytes 3145736 | tf_op jit(solution)/shard_map/ppermute | solution.py:21
  61.6 45.7 %collective-permute-start.21 = (bf16[4096,128]{1,0:T(8,128)(2,1)S(1)}, bf16[4096,128]{1,0:T(8,128)(2,1)S(1)}, u32[]{:S(2)}, u32[]{:S(2)}) collective-permute-start(bf16[4096,128]{1,0:T(8,128)(2,1)S(1)} %copy-done.2), channel_id=1, source_target_pairs={{4,8},{8,4},{5,9},{9,5},{6,10},{10,6},{7,11},{11,7},{20,24},{24,20... | collective-permute-start | bytes 3145736 | tf_op jit(solution)/shard_map/ppermute | solution.py:21
  62.5 55.0 %collective-permute-start.7 = (f32[128,128]{1,0:T(8,128)S(1)}, f32[128,128]{1,0:T(8,128)S(1)}, u32[]{:S(2)}, u32[]{:S(2)}) collective-permute-start(f32[128,128]{1,0:T(8,128)S(1)} %get-tuple-element.16), channel_id=1, source_target_pairs={{0,1},{1,0},{2,3},{3,2},{4,5},{5,4},{6,7},{7,6},{8,9},{9,8},{10,11... | collective-permute-start | bytes 196616 | tf_op jit(solution)/shard_map/ppermute | solution.py:34
  84.1 33.6 %collective-permute-start.8 = (f32[128,128]{1,0:T(8,128)S(1)}, f32[128,128]{1,0:T(8,128)S(1)}, u32[]{:S(2)}, u32[]{:S(2)}) collective-permute-start(f32[128,128]{1,0:T(8,128)S(1)} %get-tuple-element.18), channel_id=1, source_target_pairs={{0,2},{1,3},{2,0},{3,1},{4,6},{5,7},{6,4},{7,5},{8,10},{9,11},{10,... | collective-permute-start | bytes 196616 | tf_op jit(solution)/shard_map/ppermute | solution.py:34
  86.5 31.6 %collective-permute-start.9 = (f32[128,128]{1,0:T(8,128)S(1)}, f32[128,128]{1,0:T(8,128)S(1)}, u32[]{:S(2)}, u32[]{:S(2)}) collective-permute-start(f32[128,128]{1,0:T(8,128)S(1)} %get-tuple-element.17), channel_id=1, source_target_pairs={{0,3},{1,2},{2,1},{3,0},{4,7},{5,6},{6,5},{7,4},{8,11},{9,10},{10,... | collective-permute-start | bytes 196616 | tf_op jit(solution)/shard_map/ppermute | solution.py:34
  106.5 13.2 %collective-permute-start.12 = (f32[128,128]{1,0:T(8,128)S(1)}, f32[128,128]{1,0:T(8,128)S(1)}, u32[]{:S(2)}, u32[]{:S(2)}) collective-permute-start(f32[128,128]{1,0:T(8,128)S(1)} %get-tuple-element.19), channel_id=1, source_target_pairs={{0,1},{1,0},{2,3},{3,2},{4,5},{5,4},{6,7},{7,6},{8,9},{9,8},{10,11... | collective-permute-start | bytes 196616 | tf_op jit(solution)/shard_map/ppermute | solution.py:34
  107.3 12.6 %collective-permute-start.13 = (f32[128,128]{1,0:T(8,128)S(1)}, f32[128,128]{1,0:T(8,128)S(1)}, u32[]{:S(2)}, u32[]{:S(2)}) collective-permute-start(f32[128,128]{1,0:T(8,128)S(1)} %get-tuple-element.21), channel_id=1, source_target_pairs={{0,2},{1,3},{2,0},{3,1},{4,6},{5,7},{6,4},{7,5},{8,10},{9,11},{10,... | collective-permute-start | bytes 196616 | tf_op jit(solution)/shard_map/ppermute | solution.py:34
  117.7 23.4 %collective-permute-start.17 = (f32[128,128]{1,0:T(8,128)S(1)}, f32[128,128]{1,0:T(8,128)S(1)}, u32[]{:S(2)}, u32[]{:S(2)}) collective-permute-start(f32[128,128]{1,0:T(8,128)S(1)} %get-tuple-element.22), channel_id=1, source_target_pairs={{0,1},{1,0},{2,3},{3,2},{4,5},{5,4},{6,7},{7,6},{8,9},{9,8},{10,11... | collective-permute-start | bytes 196616 | tf_op jit(solution)/shard_map/ppermute | solution.py:34
  118.1 23.7 %collective-permute-start.18 = (f32[128,128]{1,0:T(8,128)S(1)}, f32[128,128]{1,0:T(8,128)S(1)}, u32[]{:S(2)}, u32[]{:S(2)}) collective-permute-start(f32[128,128]{1,0:T(8,128)S(1)} %get-tuple-element.24), channel_id=1, source_target_pairs={{0,2},{1,3},{2,0},{3,1},{4,6},{5,7},{6,4},{7,5},{8,10},{9,11},{10,... | collective-permute-start | bytes 196616 | tf_op jit(solution)/shard_map/ppermute | solution.py:34
  119.9 5.1 %collective-permute-start.26 = (f32[128,128]{1,0:T(8,128)S(1)}, f32[128,128]{1,0:T(8,128)S(1)}, u32[]{:S(2)}, u32[]{:S(2)}) collective-permute-start(f32[128,128]{1,0:T(8,128)S(1)} %get-tuple-element.30), channel_id=1, source_target_pairs={{0,2},{1,3},{2,0},{3,1},{4,6},{5,7},{6,4},{7,5},{8,10},{9,11},{10,... | collective-permute-start | bytes 196616 | tf_op jit(solution)/shard_map/ppermute | solution.py:34
  126.3 4.9 %collective-permute-start.31 = (f32[128,128]{1,0:T(8,128)S(1)}, f32[128,128]{1,0:T(8,128)S(1)}, u32[]{:S(2)}, u32[]{:S(2)}) collective-permute-start(f32[128,128]{1,0:T(8,128)S(1)} %get-tuple-element.34), channel_id=1, source_target_pairs={{0,1},{1,0},{2,3},{3,2},{4,5},{5,4},{6,7},{7,6},{8,9},{9,8},{10,11... | collective-permute-start | bytes 196616 | tf_op jit(solution)/shard_map/ppermute | solution.py:34
  129.7 4.8 %collective-permute-start.32 = (f32[128,128]{1,0:T(8,128)S(1)}, f32[128,128]{1,0:T(8,128)S(1)}, u32[]{:S(2)}, u32[]{:S(2)}) collective-permute-start(f32[128,128]{1,0:T(8,128)S(1)} %get-tuple-element.36), channel_id=1, source_target_pairs={{0,2},{1,3},{2,0},{3,1},{4,6},{5,7},{6,4},{7,5},{8,10},{9,11},{10,... | collective-permute-start | bytes 196616 | tf_op jit(solution)/shard_map/ppermute | solution.py:34
  135.8 7.3 %collective-permute-start.19 = (f32[128,128]{1,0:T(8,128)S(1)}, f32[128,128]{1,0:T(8,128)S(1)}, u32[]{:S(2)}, u32[]{:S(2)}) collective-permute-start(f32[128,128]{1,0:T(8,128)S(1)} %get-tuple-element.23), channel_id=1, source_target_pairs={{0,3},{1,2},{2,1},{3,0},{4,7},{5,6},{6,5},{7,4},{8,11},{9,10},{10,... | collective-permute-start | bytes 196616 | tf_op jit(solution)/shard_map/ppermute | solution.py:34
  141.8 11.2 %collective-permute-start.37 = (f32[128,512]{1,0:T(8,128)S(1)}, f32[128,512]{1,0:T(8,128)S(1)}, u32[]{:S(2)}, u32[]{:S(2)}) collective-permute-start(f32[128,512]{1,0:T(8,128)S(1)} %pad_maximum_fusion.1), channel_id=1, source_target_pairs={{4,0},{8,4},{12,8},{5,1},{9,5},{13,9},{6,2},{10,6},{14,10},{7,3},{... | collective-permute-start | bytes 786440 | tf_op jit(solution)/shard_map/ppermute | solution.py:92
  (18 other events, 99.1 us)

commit v2 on v0

v2 whole, which is shorter than its diff:
```python
import functools

import jax
import jax.numpy as jnp
from jax import lax
from jax.experimental import pallas as pl
from jax.experimental.pallas import tpu as pltpu
from jax.sharding import PartitionSpec as P


LANES = 128
DEPTH = 1024


def exchange(array, devices, first):
    pairs = []
    for low in range(first, devices - 1, 2):
        pairs += [(low, low + 1), (low + 1, low)]
    return lax.ppermute(array, "chain", pairs) if pairs else jnp.zeros_like(array)


def matmul(left, right):
    return lax.dot_general(left, right, (((1,), (0,)), ((), ())), preferred_element_type=jnp.float32)


def accumulate(total, terms):
    return terms if total is None else [t + u for t, u in zip(total, terms)]


def by_distance(parts, me):
    bit = 1
    while bit < len(parts):
        swap = (me // bit) % 2 == 1
        parts = [jnp.where(swap, parts[t ^ bit], parts[t]) for t in range(len(parts))]
        bit *= 2
    return parts


def own_kernel(samp, place_ref, values_ref, mean_ref, scale_ref, own_ref, *outs):
    rows, width = values_ref.shape
    part = width // samp
    total = None
    for k in range(0, rows, DEPTH):
        span = pl.ds(k, DEPTH)
        z = ((values_ref[span, :].astype(jnp.float32) - mean_ref[...]) * scale_ref[...]).astype(jnp.bfloat16)
        flat = z.T
        own_ref[:, span] = flat
        total = accumulate(total, [matmul(flat, z)])
    parts = [total[0][t * part : (t + 1) * part] for t in range(samp)]
    for out_ref, value in zip(outs, by_distance(parts, place_ref[1])):
        out_ref[...] = value


def step_kernel(samp, j, results, place_ref, sa_ref, sb_ref, a_ref, b_ref, own_ref, *rest):
    nears, fars = rest[:j], rest[j : 2 * j]
    saved, outs = rest[2 * j : len(rest) - results], rest[len(rest) - results :]
    rows, step = a_ref.shape
    part, share = own_ref.shape[0] // samp, step // samp
    even, me = place_ref[0] != 0, place_ref[1]
    cols = pl.ds(j * step, step)
    sa, sb = sa_ref[:, cols], sb_ref[:, cols]
    after = jnp.where(even, sa, sb)
    before = jnp.where(even, sb, sa)
    total = None
    for k in range(0, rows, DEPTH):
        span = pl.ds(k, DEPTH)
        a, b = a_ref[span, :].astype(jnp.float32), b_ref[span, :].astype(jnp.float32)
        near = ((jnp.where(even, a, b) - after[0:1]) * after[1:2]).astype(jnp.bfloat16)
        far = ((jnp.where(even, b, a) - before[2:3]) * before[3:4]).astype(jnp.bfloat16).T
        if saved:
            saved[0][span, :] = near
            saved[1][:, span] = far
        terms = [matmul(own_ref[:, span], near)]
        terms += [matmul(fars[i][:, span], near) for i in range(j)]
        terms += [matmul(far, jnp.concatenate([near] + [nears[i][span, :] for i in range(j)], 1))]
        total = accumulate(total, terms)
    blocks = total[1:-1] + [total[-1][:, i * step : (i + 1) * step] for i in range(j + 1)]
    parts = [
        [total[0][t * part : (t + 1) * part]] + [block[t * share : (t + 1) * share] for block in blocks]
        for t in range(samp)
    ]
    parts = [by_distance([parts[t][n] for t in range(samp)], me) for n in range(len(blocks) + 1)]
    if len(outs) != samp:
        outs = [outs[d % 2].at[d // 2] for d in range(samp)]
    for d, out_ref in enumerate(outs):
        row = 0
        for piece in parts:
            size = piece[d].shape[0]
            out_ref[row : row + size, :] = piece[d]
            row += size


def call(kernel, out_shapes, flops, *args):
    vmem = pl.BlockSpec(memory_space=pltpu.VMEM)
    moved = sum(x.size * x.dtype.itemsize for x in args[1:]) + sum(x.size * x.dtype.itemsize for x in out_shapes)
    return pl.pallas_call(
        kernel,
        out_shape=out_shapes,
        in_specs=[pl.BlockSpec(memory_space=pltpu.SMEM)] + [vmem] * (len(args) - 1),
        out_specs=[vmem] * len(out_shapes),
        cost_estimate=pl.CostEstimate(flops=flops, bytes_accessed=moved, transcendentals=0),
        compiler_params=pltpu.CompilerParams(vmem_limit_bytes=VMEM_LIMIT),
    )(*args)


VMEM_LIMIT = 32 * 2**20


def body(dosage, filter_mask, counts):
    chain, samp = lax.axis_size("chain"), lax.axis_size("samp")
    me, block = lax.axis_index("samp"), lax.axis_index("chain")
    even = block % 2 == 0
    place = jnp.stack([even.astype(jnp.int32), me.astype(jnp.int32)])
    local_rows, width = dosage.shape
    samples = local_rows * samp
    step = LANES
    chunks = width // step
    part = width // samp
    share = step // samp

    def spread(vector):
        lead = vector.shape[:-1]
        grid = vector.reshape(*lead, samp, chunks, share)
        return jnp.swapaxes(grid, -3, -2).reshape(*lead, width)

    def payload(j, up):
        lane = jnp.arange(step, dtype=jnp.int32)
        upward = lane // share * part + j * share + lane % share
        source = jnp.where(up, upward, j * step + lane)
        chosen = jnp.arange(width, dtype=jnp.int32)[:, None] == source[None, :]
        return jnp.dot(dosage, chosen.astype(jnp.bfloat16), preferred_element_type=jnp.float32).astype(jnp.bfloat16)

    def scatter_sum(parts):
        total = parts[0]
        for d in range(1, samp):
            total = total + lax.ppermute(parts[d], "samp", [(i, i ^ d) for i in range(samp)])
        return total

    def f32(*shape):
        return jax.ShapeDtypeStruct(shape, jnp.float32)

    def bf16(*shape):
        return jax.ShapeDtypeStruct(shape, jnp.bfloat16)

    raw = []
    for j in range(chunks):
        a = exchange(payload(j, even), chain, 0)
        b = exchange(payload(j, ~even), chain, 1)
        raw.append((a, b))

    values = dosage.astype(jnp.float32)
    totals, squares = lax.psum((jnp.sum(values, 0), jnp.sum(values * values, 0)), "samp")
    mean = totals / samples
    var = squares / samples - mean * mean
    live = (jnp.arange(width, dtype=jnp.int32) < counts[0]).astype(jnp.float32)
    keep = filter_mask.astype(jnp.float32) * live
    scale = lax.rsqrt(var + 1e-05) * keep
    stats = jnp.stack([mean, scale])
    stats = jnp.concatenate([stats, spread(stats)])
    sa = exchange(stats, chain, 0)
    sb = exchange(stats, chain, 1)

    own, *parts = call(
        functools.partial(own_kernel, samp),
        [bf16(width, local_rows)] + [f32(part, width)] * samp,
        2 * local_rows * width * width,
        place, dosage, mean[None], scale[None],
    )
    tile = scatter_sum(parts)

    nears, fars, near_done, shipped = [], [], [], []
    far_done = {}
    for j in range(chunks):
        size = part + (2 * j + 1) * share
        last = j == chunks - 1
        results = [f32(samp // 2, size, step)] * 2 if last else [f32(size, step)] * samp
        saved = [] if last else [bf16(local_rows, step), bf16(step, local_rows)]
        *kept, = call(
            functools.partial(step_kernel, samp, j, len(results)),
            saved + results,
            2 * local_rows * step * (width + (2 * j + 1) * step),
            place, sa, sb, *raw[j], own, *nears, *fars,
        )
        parts = kept[len(saved) :]
        nears += kept[:1] if saved else []
        fars += kept[1:2] if saved else []
        names = [(i, j) for i in range(j)] + [(j, j)] + [(j, i) for i in range(j)]
        for at, name in enumerate(names):
            far_done[name] = (j, at)
        if not last:
            total = scatter_sum(parts)
            near_done.append(total[:part])
            shipped.append(total[part:])
            if j == chunks - 2:
                early = lax.ppermute(
                    jnp.concatenate(shipped), "chain", [(i + 1, i) for i in range(chain - 1)]
                )
        else:
            pair = 2
            kept = parts[0] + lax.ppermute(parts[1], "samp", [(i, i ^ 1) for i in range(samp)])
            near_total, far_total = kept[0][:part], 0.0
            for n in range(samp // pair):
                out = kept[n]
                moved = [i ^ (n * pair) for i in range(samp)]
                pairs = [((c + 1) * samp + i, c * samp + moved[i]) for c in range(chain - 1) for i in range(samp)]
                far_total = far_total + lax.ppermute(out[part:], ("chain", "samp"), pairs)
                if n:
                    near_total = near_total + lax.ppermute(out[:part], "samp", [(i, moved[i]) for i in range(samp)])
            near_done.append(near_total)
    starts, row = [], 0
    for piece in shipped:
        starts.append(row)
        row += piece.shape[0]

    def far_block(i, j):
        at, place = far_done[i, j]
        if at == chunks - 1:
            return far_total[place * share : (place + 1) * share]
        return early[starts[at] + place * share : starts[at] + (place + 1) * share]

    far = jnp.concatenate(
        [jnp.concatenate([far_block(i, j) for j in range(chunks)], 1) for i in range(chunks)], 0
    )
    out = jnp.stack([tile, jnp.concatenate(near_done, 1), far], 1) / samples
    return out[None]


def solution(mesh):
    in_specs = (P("samp", ("groups", "chain")), P(("groups", "chain")), P(("groups", "chain")))
    out_specs = P(("groups", "chain"), "samp", None, None)
    return jax.shard_map(body, mesh=mesh, in_specs=in_specs, out_specs=out_specs, check_vma=False)
```

time: 344 us -> 158 us (0.46)
  waiting for transfers between devices: 303 us -> 48.5 us
  starting transfers between devices: 2.59 us -> 57.8 us
  Pallas kernels: 0 us -> 16.1 us
  between operations: 14.1 us -> 1.07 us
  matrix products: 7.05 us -> 17.4 us
  other arithmetic: 8.9 us -> 4.73 us
  local copies, waits for them, and re-layouts: 0.01 us -> 3.54 us
    ppermute x2 -> x27, waiting for transfers between devices: 266 us -> 48.5 us  [the longest x10 27.3 us: exchange(): lax.ppermute(array, 'chain', pairs)]
    ppermute x2 -> x27, starting transfers between devices: 2.58 us -> 57.8 us  [the longest x10 43.9 us: exchange(): lax.ppermute(array, 'chain', pairs)]
    reduce_scatter x1 -> x0, waiting for transfers between devices: 36.1 us -> none  [body(): lax.psum_scatter(jnp.stack(pieces, 1) / samples, 'samp', scatter_dimensio...]
    pallas_call x0 -> x5, Pallas kernels: none -> 16.1 us  [call(): pl.pallas_call(kernel, out_shape=out_shapes, in_specs=[pl.BlockSpec(memor...]
    dot_general x3 -> x8, matrix products: 7.05 us -> 17.4 us  [payload(): jnp.dot(dosage, chosen.astype(jnp.bfloat16), preferred_element_type=jnp.f...]
    convert_element_type x1 -> x0, other arithmetic: 3.52 us -> none  [body(): ((values - mean) * lax.rsqrt(var + 1e-05) * keep).astype(jnp.bfloat16)]
  transfers between devices with their start and end apart: 3 -> 27, of which waited for: 3 -> 11; matrix products, arithmetic and copies ran while one was open for 1% -> 11% of each run, Pallas kernels for 0% -> 10%
where the time goes in v2:
time: 158 us; the launch traced here: 157 us
  starting transfers between devices  57.8 us (37%)
  waiting for transfers between devices  48.5 us (31%)
  matrix products  17.4 us (11%)
  Pallas kernels  16.1 us (10%)
  blocking collectives  8.36 us (5%)
  other arithmetic  4.73 us (3%)
  local copies, waits for them, and re-layouts  3.54 us (2%)
    ppermute x10, starting transfers between devices, exchange(): lax.ppermute(array, 'chain', pairs)  43.9 us
    ppermute x10, waiting for transfers between devices, exchange(): lax.ppermute(array, 'chain', pairs)  27.3 us
    dot_general x8, matrix products, payload(): jnp.dot(dosage, chosen.astype(jnp.bfloat16), preferred_element_type=jnp.f...  17.4 us
    pallas_call x5, Pallas kernels, call(): pl.pallas_call(kernel, out_shape=out_shapes, in_specs=[pl.BlockSpec(memor...  16.1 us
    ppermute x12, waiting for transfers between devices, scatter_sum(): lax.ppermute(parts[d], 'samp', [(i, i ^ d) for i in range(samp)])  12.7 us
    psum x1, blocking collectives, body(): lax.psum((jnp.sum(values, 0), jnp.sum(values * values, 0)), 'samp')  8.36 us
    ppermute x12, starting transfers between devices, scatter_sum(): lax.ppermute(parts[d], 'samp', [(i, i ^ d) for i in range(samp)])  7.15 us
    ppermute x2, waiting for transfers between devices, body(): far_total = far_total + lax.ppermute(out[part:], ('chain', 'samp'), pairs)  6.89 us
  transfers between devices with their start and end apart: 27, of which 11 were waited for; matrix products, arithmetic and copies ran while one was open for 11% of the time, Pallas kernels for 10%

profile of v2, /device:TPU:0, one launch (start us, length us, event | category | flops | bytes accessed | tf_op | source)
XLA Modules:
  0.0 157.5 jit_solution(8702466558281732095)
XLA Ops:
  0.7 3.3 %convert_reduce_fusion = (f32[512]{0:T(512)S(1)}, f32[512]{0:T(512)S(1)}) fusion(bf16[4096,512]{1,0:T(8,128)(2,1)} %values_ref.1), kind=kLoop, calls=%fused_computation.1 | loop fusion | flops 8387584 | bytes 4198400 | tf_op jit(solution)/shard_map/reduce_sum | solution.py:152
  4.0 8.4 %all-reduce = (f32[512]{0:T(512)S(1)}, f32[512]{0:T(512)S(1)}) all-reduce(f32[512]{0:T(512)S(1)} %get-tuple-element.56, f32[512]{0:T(512)S(1)} %get-tuple-element.55), channel_id=1, replica_groups=mesh['groups'=2,'chain'=4,'samp'=4] {'samp'}, use_global_device_ids=true, to_apply=%region_3.4 | all-reduce | flops 1024 | bytes 8192 | tf_op jit(solution)/shard_map/psum | solution.py:152
  13.3 4.5 %collective-permute-start.3 = (f32[4,512]{1,0:T(4,128)S(1)}, f32[4,512]{1,0:T(4,128)S(1)}, u32[]{:S(2)}, u32[]{:S(2)}) collective-permute-start(f32[4,512]{1,0:T(4,128)S(1)} %pad_maximum_fusion.1), channel_id=1, source_target_pairs={{0,4},{4,0},{8,12},{12,8},{1,5},{5,1},{9,13},{13,9},{2,6},{6,2},{1... | collective-permute-start | bytes 24584 | tf_op jit(solution)/shard_map/ppermute | solution.py:19
  17.8 3.6 %fusion.4 = bf16[4096,128]{1,0:T(8,128)(2,1)S(1)} fusion(bf16[4096,512]{1,0:T(8,128)(2,1)} %values_ref.1, s32[128]{0:T(128)S(1)} %broadcast_select_fusion.2), kind=kOutput, calls=%fused_computation.14 | convolution fusion | flops 537460736 | bytes 5243392 | tf_op jit(solution)/shard_map/dot_general | solution.py:131
  25.5 4.5 %collective-permute-start.5 = (bf16[4096,128]{1,0:T(8,128)(2,1)S(1)}, bf16[4096,128]{1,0:T(8,128)(2,1)S(1)}, u32[]{:S(2)}, u32[]{:S(2)}) collective-permute-start(bf16[4096,128]{1,0:T(8,128)(2,1)S(1)} %fusion.1), channel_id=1, source_target_pairs={{0,4},{4,0},{8,12},{12,8},{1,5},{5,1},{9,13},{13,9},{2,6},{6,2},{1... | collective-permute-start | bytes 3145736 | tf_op jit(solution)/shard_map/ppermute | solution.py:19
  30.0 2.2 %fusion.5 = bf16[4096,128]{1,0:T(8,128)(2,1)} fusion(bf16[4096,512]{1,0:T(8,128)(2,1)S(1)} %copy-done, s32[128]{0:T(128)S(1)} %broadcast_select_fusion.5), kind=kOutput, calls=%fused_computation.15 | convolution fusion | flops 537460736 | bytes 5243392 | tf_op jit(solution)/shard_map/dot_general | solution.py:131
  32.2 2.3 %fusion.3 = bf16[4096,128]{1,0:T(8,128)(2,1)} fusion(bf16[4096,512]{1,0:T(8,128)(2,1)S(1)} %copy-done, s32[128]{0:T(128)S(1)} %broadcast_select_fusion.6), kind=kOutput, calls=%fused_computation.13 | convolution fusion | flops 537460736 | bytes 5243392 | tf_op jit(solution)/shard_map/dot_general | solution.py:131
  34.5 2.2 %fusion.8 = bf16[4096,128]{1,0:T(8,128)(2,1)} fusion(bf16[4096,512]{1,0:T(8,128)(2,1)S(1)} %copy-done, s32[128]{0:T(128)S(1)} %broadcast_select_fusion), kind=kOutput, calls=%fused_computation.18 | convolution fusion | flops 537460736 | bytes 5243392 | tf_op jit(solution)/shard_map/dot_general | solution.py:131
  36.8 2.3 %fusion.6 = bf16[4096,128]{1,0:T(8,128)(2,1)} fusion(bf16[4096,512]{1,0:T(8,128)(2,1)S(1)} %copy-done, s32[128]{0:T(128)S(1)} %broadcast_select_fusion.1), kind=kOutput, calls=%fused_computation.16 | convolution fusion | flops 537460736 | bytes 5243392 | tf_op jit(solution)/shard_map/dot_general | solution.py:131
  41.6 7.8 %collective-permute-start.10 = (bf16[4096,128]{1,0:T(8,128)(2,1)}, bf16[4096,128]{1,0:T(8,128)(2,1)}, u32[]{:S(2)}, u32[]{:S(2)}) collective-permute-start(bf16[4096,128]{1,0:T(8,128)(2,1)} %fusion.3), channel_id=1, source_target_pairs={{0,4},{4,0},{8,12},{12,8},{1,5},{5,1},{9,13},{13,9},{2,6},{6,2},{1... | collective-permute-start | bytes 3145736 | tf_op jit(solution)/shard_map/ppermute | solution.py:19
  49.4 22.5 %collective-permute-start.15 = (bf16[4096,128]{1,0:T(8,128)(2,1)}, bf16[4096,128]{1,0:T(8,128)(2,1)}, u32[]{:S(2)}, u32[]{:S(2)}) collective-permute-start(bf16[4096,128]{1,0:T(8,128)(2,1)} %fusion.5), channel_id=1, source_target_pairs={{0,4},{4,0},{8,12},{12,8},{1,5},{5,1},{9,13},{13,9},{2,6},{6,2},{1... | collective-permute-start | bytes 3145736 | tf_op jit(solution)/shard_map/ppermute | solution.py:19
  71.9 2.2 %fusion.7 = bf16[4096,128]{1,0:T(8,128)(2,1)} fusion(bf16[4096,512]{1,0:T(8,128)(2,1)S(1)} %copy-done, s32[128]{0:T(128)S(1)} %broadcast_select_fusion.4), kind=kOutput, calls=%fused_computation.17 | convolution fusion | flops 537460736 | bytes 5243392 | tf_op jit(solution)/shard_map/dot_general | solution.py:131
  77.4 2.9 %shard_map.37 = (bf16[512,4096]{1,0:T(8,128)(2,1)S(1)}, f32[128,512]{1,0:T(8,128)S(1)}, f32[128,512]{1,0:T(8,128)S(1)}, f32[128,512]{1,0:T(8,128)S(1)}, f32[128,512]{1,0:T(8,128)S(1)}) custom-call(s32[2]{0:T(128)S(1)} %pad_add_fusion.place_ref, bf16[4096,512]{1,0:T(8,128)(2,1)S(1)} %copy-done.1, f32[1,512]{1,0:T(1,128)S(1)} %bitcast.49, f32[1,512]{1,0:T(1,128)S(1)} %bitcast.51), custom_call_target="tpu_custom_call" | custom-call | flops 2147483648 | bytes 9441280 | tf_op jit(solution)/shard_map/pallas_call | solution.py:96
  80.4 2.2 %shard_map.38 = (bf16[4096,128]{1,0:T(8,128)(2,1)S(1)}, bf16[128,4096]{1,0:T(8,128)(2,1)S(1)}, f32[160,128]{1,0:T(8,128)S(1)}, f32[160,128]{1,0:T(8,128)S(1)}, f...) custom-call(s32[2]{0:T(128)S(1)} %pad_add_fusion.place_ref, f32[4,512]{1,0:T(4,128)S(1)} %collective-permute-done.3.sa_ref, ...), custom_call_target="tpu_custom_call" | custom-call | flops 671088640 | bytes 8732672 | tf_op jit(solution)/shard_map/pallas_call | solution.py:96
  82.7 3.2 %shard_map.39 = (bf16[4096,128]{1,0:T(8,128)(2,1)S(1)}, bf16[128,4096]{1,0:T(8,128)(2,1)S(1)}, f32[224,128]{1,0:T(8,128)S(1)}, f32[224,128]{1,0:T(8,128)S(1)}, f...) custom-call(s32[2]{0:T(128)S(1)} %pad_add_fusion.place_ref, f32[4,512]{1,0:T(4,128)S(1)} %collective-permute-done.3.sa_ref, ...), custom_call_target="tpu_custom_call" | custom-call | flops 939524096 | bytes 10960896 | tf_op jit(solution)/shard_map/pallas_call | solution.py:96
  86.5 12.5 %collective-permute-done.15.a_ref = bf16[4096,128]{1,0:T(8,128)(2,1)} collective-permute-done((bf16[4096,128]{1,0:T(8,128)(2,1)}, bf16[4096,128]{1,0:T(8,128)(2,1)}, u32[]{:S(2)}, u32[]{:S(2)}) %collective-permute-start.15) | collective-permute-done | bytes 1048608 | tf_op jit(solution)/shard_map/ppermute | solution.py:19
  99.0 4.1 %shard_map.40 = (bf16[4096,128]{1,0:T(8,128)(2,1)S(1)}, bf16[128,4096]{1,0:T(8,128)(2,1)S(1)}, f32[288,128]{1,0:T(8,128)S(1)}, f32[288,128]{1,0:T(8,128)S(1)}, f...) custom-call(s32[2]{0:T(128)S(1)} %pad_add_fusion.place_ref, f32[4,512]{1,0:T(4,128)S(1)} %collective-permute-done.3.sa_ref, ...), custom_call_target="tpu_custom_call" | custom-call | flops 1207959552 | bytes 13189120 | tf_op jit(solution)/shard_map/pallas_call | solution.py:96
  103.7 14.8 %collective-permute-done.20.a_ref = bf16[4096,128]{1,0:T(8,128)(2,1)S(1)} collective-permute-done((bf16[4096,128]{1,0:T(8,128)(2,1)}, bf16[4096,128]{1,0:T(8,128)(2,1)S(1)}, u32[]{:S(2)}, u32[]{:S(2)}) %collective-permute-start.20) | collective-permute-done | bytes 1048608 | tf_op jit(solution)/shard_map/ppermute | solution.py:19
  118.5 3.6 %shard_map.41 = (f32[2,352,128]{2,1,0:T(8,128)S(1)}, f32[2,352,128]{2,1,0:T(8,128)S(1)}) custom-call(s32[2]{0:T(128)S(1)} %pad_add_fusion.place_ref, f32[4,512]{1,0:T(4,128)S(1)} %collective-permute-done.3.sa_ref, f32[4,512]{1,0:T(4,128)S(1)} %collective-permute-done.4.sb_ref, bf16[4096,128]{1,0:T(8,128)(2,1)S(1)} %collective-permute-done.20.a_ref, ...), custom_call_target="tpu_custom_call" | custom-call | flops 1476395008 | bytes 13320192 | tf_op jit(solution)/shard_map/pallas_call | solution.py:96
  126.1 3.8 %collective-permute-done.13 = f32[224,128]{1,0:T(8,128)S(1)} collective-permute-done((f32[224,128]{1,0:T(8,128)S(1)}, f32[224,128]{1,0:T(8,128)S(1)}, u32[]{:S(2)}, u32[]{:S(2)}) %collective-permute-start.13) | collective-permute-done | bytes 114720 | tf_op jit(solution)/shard_map/ppermute | solution.py:136
  132.4 4.1 %collective-permute-done.18 = f32[288,128]{1,0:T(8,128)S(1)} collective-permute-done((f32[288,128]{1,0:T(8,128)S(1)}, f32[288,128]{1,0:T(8,128)S(1)}, u32[]{:S(2)}, u32[]{:S(2)}) %collective-permute-start.18) | collective-permute-done | bytes 147488 | tf_op jit(solution)/shard_map/ppermute | solution.py:136
  138.1 4.2 %collective-permute-done.2 = f32[128,512]{1,0:T(8,128)S(1)} collective-permute-done((f32[128,512]{1,0:T(8,128)S(1)}, f32[128,512]{1,0:T(8,128)S(1)}, u32[]{:S(2)}, u32[]{:S(2)}) %collective-permute-start.2) | collective-permute-done | bytes 262176 | tf_op jit(solution)/shard_map/ppermute | solution.py:136
  143.9 2.9 %collective-permute-start.23 = (f32[128,128]{1,0:T(8,128)S(1)}, f32[128,128]{1,0:T(8,128)S(1)}, u32[]{:S(2)}, u32[]{:S(2)}) collective-permute-start(f32[128,128]{1,0:T(8,128)S(1)} %slice_bitcast_fusion.2), channel_id=1, source_target_pairs={{0,2},{1,3},{2,0},{3,1},{4,6},{5,7},{6,4},{7,5},{8,10},{9,11},{10,... | collective-permute-start | bytes 196616 | tf_op jit(solution)/shard_map/ppermute | solution.py:208
  149.6 5.7 %collective-permute-done.26 = f32[224,128]{1,0:T(8,128)S(1)} collective-permute-done((f32[224,128]{1,0:T(8,128)S(1)}, f32[224,128]{1,0:T(8,128)S(1)}, u32[]{:S(2)}, u32[]{:S(2)}) %collective-permute-start.26) | collective-permute-done | bytes 114720 | tf_op jit(solution)/shard_map/ppermute | solution.py:206
  (96 shorter events, 26.6 us)
Async XLA Ops:
  12.7 26.4 %collective-permute-start.4 = (f32[4,512]{1,0:T(4,128)S(1)}, f32[4,512]{1,0:T(4,128)S(1)}, u32[]{:S(2)}, u32[]{:S(2)}) collective-permute-start(f32[4,512]{1,0:T(4,128)S(1)} %pad_maximum_fusion.1), channel_id=1, source_target_pairs={{4,8},{8,4},{5,9},{9,5},{6,10},{10,6},{7,11},{11,7},{20,24},{24,20... | collective-permute-start | bytes 24584 | tf_op jit(solution)/shard_map/ppermute | solution.py:19
  13.3 27.4 %collective-permute-start.3 = (f32[4,512]{1,0:T(4,128)S(1)}, f32[4,512]{1,0:T(4,128)S(1)}, u32[]{:S(2)}, u32[]{:S(2)}) collective-permute-start(f32[4,512]{1,0:T(4,128)S(1)} %pad_maximum_fusion.1), channel_id=1, source_target_pairs={{0,4},{4,0},{8,12},{12,8},{1,5},{5,1},{9,13},{13,9},{2,6},{6,2},{1... | collective-permute-start | bytes 24584 | tf_op jit(solution)/shard_map/ppermute | solution.py:19
  21.4 20.2 %collective-permute-start.11 = (bf16[4096,128]{1,0:T(8,128)(2,1)S(1)}, bf16[4096,128]{1,0:T(8,128)(2,1)S(1)}, u32[]{:S(2)}, u32[]{:S(2)}) collective-permute-start(bf16[4096,128]{1,0:T(8,128)(2,1)S(1)} %fusion.4), channel_id=1, source_target_pairs={{4,8},{8,4},{5,9},{9,5},{6,10},{10,6},{7,11},{11,7},{20,24},{24,20... | collective-permute-start | bytes 3145736 | tf_op jit(solution)/shard_map/ppermute | solution.py:19
  23.5 26.0 %collective-permute-start.6 = (bf16[4096,128]{1,0:T(8,128)(2,1)S(1)}, bf16[4096,128]{1,0:T(8,128)(2,1)S(1)}, u32[]{:S(2)}, u32[]{:S(2)}) collective-permute-start(bf16[4096,128]{1,0:T(8,128)(2,1)S(1)} %fusion.2), channel_id=1, source_target_pairs={{4,8},{8,4},{5,9},{9,5},{6,10},{10,6},{7,11},{11,7},{20,24},{24,20... | collective-permute-start | bytes 3145736 | tf_op jit(solution)/shard_map/ppermute | solution.py:19
  25.5 48.7 %collective-permute-start.5 = (bf16[4096,128]{1,0:T(8,128)(2,1)S(1)}, bf16[4096,128]{1,0:T(8,128)(2,1)S(1)}, u32[]{:S(2)}, u32[]{:S(2)}) collective-permute-start(bf16[4096,128]{1,0:T(8,128)(2,1)S(1)} %fusion.1), channel_id=1, source_target_pairs={{0,4},{4,0},{8,12},{12,8},{1,5},{5,1},{9,13},{13,9},{2,6},{6,2},{1... | collective-permute-start | bytes 3145736 | tf_op jit(solution)/shard_map/ppermute | solution.py:19
  39.1 46.9 %collective-permute-start.16 = (bf16[4096,128]{1,0:T(8,128)(2,1)}, bf16[4096,128]{1,0:T(8,128)(2,1)}, u32[]{:S(2)}, u32[]{:S(2)}) collective-permute-start(bf16[4096,128]{1,0:T(8,128)(2,1)} %fusion.6), channel_id=1, source_target_pairs={{4,8},{8,4},{5,9},{9,5},{6,10},{10,6},{7,11},{11,7},{20,24},{24,20... | collective-permute-start | bytes 3145736 | tf_op jit(solution)/shard_map/ppermute | solution.py:19
  40.7 62.4 %collective-permute-start.21 = (bf16[4096,128]{1,0:T(8,128)(2,1)}, bf16[4096,128]{1,0:T(8,128)(2,1)S(1)}, u32[]{:S(2)}, u32[]{:S(2)}) collective-permute-start(bf16[4096,128]{1,0:T(8,128)(2,1)} %fusion.8), channel_id=1, source_target_pairs={{4,8},{8,4},{5,9},{9,5},{6,10},{10,6},{7,11},{11,7},{20,24},{24,20... | collective-permute-start | bytes 3145736 | tf_op jit(solution)/shard_map/ppermute | solution.py:19
  41.6 41.0 %collective-permute-start.10 = (bf16[4096,128]{1,0:T(8,128)(2,1)}, bf16[4096,128]{1,0:T(8,128)(2,1)}, u32[]{:S(2)}, u32[]{:S(2)}) collective-permute-start(bf16[4096,128]{1,0:T(8,128)(2,1)} %fusion.3), channel_id=1, source_target_pairs={{0,4},{4,0},{8,12},{12,8},{1,5},{5,1},{9,13},{13,9},{2,6},{6,2},{1... | collective-permute-start | bytes 3145736 | tf_op jit(solution)/shard_map/ppermute | solution.py:19
  49.4 49.6 %collective-permute-start.15 = (bf16[4096,128]{1,0:T(8,128)(2,1)}, bf16[4096,128]{1,0:T(8,128)(2,1)}, u32[]{:S(2)}, u32[]{:S(2)}) collective-permute-start(bf16[4096,128]{1,0:T(8,128)(2,1)} %fusion.5), channel_id=1, source_target_pairs={{0,4},{4,0},{8,12},{12,8},{1,5},{5,1},{9,13},{13,9},{2,6},{6,2},{1... | collective-permute-start | bytes 3145736 | tf_op jit(solution)/shard_map/ppermute | solution.py:19
  75.1 43.4 %collective-permute-start.20 = (bf16[4096,128]{1,0:T(8,128)(2,1)}, bf16[4096,128]{1,0:T(8,128)(2,1)S(1)}, u32[]{:S(2)}, u32[]{:S(2)}) collective-permute-start(bf16[4096,128]{1,0:T(8,128)(2,1)} %fusion.7), channel_id=1, source_target_pairs={{0,4},{4,0},{8,12},{12,8},{1,5},{5,1},{9,13},{13,9},{2,6},{6,2},{1... | collective-permute-start | bytes 3145736 | tf_op jit(solution)/shard_map/ppermute | solution.py:19
  82.6 55.4 %collective-permute-start = (f32[128,512]{1,0:T(8,128)S(1)}, f32[128,512]{1,0:T(8,128)S(1)}, u32[]{:S(2)}, u32[]{:S(2)}) collective-permute-start(f32[128,512]{1,0:T(8,128)S(1)} %get-tuple-element.31), channel_id=1, source_target_pairs={{0,1},{1,0},{2,3},{3,2},{4,5},{5,4},{6,7},{7,6},{8,9},{9,8},{10,11... | collective-permute-start | bytes 786440 | tf_op jit(solution)/shard_map/ppermute | solution.py:136
  86.0 52.1 %collective-permute-start.1 = (f32[128,512]{1,0:T(8,128)S(1)}, f32[128,512]{1,0:T(8,128)S(1)}, u32[]{:S(2)}, u32[]{:S(2)}) collective-permute-start(f32[128,512]{1,0:T(8,128)S(1)} %get-tuple-element.32), channel_id=1, source_target_pairs={{0,2},{1,3},{2,0},{3,1},{4,6},{5,7},{6,4},{7,5},{8,10},{9,11},{10,... | collective-permute-start | bytes 786440 | tf_op jit(solution)/shard_map/ppermute | solution.py:136
  99.0 23.1 %collective-permute-start.7 = (f32[160,128]{1,0:T(8,128)S(1)}, f32[160,128]{1,0:T(8,128)S(1)}, u32[]{:S(2)}, u32[]{:S(2)}) collective-permute-start(f32[160,128]{1,0:T(8,128)S(1)} %get-tuple-element.36), channel_id=1, source_target_pairs={{0,1},{1,0},{2,3},{3,2},{4,5},{5,4},{6,7},{7,6},{8,9},{9,8},{10,11... | collective-permute-start | bytes 245768 | tf_op jit(solution)/shard_map/ppermute | solution.py:136
  103.2 20.7 %collective-permute-start.8 = (f32[160,128]{1,0:T(8,128)S(1)}, f32[160,128]{1,0:T(8,128)S(1)}, u32[]{:S(2)}, u32[]{:S(2)}) collective-permute-start(f32[160,128]{1,0:T(8,128)S(1)} %get-tuple-element.37), channel_id=1, source_target_pairs={{0,2},{1,3},{2,0},{3,1},{4,6},{5,7},{6,4},{7,5},{8,10},{9,11},{10,... | collective-permute-start | bytes 245768 | tf_op jit(solution)/shard_map/ppermute | solution.py:136
  123.8 6.0 %collective-permute-start.13 = (f32[224,128]{1,0:T(8,128)S(1)}, f32[224,128]{1,0:T(8,128)S(1)}, u32[]{:S(2)}, u32[]{:S(2)}) collective-permute-start(f32[224,128]{1,0:T(8,128)S(1)} %get-tuple-element.43), channel_id=1, source_target_pairs={{0,2},{1,3},{2,0},{3,1},{4,6},{5,7},{6,4},{7,5},{8,10},{9,11},{10,... | collective-permute-start | bytes 344072 | tf_op jit(solution)/shard_map/ppermute | solution.py:136
  124.3 6.2 %collective-permute-start.14 = (f32[224,128]{1,0:T(8,128)S(1)}, f32[224,128]{1,0:T(8,128)S(1)}, u32[]{:S(2)}, u32[]{:S(2)}) collective-permute-start(f32[224,128]{1,0:T(8,128)S(1)} %get-tuple-element.44), channel_id=1, source_target_pairs={{0,3},{1,2},{2,1},{3,0},{4,7},{5,6},{6,5},{7,4},{8,11},{9,10},{10,... | collective-permute-start | bytes 344072 | tf_op jit(solution)/shard_map/ppermute | solution.py:136
  125.3 6.7 %collective-permute-start.17 = (f32[288,128]{1,0:T(8,128)S(1)}, f32[288,128]{1,0:T(8,128)S(1)}, u32[]{:S(2)}, u32[]{:S(2)}) collective-permute-start(f32[288,128]{1,0:T(8,128)S(1)} %get-tuple-element.48), channel_id=1, source_target_pairs={{0,1},{1,0},{2,3},{3,2},{4,5},{5,4},{6,7},{7,6},{8,9},{9,8},{10,11... | collective-permute-start | bytes 442376 | tf_op jit(solution)/shard_map/ppermute | solution.py:136
  129.9 6.6 %collective-permute-start.18 = (f32[288,128]{1,0:T(8,128)S(1)}, f32[288,128]{1,0:T(8,128)S(1)}, u32[]{:S(2)}, u32[]{:S(2)}) collective-permute-start(f32[288,128]{1,0:T(8,128)S(1)} %get-tuple-element.49), channel_id=1, source_target_pairs={{0,2},{1,3},{2,0},{3,1},{4,6},{5,7},{6,4},{7,5},{8,10},{9,11},{10,... | collective-permute-start | bytes 442376 | tf_op jit(solution)/shard_map/ppermute | solution.py:136
  130.5 6.1 %collective-permute-start.19 = (f32[288,128]{1,0:T(8,128)S(1)}, f32[288,128]{1,0:T(8,128)S(1)}, u32[]{:S(2)}, u32[]{:S(2)}) collective-permute-start(f32[288,128]{1,0:T(8,128)S(1)} %get-tuple-element.50), channel_id=1, source_target_pairs={{0,3},{1,2},{2,1},{3,0},{4,7},{5,6},{6,5},{7,4},{8,11},{9,10},{10,... | collective-permute-start | bytes 442376 | tf_op jit(solution)/shard_map/ppermute | solution.py:136
  132.0 10.3 %collective-permute-start.2 = (f32[128,512]{1,0:T(8,128)S(1)}, f32[128,512]{1,0:T(8,128)S(1)}, u32[]{:S(2)}, u32[]{:S(2)}) collective-permute-start(f32[128,512]{1,0:T(8,128)S(1)} %get-tuple-element.33), channel_id=1, source_target_pairs={{0,3},{1,2},{2,1},{3,0},{4,7},{5,6},{6,5},{7,4},{8,11},{9,10},{10,... | collective-permute-start | bytes 786440 | tf_op jit(solution)/shard_map/ppermute | solution.py:136
  136.5 7.3 %collective-permute-start.22 = (f32[2,352,128]{2,1,0:T(8,128)S(1)}, f32[2,352,128]{2,1,0:T(8,128)S(1)}, u32[]{:S(2)}, u32[]{:S(2)}) collective-permute-start(f32[2,352,128]{2,1,0:T(8,128)S(1)} %get-tuple-element.54), channel_id=1, source_target_pairs={{0,1},{1,0},{2,3},{3,2},{4,5},{5,4},{6,7},{7,6},{8,9},{9,8},{10,11... | collective-permute-start | bytes 1081352 | tf_op jit(solution)/shard_map/ppermute | solution.py:200
  136.8 7.0 %collective-permute-start.24 = (f32[288,128]{1,0:T(8,128)S(1)}, f32[288,128]{1,0:T(8,128)S(1)}, u32[]{:S(2)}, u32[]{:S(2)}) collective-permute-start(f32[288,128]{1,0:T(8,128)S(1)} %pad_maximum_fusion), channel_id=1, source_target_pairs={{4,0},{8,4},{12,8},{5,1},{9,5},{13,9},{6,2},{10,6},{14,10},{7,3},{... | collective-permute-start | bytes 442376 | tf_op jit(solution)/shard_map/ppermute | solution.py:195
  146.8 8.5 %collective-permute-start.26 = (f32[224,128]{1,0:T(8,128)S(1)}, f32[224,128]{1,0:T(8,128)S(1)}, u32[]{:S(2)}, u32[]{:S(2)}) collective-permute-start(f32[224,128]{1,0:T(8,128)S(1)} %get-tuple-element.59), channel_id=1, source_target_pairs={{4,2},{5,3},{6,0},{7,1},{8,6},{9,7},{10,4},{11,5},{12,10},{13,11},... | collective-permute-start | bytes 344072 | tf_op jit(solution)/shard_map/ppermute | solution.py:206
  148.1 8.4 %collective-permute-start.25 = (f32[224,128]{1,0:T(8,128)S(1)}, f32[224,128]{1,0:T(8,128)S(1)}, u32[]{:S(2)}, u32[]{:S(2)}) collective-permute-start(f32[224,128]{1,0:T(8,128)S(1)} %get-tuple-element.60), channel_id=1, source_target_pairs={{4,0},{5,1},{6,2},{7,3},{8,4},{9,5},{10,6},{11,7},{12,8},{13,9},{1... | collective-permute-start | bytes 344072 | tf_op jit(solution)/shard_map/ppermute | solution.py:206
  (10 other events, 65.2 us)

commit v3 on v2

--- a/solution.py
+++ b/solution.py
@@ -10,6 +10,7 @@
 
 LANES = 128
 DEPTH = 1024
+BLOCKS = 8
 
 
 def exchange(array, devices, first):
@@ -34,6 +35,70 @@
         parts = [jnp.where(swap, parts[t ^ bit], parts[t]) for t in range(len(parts))]
         bit *= 2
     return parts
+
+
+def choose(width, samp, j, even):
+    step = LANES
+    part, share = width // samp, step // samp
+    lane = lax.broadcasted_iota(jnp.int32, (width, step), 1)
+    row = lax.broadcasted_iota(jnp.int32, (width, step), 0)
+    up = lane // share * part + j * share + lane % share
+    down = j * step + lane
+    first, second = jnp.where(even, up, down), jnp.where(even, down, up)
+    return jnp.concatenate([row == first, row == second], 1).astype(jnp.float32).astype(jnp.bfloat16)
+
+
+def front_kernel(samp, place_ref, values_hbm, a_hbm, b_hbm, values_ref, a_ref, b_ref, sems):
+    rows, width = values_ref.shape
+    blocks = sems.shape[1]
+    size = rows // blocks
+    spans = [pl.ds(k * size, size) for k in range(blocks)]
+    arrive = [pltpu.make_async_copy(values_hbm.at[s], values_ref.at[s], sems.at[0, k]) for k, s in enumerate(spans)]
+    leave = [pltpu.make_async_copy(a_ref.at[s], a_hbm.at[s], sems.at[1, k]) for k, s in enumerate(spans)]
+    leave += [pltpu.make_async_copy(b_ref.at[s], b_hbm.at[s], sems.at[2, k]) for k, s in enumerate(spans)]
+    for copy in arrive:
+        copy.start()
+    chosen = choose(width, samp, 0, place_ref[0] != 0)
+    for k, span in enumerate(spans):
+        arrive[k].wait()
+        both = matmul(values_ref[span, :], chosen).astype(jnp.bfloat16)
+        a_ref[span, :] = both[:, :LANES]
+        b_ref[span, :] = both[:, LANES:]
+        leave[k].start()
+        leave[blocks + k].start()
+    for copy in leave:
+        copy.wait()
+
+
+def pick_kernel(samp, j, place_ref, values_ref, a_ref, b_ref):
+    rows, width = values_ref.shape
+    chosen = choose(width, samp, j, place_ref[0] != 0)
+    for k in range(0, rows, DEPTH):
+        span = pl.ds(k, DEPTH)
+        both = matmul(values_ref[span, :], chosen).astype(jnp.bfloat16)
+        a_ref[span, :] = both[:, :LANES]
+        b_ref[span, :] = both[:, LANES:]
+
+
+def final_kernel(samples, chunks, share, tile_ref, kept_ref, other_ref, early_ref, far0_ref, far1_ref, *rest):
+    nears, out_ref = rest[:-1], rest[-1]
+    part = tile_ref.shape[0]
+    step = LANES
+    scale = 1.0 / samples
+    out_ref[0] = tile_ref[...] * scale
+    for j, near_ref in enumerate(nears):
+        out_ref[1, :, j * step : (j + 1) * step] = near_ref[:part, :] * scale
+    out_ref[1, :, len(nears) * step :] = (kept_ref[0, :part, :] + other_ref[...]) * scale
+    at = 0
+    for j in range(chunks):
+        names = [(i, j) for i in range(j)] + [(j, j)] + [(j, i) for i in range(j)]
+        if j == chunks - 1:
+            at = 0
+        for row, column in names:
+            rows = slice(at, at + share)
+            piece = early_ref[rows, :] if j < chunks - 1 else far0_ref[rows, :] + far1_ref[rows, :]
+            out_ref[2, row * share : (row + 1) * share, column * step : (column + 1) * step] = piece * scale
+            at += share
 
 
 def own_kernel(samp, place_ref, values_ref, mean_ref, scale_ref, own_ref, *outs):
@@ -90,20 +155,27 @@
             row += size
 
 
-def call(kernel, out_shapes, flops, *args):
+def call(kernel, out_shapes, flops, *args, scalars=True, in_hbm=(), scratch=(), out_space=pltpu.VMEM, limit=None):
     vmem = pl.BlockSpec(memory_space=pltpu.VMEM)
-    moved = sum(x.size * x.dtype.itemsize for x in args[1:]) + sum(x.size * x.dtype.itemsize for x in out_shapes)
+    specs = [vmem] * len(args)
+    if scalars:
+        specs[0] = pl.BlockSpec(memory_space=pltpu.SMEM)
+    for n in in_hbm:
+        specs[n] = pl.BlockSpec(memory_space=pltpu.HBM)
+    moved = sum(x.size * x.dtype.itemsize for x in args) + sum(x.size * x.dtype.itemsize for x in out_shapes)
     return pl.pallas_call(
         kernel,
         out_shape=out_shapes,
-        in_specs=[pl.BlockSpec(memory_space=pltpu.SMEM)] + [vmem] * (len(args) - 1),
-        out_specs=[vmem] * len(out_shapes),
+        in_specs=specs,
+        out_specs=[pl.BlockSpec(memory_space=out_space)] * len(out_shapes),
+        scratch_shapes=scratch,
         cost_estimate=pl.CostEstimate(flops=flops, bytes_accessed=moved, transcendentals=0),
-        compiler_params=pltpu.CompilerParams(vmem_limit_bytes=VMEM_LIMIT),
+        compiler_params=pltpu.CompilerParams(vmem_limit_bytes=limit or VMEM_LIMIT),
     )(*args)
 
 
-VMEM_LIMIT = 32 * 2**20
+VMEM_LIMIT = 20 * 2**20
+FRONT_LIMIT = 54 * 2**20
 
 
 def body(dosage, filter_mask, counts):
@@ -123,13 +195,6 @@
         grid = vector.reshape(*lead, samp, chunks, share)
         return jnp.swapaxes(grid, -3, -2).reshape(*lead, width)
 
-    def payload(j, up):
-        lane = jnp.arange(step, dtype=jnp.int32)
-        upward = lane // share * part + j * share + lane % share
-        source = jnp.where(up, upward, j * step + lane)
-        chosen = jnp.arange(width, dtype=jnp.int32)[:, None] == source[None, :]
-        return jnp.dot(dosage, chosen.astype(jnp.bfloat16), preferred_element_type=jnp.float32).astype(jnp.bfloat16)
-
     def scatter_sum(parts):
         total = parts[0]
         for d in range(1, samp):
@@ -143,9 +208,24 @@
         return jax.ShapeDtypeStruct(shape, jnp.bfloat16)
 
     raw = []
+    chunk = bf16(local_rows, step)
+    flops = 4 * local_rows * width * step
     for j in range(chunks):
-        a = exchange(payload(j, even), chain, 0)
-        b = exchange(payload(j, ~even), chain, 1)
+        if j == 0:
+            a, b = call(
+                functools.partial(front_kernel, samp), [chunk, chunk], flops, place, dosage, in_hbm=(1,),
+                out_space=pltpu.HBM, limit=FRONT_LIMIT,
+                scratch=[
+                    pltpu.VMEM(dosage.shape, dosage.dtype),
+                    pltpu.VMEM(chunk.shape, chunk.dtype),
+                    pltpu.VMEM(chunk.shape, chunk.dtype),
+                    pltpu.SemaphoreType.DMA((3, BLOCKS)),
+                ],
+            )
+        else:
+            a, b = call(functools.partial(pick_kernel, samp, j), [chunk, chunk], flops, place, dosage)
+        a = exchange(a, chain, 0)
+        b = exchange(b, chain, 1)
         raw.append((a, b))
 
     values = dosage.astype(jnp.float32)
@@ -168,61 +248,42 @@
     )
     tile = scatter_sum(parts)
 
-    nears, fars, near_done, shipped = [], [], [], []
-    far_done = {}
+    nears, fars, totals = [], [], []
     for j in range(chunks):
         size = part + (2 * j + 1) * share
         last = j == chunks - 1
         results = [f32(samp // 2, size, step)] * 2 if last else [f32(size, step)] * samp
         saved = [] if last else [bf16(local_rows, step), bf16(step, local_rows)]
-        *kept, = call(
+        kept = call(
             functools.partial(step_kernel, samp, j, len(results)),
             saved + results,
             2 * local_rows * step * (width + (2 * j + 1) * step),
             place, sa, sb, *raw[j], own, *nears, *fars,
         )
         parts = kept[len(saved) :]
-        nears += kept[:1] if saved else []
-        fars += kept[1:2] if saved else []
-        names = [(i, j) for i in range(j)] + [(j, j)] + [(j, i) for i in range(j)]
-        for at, name in enumerate(names):
-            far_done[name] = (j, at)
         if not last:
-            total = scatter_sum(parts)
-            near_done.append(total[:part])
-            shipped.append(total[part:])
-            if j == chunks - 2:
-                early = lax.ppermute(
-                    jnp.concatenate(shipped), "chain", [(i + 1, i) for i in range(chain - 1)]
-                )
-        else:
-            pair = 2
-            kept = parts[0] + lax.ppermute(parts[1], "samp", [(i, i ^ 1) for i in range(samp)])
-            near_total, far_total = kept[0][:part], 0.0
-            for n in range(samp // pair):
-                out = kept[n]
-                moved = [i ^ (n * pair) for i in range(samp)]
-                pairs = [((c + 1) * samp + i, c * samp + moved[i]) for c in range(chain - 1) for i in range(samp)]
-                far_total = far_total + lax.ppermute(out[part:], ("chain", "samp"), pairs)
-                if n:
-                    near_total = near_total + lax.ppermute(out[:part], "samp", [(i, moved[i]) for i in range(samp)])
-            near_done.append(near_total)
-    starts, row = [], 0
-    for piece in shipped:
-        starts.append(row)
-        row += piece.shape[0]
-
-    def far_block(i, j):
-        at, place = far_done[i, j]
-        if at == chunks - 1:
-            return far_total[place * share : (place + 1) * share]
-        return early[starts[at] + place * share : starts[at] + (place + 1) * share]
-
-    far = jnp.concatenate(
-        [jnp.concatenate([far_block(i, j) for j in range(chunks)], 1) for i in range(chunks)], 0
+            nears.append(kept[0])
+            fars.append(kept[1])
+            totals.append(scatter_sum(parts))
+    early = lax.ppermute(
+        jnp.concatenate([total[part:] for total in totals]), "chain", [(i + 1, i) for i in range(chain - 1)]
     )
-    out = jnp.stack([tile, jnp.concatenate(near_done, 1), far], 1) / samples
-    return out[None]
+    kept = parts[0] + lax.ppermute(parts[1], "samp", [(i, i ^ 1) for i in range(samp)])
+    others, far = [], []
+    for n in range(samp // 2):
+        moved = [i ^ (2 * n) for i in range(samp)]
+        pairs = [((c + 1) * samp + i, c * samp + moved[i]) for c in range(chain - 1) for i in range(samp)]
+        far.append(lax.ppermute(kept[n, part:], ("chain", "samp"), pairs))
+        if n:
+            others.append(lax.ppermute(kept[n, :part], "samp", [(i, moved[i]) for i in range(samp)]))
+    (out,) = call(
+        functools.partial(final_kernel, samples, chunks, share),
+        [f32(3, part, width)],
+        0,
+        tile, kept, sum(others), early, far[0], sum(far[1:]), *totals,
+        scalars=False,
+    )
+    return jnp.swapaxes(out, 0, 1)[None]
 
 
 def solution(mesh):

time: 158 us -> 141 us (0.89)
  matrix products: 17.4 us -> 0 us
  Pallas kernels: 16.1 us -> 27.6 us
  starting transfers between devices: 57.8 us -> 50.6 us
  other arithmetic: 4.73 us -> 2.1 us
  blocking collectives: 8.36 us -> 6.59 us
    dot_general x8 -> x0, matrix products: 17.4 us -> none  [payload(): jnp.dot(dosage, chosen.astype(jnp.bfloat16), preferred_element_type=jnp.f...]
    pallas_call x5 -> x10, Pallas kernels: 16.1 us -> 27.6 us  [call(): pl.pallas_call(kernel, out_shape=out_shapes, in_specs=specs, out_specs=[p...]
    ppermute x10, starting transfers between devices: 43.9 us -> 38.6 us  [exchange(): lax.ppermute(array, 'chain', pairs)]
    ppermute x4, waiting for transfers between devices: 8.41 us -> 4.73 us  [the longest x1 4.73 us: body(): lax.ppermute(kept[n, :part], 'samp', [(i, moved[i]) for i in range(samp)])]
    ppermute x4, starting transfers between devices: 6.74 us -> 4.01 us  [the longest x2 2.58 us: body(): far.append(lax.ppermute(kept[n, part:], ('chain', 'samp'), pairs))]
    ppermute x12, waiting for transfers between devices: 12.7 us -> 15.1 us  [scatter_sum(): lax.ppermute(parts[d], 'samp', [(i, i ^ d) for i in range(samp)])]
    reduce_sum x1, other arithmetic: 3.33 us -> 1.14 us  [body(): jnp.sum(values * values, 0)]
    ppermute x10, waiting for transfers between devices: 27.3 us -> 29.5 us  [exchange(): lax.ppermute(array, 'chain', pairs)]
  transfers between devices with their start and end apart: 27 -> 27, of which waited for: 11 -> 10; matrix products, arithmetic and copies ran while one was open for 11% -> 1% of each run, Pallas kernels for 10% -> 15%
where the time goes in v3:
time: 141 us
  starting transfers between devices  50.6 us (36%)
  waiting for transfers between devices  49.3 us (35%)
  Pallas kernels  27.6 us (20%)
  blocking collectives  6.59 us (5%)
  local copies, waits for them, and re-layouts  3.47 us (2%)
  other arithmetic  2.1 us (1%)
    ppermute x10, starting transfers between devices, exchange(): lax.ppermute(array, 'chain', pairs)  38.6 us
    ppermute x10, waiting for transfers between devices, exchange(): lax.ppermute(array, 'chain', pairs)  29.5 us
    pallas_call x10, Pallas kernels, call(): pl.pallas_call(kernel, out_shape=out_shapes, in_specs=specs, out_specs=[p...  27.6 us
    ppermute x12, waiting for transfers between devices, scatter_sum(): lax.ppermute(parts[d], 'samp', [(i, i ^ d) for i in range(samp)])  15.1 us
    psum x1, blocking collectives, body(): lax.psum((jnp.sum(values, 0), jnp.sum(values * values, 0)), 'samp')  6.59 us
    ppermute x12, starting transfers between devices, scatter_sum(): lax.ppermute(parts[d], 'samp', [(i, i ^ d) for i in range(samp)])  6.19 us
    ppermute x1, waiting for transfers between devices, body(): lax.ppermute(kept[n, :part], 'samp', [(i, moved[i]) for i in range(samp)])  4.73 us
    unnamed x10, local copies, waits for them, and re-layouts  3.17 us
  transfers between devices with their start and end apart: 27, of which 10 were waited for; matrix products, arithmetic and copies ran while one was open for 1% of the time, Pallas kernels for 15%

profile of v3, /device:TPU:0, one launch (start us, length us, event | category | flops | bytes accessed | tf_op | source)
XLA Modules:
  0.0 140.5 jit_solution(17005755431139275004)
XLA Ops:
  0.7 6.1 %shard_map.39 = (bf16[4096,128]{1,0:T(8,128)(2,1)}, bf16[4096,128]{1,0:T(8,128)(2,1)}) custom-call(s32[2]{0:T(128)} %pad_add_fusion.place_ref, bf16[4096,512]{1,0:T(8,128)(2,1)} %values_ref.7), custom_call_target="tpu_custom_call" | custom-call | flops 1073741824 | bytes 6291464 | tf_op jit(solution)/shard_map/pallas_call | solution.py:166
  6.8 3.1 %collective-permute-start.7 = (bf16[4096,128]{1,0:T(8,128)(2,1)}, bf16[4096,128]{1,0:T(8,128)(2,1)S(1)}, u32[]{:S(2)}, u32[]{:S(2)}) collective-permute-start(bf16[4096,128]{1,0:T(8,128)(2,1)} %get-tuple-element.45), channel_id=1, source_target_pairs={{0,4},{4,0},{8,12},{12,8},{1,5},{5,1},{9,13},{13,9},{2,6},{6,2},{1... | collective-permute-start | bytes 3145736 | tf_op jit(solution)/shard_map/ppermute | solution.py:20
  10.8 2.8 %shard_map.41 = (bf16[4096,128]{1,0:T(8,128)(2,1)S(1)}, bf16[4096,128]{1,0:T(8,128)(2,1)}) custom-call(s32[2]{0:T(128)S(1)} %copy-done.2, bf16[4096,512]{1,0:T(8,128)(2,1)S(1)} %copy-done), custom_call_target="tpu_custom_call" | custom-call | flops 1073741824 | bytes 6291464 | tf_op jit(solution)/shard_map/pallas_call | solution.py:166
  17.0 6.6 %all-reduce = (f32[512]{0:T(512)S(1)}, f32[512]{0:T(512)S(1)}) all-reduce(f32[512]{0:T(512)S(1)} %get-tuple-element.72, f32[512]{0:T(512)S(1)} %get-tuple-element.71), channel_id=1, replica_groups=mesh['groups'=2,'chain'=4,'samp'=4] {'samp'}, use_global_device_ids=true, to_apply=%region_1.2 | all-reduce | flops 1024 | bytes 8192 | tf_op jit(solution)/shard_map/psum | solution.py:232
  24.0 5.3 %collective-permute-start.3 = (f32[4,512]{1,0:T(4,128)S(1)}, f32[4,512]{1,0:T(4,128)S(1)}, u32[]{:S(2)}, u32[]{:S(2)}) collective-permute-start(f32[4,512]{1,0:T(4,128)S(1)} %pad_maximum_fusion.1), channel_id=1, source_target_pairs={{0,4},{4,0},{8,12},{12,8},{1,5},{5,1},{9,13},{13,9},{2,6},{6,2},{1... | collective-permute-start | bytes 24584 | tf_op jit(solution)/shard_map/ppermute | solution.py:20
  29.9 3.5 %collective-permute-done.3.sa_ref = f32[4,512]{1,0:T(4,128)S(1)} collective-permute-done((f32[4,512]{1,0:T(4,128)S(1)}, f32[4,512]{1,0:T(4,128)S(1)}, u32[]{:S(2)}, u32[]{:S(2)}) %collective-permute-start.3) | collective-permute-done | bytes 8224 | tf_op jit(solution)/shard_map/ppermute | solution.py:20
  35.2 2.2 %copy-done.1 = bf16[4096,512]{1,0:T(8,128)(2,1)S(1)} copy-done((bf16[4096,512]{1,0:T(8,128)(2,1)S(1)}, bf16[4096,512]{1,0:T(8,128)(2,1)}, u32[]{:S(2)}) %copy-start.1) | copy-done | bytes 4194328
  37.4 1.8 %shard_map.43 = (bf16[4096,128]{1,0:T(8,128)(2,1)S(1)}, bf16[4096,128]{1,0:T(8,128)(2,1)S(1)}) custom-call(s32[2]{0:T(128)S(1)} %copy-done.2, bf16[4096,512]{1,0:T(8,128)(2,1)S(1)} %copy-done.1), custom_call_target="tpu_custom_call" | custom-call | flops 1073741824 | bytes 6291464 | tf_op jit(solution)/shard_map/pallas_call | solution.py:166
  39.2 21.6 %collective-permute-start.11 = (bf16[4096,128]{1,0:T(8,128)(2,1)S(1)}, bf16[4096,128]{1,0:T(8,128)(2,1)S(1)}, u32[]{:S(2)}, u32[]{:S(2)}) collective-permute-start(bf16[4096,128]{1,0:T(8,128)(2,1)S(1)} %get-tuple-element.52), channel_id=1, source_target_pairs={{0,4},{4,0},{8,12},{12,8},{1,5},{5,1},{9,13},{13,9},{2,6},{6,2},{1... | collective-permute-start | bytes 3145736 | tf_op jit(solution)/shard_map/ppermute | solution.py:20
  61.5 1.8 %shard_map.38 = (bf16[4096,128]{1,0:T(8,128)(2,1)S(1)}, bf16[4096,128]{1,0:T(8,128)(2,1)S(1)}) custom-call(s32[2]{0:T(128)S(1)} %copy-done.2, bf16[4096,512]{1,0:T(8,128)(2,1)S(1)} %copy-done.1), custom_call_target="tpu_custom_call" | custom-call | flops 1073741824 | bytes 6291464 | tf_op jit(solution)/shard_map/pallas_call | solution.py:166
  63.3 3.0 %collective-permute-start.5 = (bf16[4096,128]{1,0:T(8,128)(2,1)S(1)}, bf16[4096,128]{1,0:T(8,128)(2,1)S(1)}, u32[]{:S(2)}, u32[]{:S(2)}) collective-permute-start(bf16[4096,128]{1,0:T(8,128)(2,1)S(1)} %get-tuple-element.42), channel_id=1, source_target_pairs={{0,4},{4,0},{8,12},{12,8},{1,5},{5,1},{9,13},{13,9},{2,6},{6,2},{1... | collective-permute-start | bytes 3145736 | tf_op jit(solution)/shard_map/ppermute | solution.py:20
  67.2 2.9 %shard_map.37 = (bf16[512,4096]{1,0:T(8,128)(2,1)S(1)}, f32[128,512]{1,0:T(8,128)S(1)}, f32[128,512]{1,0:T(8,128)S(1)}, f32[128,512]{1,0:T(8,128)S(1)}, f32[128,512]{1,0:T(8,128)S(1)}) custom-call(s32[2]{0:T(128)S(1)} %copy-done.2, bf16[4096,512]{1,0:T(8,128)(2,1)S(1)} %copy-done.1, f32[1,512]{1,0:T(1,128)S(1)} %bitcast.20, f32[1,512]{1,0:T(1,128)S(1)} %bitcast.18), custom_call_target="tpu_custom_call" | custom-call | flops 2147483648 | bytes 9441288 | tf_op jit(solution)/shard_map/pallas_call | solution.py:166
  70.2 2.2 %shard_map.40 = (bf16[4096,128]{1,0:T(8,128)(2,1)S(1)}, bf16[128,4096]{1,0:T(8,128)(2,1)S(1)}, f32[160,128]{1,0:T(8,128)S(1)}, f32[160,128]{1,0:T(8,128)S(1)}, f...) custom-call(s32[2]{0:T(128)S(1)} %copy-done.2, f32[4,512]{1,0:T(4,128)S(1)} %collective-permute-done.3.sa_ref, ...), custom_call_target="tpu_custom_call" | custom-call | flops 671088640 | bytes 8732680 | tf_op jit(solution)/shard_map/pallas_call | solution.py:166
  72.5 2.5 %shard_map.42 = (bf16[4096,128]{1,0:T(8,128)(2,1)S(1)}, bf16[128,4096]{1,0:T(8,128)(2,1)S(1)}, f32[224,128]{1,0:T(8,128)S(1)}, f32[224,128]{1,0:T(8,128)S(1)}, f...) custom-call(s32[2]{0:T(128)S(1)} %copy-done.2, f32[4,512]{1,0:T(4,128)S(1)} %collective-permute-done.3.sa_ref, ...), custom_call_target="tpu_custom_call" | custom-call | flops 939524096 | bytes 10960904 | tf_op jit(solution)/shard_map/pallas_call | solution.py:166
  75.1 9.7 %collective-permute-done.11.a_ref = bf16[4096,128]{1,0:T(8,128)(2,1)S(1)} collective-permute-done((bf16[4096,128]{1,0:T(8,128)(2,1)S(1)}, bf16[4096,128]{1,0:T(8,128)(2,1)S(1)}, u32[]{:S(2)}, u32[]{:S(2)}) %collective-permute-start.11) | collective-permute-done | bytes 1048608 | tf_op jit(solution)/shard_map/ppermute | solution.py:20
  86.3 3.0 %shard_map.44 = (bf16[4096,128]{1,0:T(8,128)(2,1)S(1)}, bf16[128,4096]{1,0:T(8,128)(2,1)S(1)}, f32[288,128]{1,0:T(8,128)S(1)}, f32[288,128]{1,0:T(8,128)S(1)}, f...) custom-call(s32[2]{0:T(128)S(1)} %copy-done.2, f32[4,512]{1,0:T(4,128)S(1)} %collective-permute-done.3.sa_ref, ...), custom_call_target="tpu_custom_call" | custom-call | flops 1207959552 | bytes 13189128 | tf_op jit(solution)/shard_map/pallas_call | solution.py:166
  89.4 16.2 %collective-permute-done.5.a_ref = bf16[4096,128]{1,0:T(8,128)(2,1)S(1)} collective-permute-done((bf16[4096,128]{1,0:T(8,128)(2,1)S(1)}, bf16[4096,128]{1,0:T(8,128)(2,1)S(1)}, u32[]{:S(2)}, u32[]{:S(2)}) %collective-permute-start.5) | collective-permute-done | bytes 1048608 | tf_op jit(solution)/shard_map/ppermute | solution.py:20
  107.2 3.4 %shard_map.45 = (f32[2,352,128]{2,1,0:T(8,128)S(1)}, f32[2,352,128]{2,1,0:T(8,128)S(1)}) custom-call(s32[2]{0:T(128)S(1)} %copy-done.2, f32[4,512]{1,0:T(4,128)S(1)} %collective-permute-done.3.sa_ref, f32[4,512]{1,0:T(4,128)S(1)} %collective-permute-done.4.sb_ref, bf16[4096,128]{1,0:T(8,128)(2,1)S(1)} %collective-permute-done.5.a_ref, ...), custom_call_target="tpu_custom_call" | custom-call | flops 1476395008 | bytes 13320200 | tf_op jit(solution)/shard_map/pallas_call | solution.py:166
  113.4 3.2 %collective-permute-done.19 = f32[224,128]{1,0:T(8,128)S(1)} collective-permute-done((f32[224,128]{1,0:T(8,128)S(1)}, f32[224,128]{1,0:T(8,128)S(1)}, u32[]{:S(2)}, u32[]{:S(2)}) %collective-permute-start.19) | collective-permute-done | bytes 114720 | tf_op jit(solution)/shard_map/ppermute | solution.py:201
  117.2 1.8 %collective-permute-start.13 = (f32[2,352,128]{2,1,0:T(8,128)S(1)}, f32[2,352,128]{2,1,0:T(8,128)S(1)}, u32[]{:S(2)}, u32[]{:S(2)}) collective-permute-start(f32[2,352,128]{2,1,0:T(8,128)S(1)} %get-tuple-element.58), channel_id=1, source_target_pairs={{0,1},{1,0},{2,3},{3,2},{4,5},{5,4},{6,7},{7,6},{8,9},{9,8},{10,11... | collective-permute-start | bytes 1081352 | tf_op jit(solution)/shard_map/ppermute | solution.py:271
  119.2 3.1 %collective-permute-done.22 = f32[288,128]{1,0:T(8,128)S(1)} collective-permute-done((f32[288,128]{1,0:T(8,128)S(1)}, f32[288,128]{1,0:T(8,128)S(1)}, u32[]{:S(2)}, u32[]{:S(2)}) %collective-permute-start.22) | collective-permute-done | bytes 147488 | tf_op jit(solution)/shard_map/ppermute | solution.py:201
  127.6 3.5 %collective-permute-done.1 = f32[128,512]{1,0:T(8,128)S(1)} collective-permute-done((f32[128,512]{1,0:T(8,128)S(1)}, f32[128,512]{1,0:T(8,128)S(1)}, u32[]{:S(2)}, u32[]{:S(2)}) %collective-permute-start.1) | collective-permute-done | bytes 262176 | tf_op jit(solution)/shard_map/ppermute | solution.py:201
  131.2 3.5 %collective-permute-done.2 = f32[128,512]{1,0:T(8,128)S(1)} collective-permute-done((f32[128,512]{1,0:T(8,128)S(1)}, f32[128,512]{1,0:T(8,128)S(1)}, u32[]{:S(2)}, u32[]{:S(2)}) %collective-permute-start.2) | collective-permute-done | bytes 262176 | tf_op jit(solution)/shard_map/ppermute | solution.py:201
  134.8 4.7 %collective-permute-done.14.other_ref = f32[128,128]{1,0:T(8,128)S(1)} collective-permute-done((f32[128,128]{1,0:T(8,128)S(1)}, f32[128,128]{1,0:T(8,128)S(1)}, u32[]{:S(2)}, u32[]{:S(2)}) %collective-permute-start.14) | collective-permute-done | bytes 65568 | tf_op jit(solution)/shard_map/ppermute | solution.py:278
  (71 shorter events, 21.9 us)
Async XLA Ops:
  6.8 54.0 %collective-permute-start.7 = (bf16[4096,128]{1,0:T(8,128)(2,1)}, bf16[4096,128]{1,0:T(8,128)(2,1)S(1)}, u32[]{:S(2)}, u32[]{:S(2)}) collective-permute-start(bf16[4096,128]{1,0:T(8,128)(2,1)} %get-tuple-element.45), channel_id=1, source_target_pairs={{0,4},{4,0},{8,12},{12,8},{1,5},{5,1},{9,13},{13,9},{2,6},{6,2},{1... | collective-permute-start | bytes 3145736 | tf_op jit(solution)/shard_map/ppermute | solution.py:20
  9.9 53.4 %collective-permute-start.8 = (bf16[4096,128]{1,0:T(8,128)(2,1)}, bf16[4096,128]{1,0:T(8,128)(2,1)S(1)}, u32[]{:S(2)}, u32[]{:S(2)}) collective-permute-start(bf16[4096,128]{1,0:T(8,128)(2,1)} %get-tuple-element.46), channel_id=1, source_target_pairs={{4,8},{8,4},{5,9},{9,5},{6,10},{10,6},{7,11},{11,7},{20,24},{24,20... | collective-permute-start | bytes 3145736 | tf_op jit(solution)/shard_map/ppermute | solution.py:20
  14.5 51.8 %collective-permute-start.10 = (bf16[4096,128]{1,0:T(8,128)(2,1)}, bf16[4096,128]{1,0:T(8,128)(2,1)S(1)}, u32[]{:S(2)}, u32[]{:S(2)}) collective-permute-start(bf16[4096,128]{1,0:T(8,128)(2,1)} %get-tuple-element.49), channel_id=1, source_target_pairs={{4,8},{8,4},{5,9},{9,5},{6,10},{10,6},{7,11},{11,7},{20,24},{24,20... | collective-permute-start | bytes 3145736 | tf_op jit(solution)/shard_map/ppermute | solution.py:20
  24.0 9.5 %collective-permute-start.3 = (f32[4,512]{1,0:T(4,128)S(1)}, f32[4,512]{1,0:T(4,128)S(1)}, u32[]{:S(2)}, u32[]{:S(2)}) collective-permute-start(f32[4,512]{1,0:T(4,128)S(1)} %pad_maximum_fusion.1), channel_id=1, source_target_pairs={{0,4},{4,0},{8,12},{12,8},{1,5},{5,1},{9,13},{13,9},{2,6},{6,2},{1... | collective-permute-start | bytes 24584 | tf_op jit(solution)/shard_map/ppermute | solution.py:20
  29.3 9.9 %collective-permute-start.4 = (f32[4,512]{1,0:T(4,128)S(1)}, f32[4,512]{1,0:T(4,128)S(1)}, u32[]{:S(2)}, u32[]{:S(2)}) collective-permute-start(f32[4,512]{1,0:T(4,128)S(1)} %pad_maximum_fusion.1), channel_id=1, source_target_pairs={{4,8},{8,4},{5,9},{9,5},{6,10},{10,6},{7,11},{11,7},{20,24},{24,20... | collective-permute-start | bytes 24584 | tf_op jit(solution)/shard_map/ppermute | solution.py:20
  33.4 39.0 %collective-permute-start.9 = (bf16[4096,128]{1,0:T(8,128)(2,1)}, bf16[4096,128]{1,0:T(8,128)(2,1)S(1)}, u32[]{:S(2)}, u32[]{:S(2)}) collective-permute-start(bf16[4096,128]{1,0:T(8,128)(2,1)} %copy-done.3), channel_id=1, source_target_pairs={{0,4},{4,0},{8,12},{12,8},{1,5},{5,1},{9,13},{13,9},{2,6},{6,2},{1... | collective-permute-start | bytes 3145736 | tf_op jit(solution)/shard_map/ppermute | solution.py:20
  39.2 45.6 %collective-permute-start.11 = (bf16[4096,128]{1,0:T(8,128)(2,1)S(1)}, bf16[4096,128]{1,0:T(8,128)(2,1)S(1)}, u32[]{:S(2)}, u32[]{:S(2)}) collective-permute-start(bf16[4096,128]{1,0:T(8,128)(2,1)S(1)} %get-tuple-element.52), channel_id=1, source_target_pairs={{0,4},{4,0},{8,12},{12,8},{1,5},{5,1},{9,13},{13,9},{2,6},{6,2},{1... | collective-permute-start | bytes 3145736 | tf_op jit(solution)/shard_map/ppermute | solution.py:20
  60.8 24.0 %collective-permute-start.12 = (bf16[4096,128]{1,0:T(8,128)(2,1)S(1)}, bf16[4096,128]{1,0:T(8,128)(2,1)S(1)}, u32[]{:S(2)}, u32[]{:S(2)}) collective-permute-start(bf16[4096,128]{1,0:T(8,128)(2,1)S(1)} %get-tuple-element.53), channel_id=1, source_target_pairs={{4,8},{8,4},{5,9},{9,5},{6,10},{10,6},{7,11},{11,7},{20,24},{24,20... | collective-permute-start | bytes 3145736 | tf_op jit(solution)/shard_map/ppermute | solution.py:20
  63.3 42.2 %collective-permute-start.5 = (bf16[4096,128]{1,0:T(8,128)(2,1)S(1)}, bf16[4096,128]{1,0:T(8,128)(2,1)S(1)}, u32[]{:S(2)}, u32[]{:S(2)}) collective-permute-start(bf16[4096,128]{1,0:T(8,128)(2,1)S(1)} %get-tuple-element.42), channel_id=1, source_target_pairs={{0,4},{4,0},{8,12},{12,8},{1,5},{5,1},{9,13},{13,9},{2,6},{6,2},{1... | collective-permute-start | bytes 3145736 | tf_op jit(solution)/shard_map/ppermute | solution.py:20
  66.3 39.3 %collective-permute-start.6 = (bf16[4096,128]{1,0:T(8,128)(2,1)S(1)}, bf16[4096,128]{1,0:T(8,128)(2,1)S(1)}, u32[]{:S(2)}, u32[]{:S(2)}) collective-permute-start(bf16[4096,128]{1,0:T(8,128)(2,1)S(1)} %get-tuple-element.43), channel_id=1, source_target_pairs={{4,8},{8,4},{5,9},{9,5},{6,10},{10,6},{7,11},{11,7},{20,24},{24,20... | collective-permute-start | bytes 3145736 | tf_op jit(solution)/shard_map/ppermute | solution.py:20
  72.5 53.8 %collective-permute-start = (f32[128,512]{1,0:T(8,128)S(1)}, f32[128,512]{1,0:T(8,128)S(1)}, u32[]{:S(2)}, u32[]{:S(2)}) collective-permute-start(f32[128,512]{1,0:T(8,128)S(1)} %get-tuple-element.39), channel_id=1, source_target_pairs={{0,1},{1,0},{2,3},{3,2},{4,5},{5,4},{6,7},{7,6},{8,9},{9,8},{10,11... | collective-permute-start | bytes 786440 | tf_op jit(solution)/shard_map/ppermute | solution.py:201
  84.8 25.7 %collective-permute-start.15 = (f32[160,128]{1,0:T(8,128)S(1)}, f32[160,128]{1,0:T(8,128)S(1)}, u32[]{:S(2)}, u32[]{:S(2)}) collective-permute-start(f32[160,128]{1,0:T(8,128)S(1)} %get-tuple-element.60), channel_id=1, source_target_pairs={{0,1},{1,0},{2,3},{3,2},{4,5},{5,4},{6,7},{7,6},{8,9},{9,8},{10,11... | collective-permute-start | bytes 245768 | tf_op jit(solution)/shard_map/ppermute | solution.py:201
  84.8 26.3 %collective-permute-start.16 = (f32[160,128]{1,0:T(8,128)S(1)}, f32[160,128]{1,0:T(8,128)S(1)}, u32[]{:S(2)}, u32[]{:S(2)}) collective-permute-start(f32[160,128]{1,0:T(8,128)S(1)} %get-tuple-element.61), channel_id=1, source_target_pairs={{0,2},{1,3},{2,0},{3,1},{4,6},{5,7},{6,4},{7,5},{8,10},{9,11},{10,... | collective-permute-start | bytes 245768 | tf_op jit(solution)/shard_map/ppermute | solution.py:201
  105.6 7.2 %collective-permute-start.18 = (f32[224,128]{1,0:T(8,128)S(1)}, f32[224,128]{1,0:T(8,128)S(1)}, u32[]{:S(2)}, u32[]{:S(2)}) collective-permute-start(f32[224,128]{1,0:T(8,128)S(1)} %get-tuple-element.64), channel_id=1, source_target_pairs={{0,1},{1,0},{2,3},{3,2},{4,5},{5,4},{6,7},{7,6},{8,9},{9,8},{10,11... | collective-permute-start | bytes 344072 | tf_op jit(solution)/shard_map/ppermute | solution.py:201
  112.0 7.0 %collective-permute-start.21 = (f32[288,128]{1,0:T(8,128)S(1)}, f32[288,128]{1,0:T(8,128)S(1)}, u32[]{:S(2)}, u32[]{:S(2)}) collective-permute-start(f32[288,128]{1,0:T(8,128)S(1)} %get-tuple-element.68), channel_id=1, source_target_pairs={{0,1},{1,0},{2,3},{3,2},{4,5},{5,4},{6,7},{7,6},{8,9},{9,8},{10,11... | collective-permute-start | bytes 442376 | tf_op jit(solution)/shard_map/ppermute | solution.py:201
  112.8 9.4 %collective-permute-start.22 = (f32[288,128]{1,0:T(8,128)S(1)}, f32[288,128]{1,0:T(8,128)S(1)}, u32[]{:S(2)}, u32[]{:S(2)}) collective-permute-start(f32[288,128]{1,0:T(8,128)S(1)} %get-tuple-element.69), channel_id=1, source_target_pairs={{0,2},{1,3},{2,0},{3,1},{4,6},{5,7},{6,4},{7,5},{8,10},{9,11},{10,... | collective-permute-start | bytes 442376 | tf_op jit(solution)/shard_map/ppermute | solution.py:201
  116.7 6.8 %collective-permute-start.23 = (f32[288,128]{1,0:T(8,128)S(1)}, f32[288,128]{1,0:T(8,128)S(1)}, u32[]{:S(2)}, u32[]{:S(2)}) collective-permute-start(f32[288,128]{1,0:T(8,128)S(1)} %get-tuple-element.70), channel_id=1, source_target_pairs={{0,3},{1,2},{2,1},{3,0},{4,7},{5,6},{6,5},{7,4},{8,11},{9,10},{10,... | collective-permute-start | bytes 442376 | tf_op jit(solution)/shard_map/ppermute | solution.py:201
  117.2 7.7 %collective-permute-start.13 = (f32[2,352,128]{2,1,0:T(8,128)S(1)}, f32[2,352,128]{2,1,0:T(8,128)S(1)}, u32[]{:S(2)}, u32[]{:S(2)}) collective-permute-start(f32[2,352,128]{2,1,0:T(8,128)S(1)} %get-tuple-element.58), channel_id=1, source_target_pairs={{0,1},{1,0},{2,3},{3,2},{4,5},{5,4},{6,7},{7,6},{8,9},{9,8},{10,11... | collective-permute-start | bytes 1081352 | tf_op jit(solution)/shard_map/ppermute | solution.py:271
  119.0 12.1 %collective-permute-start.1 = (f32[128,512]{1,0:T(8,128)S(1)}, f32[128,512]{1,0:T(8,128)S(1)}, u32[]{:S(2)}, u32[]{:S(2)}) collective-permute-start(f32[128,512]{1,0:T(8,128)S(1)} %get-tuple-element.40), channel_id=1, source_target_pairs={{0,2},{1,3},{2,0},{3,1},{4,6},{5,7},{6,4},{7,5},{8,10},{9,11},{10,... | collective-permute-start | bytes 786440 | tf_op jit(solution)/shard_map/ppermute | solution.py:201
  122.3 12.5 %collective-permute-start.2 = (f32[128,512]{1,0:T(8,128)S(1)}, f32[128,512]{1,0:T(8,128)S(1)}, u32[]{:S(2)}, u32[]{:S(2)}) collective-permute-start(f32[128,512]{1,0:T(8,128)S(1)} %get-tuple-element.41), channel_id=1, source_target_pairs={{0,3},{1,2},{2,1},{3,0},{4,7},{5,6},{6,5},{7,4},{8,11},{9,10},{10,... | collective-permute-start | bytes 786440 | tf_op jit(solution)/shard_map/ppermute | solution.py:201
  123.6 11.3 %collective-permute-start.24 = (f32[288,128]{1,0:T(8,128)S(1)}, f32[288,128]{1,0:T(8,128)S(1)}, u32[]{:S(2)}, u32[]{:S(2)}) collective-permute-start(f32[288,128]{1,0:T(8,128)S(1)} %pad_maximum_fusion), channel_id=1, source_target_pairs={{4,0},{8,4},{12,8},{5,1},{9,5},{13,9},{6,2},{10,6},{14,10},{7,3},{... | collective-permute-start | bytes 442376 | tf_op jit(solution)/shard_map/ppermute | solution.py:268
  125.0 14.6 %collective-permute-start.25 = (f32[224,128]{1,0:T(8,128)S(1)}, f32[224,128]{1,0:T(8,128)S(1)}, u32[]{:S(2)}, u32[]{:S(2)}) collective-permute-start(f32[224,128]{1,0:T(8,128)S(1)} %get-tuple-element.76), channel_id=1, source_target_pairs={{4,0},{5,1},{6,2},{7,3},{8,4},{9,5},{10,6},{11,7},{12,8},{13,9},{1... | collective-permute-start | bytes 344072 | tf_op jit(solution)/shard_map/ppermute | solution.py:276
  126.3 13.3 %collective-permute-start.26 = (f32[224,128]{1,0:T(8,128)S(1)}, f32[224,128]{1,0:T(8,128)S(1)}, u32[]{:S(2)}, u32[]{:S(2)}) collective-permute-start(f32[224,128]{1,0:T(8,128)S(1)} %get-tuple-element.75), channel_id=1, source_target_pairs={{4,2},{5,3},{6,0},{7,1},{8,6},{9,7},{10,4},{11,5},{12,10},{13,11},... | collective-permute-start | bytes 344072 | tf_op jit(solution)/shard_map/ppermute | solution.py:276
  131.0 8.5 %collective-permute-start.14 = (f32[128,128]{1,0:T(8,128)S(1)}, f32[128,128]{1,0:T(8,128)S(1)}, u32[]{:S(2)}, u32[]{:S(2)}) collective-permute-start(f32[128,128]{1,0:T(8,128)S(1)} %slice_bitcast_fusion.2), channel_id=1, source_target_pairs={{0,2},{1,3},{2,0},{3,1},{4,6},{5,7},{6,4},{7,5},{8,10},{9,11},{10,... | collective-permute-start | bytes 196616 | tf_op jit(solution)/shard_map/ppermute | solution.py:278
  (8 other events, 56.3 us)

commit v4 on v3

--- a/solution.py
+++ b/solution.py
@@ -10,7 +10,6 @@
 
 LANES = 128
 DEPTH = 1024
-BLOCKS = 8
 
 
 def exchange(array, devices, first):
@@ -48,34 +47,13 @@
     return jnp.concatenate([row == first, row == second], 1).astype(jnp.float32).astype(jnp.bfloat16)
 
 
-def front_kernel(samp, place_ref, values_hbm, a_hbm, b_hbm, values_ref, a_ref, b_ref, sems):
-    rows, width = values_ref.shape
-    blocks = sems.shape[1]
-    size = rows // blocks
-    spans = [pl.ds(k * size, size) for k in range(blocks)]
-    arrive = [pltpu.make_async_copy(values_hbm.at[s], values_ref.at[s], sems.at[0, k]) for k, s in enumerate(spans)]
-    leave = [pltpu.make_async_copy(a_ref.at[s], a_hbm.at[s], sems.at[1, k]) for k, s in enumerate(spans)]
-    leave += [pltpu.make_async_copy(b_ref.at[s], b_hbm.at[s], sems.at[2, k]) for k, s in enumerate(spans)]
-    for copy in arrive:
-        copy.start()
-    chosen = choose(width, samp, 0, place_ref[0] != 0)
-    for k, span in enumerate(spans):
-        arrive[k].wait()
-        both = matmul(values_ref[span, :], chosen).astype(jnp.bfloat16)
-        a_ref[span, :] = both[:, :LANES]
-        b_ref[span, :] = both[:, LANES:]
-        leave[k].start()
-        leave[blocks + k].start()
-    for copy in leave:
-        copy.wait()
-
-
 def pick_kernel(samp, j, place_ref, values_ref, a_ref, b_ref):
     rows, width = values_ref.shape
+    skip = rows - a_ref.shape[0]
     chosen = choose(width, samp, j, place_ref[0] != 0)
-    for k in range(0, rows, DEPTH):
+    for k in range(0, rows - skip, DEPTH):
         span = pl.ds(k, DEPTH)
-        both = matmul(values_ref[span, :], chosen).astype(jnp.bfloat16)
+        both = matmul(values_ref[pl.ds(skip + k, DEPTH), :], chosen).astype(jnp.bfloat16)
         a_ref[span, :] = both[:, :LANES]
         b_ref[span, :] = both[:, LANES:]
 
@@ -116,10 +94,31 @@
         out_ref[...] = value
 
 
-def step_kernel(samp, j, results, place_ref, sa_ref, sb_ref, a_ref, b_ref, own_ref, *rest):
+def base_kernel(place_ref, sa_ref, sb_ref, own_ref, *rest):
+    raw, (near_out, far_out) = rest[:-2], rest[-2:]
+    even = place_ref[0] != 0
+    after = jnp.where(even, sa_ref[...], sb_ref[...])
+    before = jnp.where(even, sb_ref[...], sa_ref[...])
+    total, at = None, 0
+    for a_ref, b_ref in zip(raw[::2], raw[1::2]):
+        rows = a_ref.shape[0]
+        for k in range(0, rows, min(rows, DEPTH // 2)):
+            size = min(rows, DEPTH // 2)
+            span = pl.ds(k, size)
+            a, b = a_ref[span, :].astype(jnp.float32), b_ref[span, :].astype(jnp.float32)
+            near = ((jnp.where(even, a, b) - after[0:1]) * after[1:2]).astype(jnp.bfloat16)
+            far = ((jnp.where(even, b, a) - before[0:1]) * before[1:2]).astype(jnp.bfloat16).T
+            total = accumulate(total, [matmul(own_ref[:, pl.ds(at, size)], near), matmul(far, near)])
+            at += size
+    near_out[...] = total[0]
+    far_out[...] = total[1]
+
+
+def step_kernel(samp, j, results, place_ref, sa_ref, sb_ref, a_ref, b_ref, own_ref, base_near, base_far, *rest):
     nears, fars = rest[:j], rest[j : 2 * j]
     saved, outs = rest[2 * j : len(rest) - results], rest[len(rest) - results :]
     rows, step = a_ref.shape
+    skip = own_ref.shape[1] - rows
     part, share = own_ref.shape[0] // samp, step // samp
     even, me = place_ref[0] != 0, place_ref[1]
     cols = pl.ds(j * step, step)
@@ -135,15 +134,19 @@
         if saved:
             saved[0][span, :] = near
             saved[1][:, span] = far
-        terms = [matmul(own_ref[:, span], near)]
+        terms = [matmul(own_ref[:, pl.ds(skip + k, DEPTH)], near)]
         terms += [matmul(fars[i][:, span], near) for i in range(j)]
         terms += [matmul(far, jnp.concatenate([near] + [nears[i][span, :] for i in range(j)], 1))]
         total = accumulate(total, terms)
     blocks = total[1:-1] + [total[-1][:, i * step : (i + 1) * step] for i in range(j + 1)]
-    parts = [
-        [total[0][t * part : (t + 1) * part]] + [block[t * share : (t + 1) * share] for block in blocks]
-        for t in range(samp)
-    ]
+    names = [(i, j) for i in range(j)] + [(j, j)] + [(j, i) for i in range(j)]
+    parts = []
+    for t in range(samp):
+        parts.append([total[0][t * part : (t + 1) * part] + base_near[t * part : (t + 1) * part, cols]])
+        for block, (row, column) in zip(blocks, names):
+            first = t * part + row * share
+            base = base_far[first : first + share, column * step : (column + 1) * step]
+            parts[t].append(block[t * share : (t + 1) * share] + base)
     parts = [by_distance([parts[t][n] for t in range(samp)], me) for n in range(len(blocks) + 1)]
     if len(outs) != samp:
         outs = [outs[d % 2].at[d // 2] for d in range(samp)]
@@ -155,27 +158,23 @@
             row += size
 
 
-def call(kernel, out_shapes, flops, *args, scalars=True, in_hbm=(), scratch=(), out_space=pltpu.VMEM, limit=None):
+def call(kernel, out_shapes, flops, *args, scalars=True):
     vmem = pl.BlockSpec(memory_space=pltpu.VMEM)
     specs = [vmem] * len(args)
     if scalars:
         specs[0] = pl.BlockSpec(memory_space=pltpu.SMEM)
-    for n in in_hbm:
-        specs[n] = pl.BlockSpec(memory_space=pltpu.HBM)
     moved = sum(x.size * x.dtype.itemsize for x in args) + sum(x.size * x.dtype.itemsize for x in out_shapes)
     return pl.pallas_call(
         kernel,
         out_shape=out_shapes,
         in_specs=specs,
-        out_specs=[pl.BlockSpec(memory_space=out_space)] * len(out_shapes),
-        scratch_shapes=scratch,
+        out_specs=[vmem] * len(out_shapes),
         cost_estimate=pl.CostEstimate(flops=flops, bytes_accessed=moved, transcendentals=0),
-        compiler_params=pltpu.CompilerParams(vmem_limit_bytes=limit or VMEM_LIMIT),
+        compiler_params=pltpu.CompilerParams(vmem_limit_bytes=VMEM_LIMIT),
     )(*args)
 
 
 VMEM_LIMIT = 20 * 2**20
-FRONT_LIMIT = 54 * 2**20
 
 
 def body(dosage, filter_mask, counts):
@@ -207,23 +206,18 @@
     def bf16(*shape):
         return jax.ShapeDtypeStruct(shape, jnp.bfloat16)
 
+    half = local_rows // 2
+    first = half // 4
+    heads = []
+    for low, high in [(0, first), (first, half)]:
+        piece = dosage[low:high]
+        piece, dosage = lax.optimization_barrier((piece, dosage))
+        heads.append(exchange(piece, chain, 0))
+        heads.append(exchange(piece, chain, 1))
     raw = []
-    chunk = bf16(local_rows, step)
-    flops = 4 * local_rows * width * step
+    chunk = bf16(half, step)
     for j in range(chunks):
-        if j == 0:
-            a, b = call(
-                functools.partial(front_kernel, samp), [chunk, chunk], flops, place, dosage, in_hbm=(1,),
-                out_space=pltpu.HBM, limit=FRONT_LIMIT,
-                scratch=[
-                    pltpu.VMEM(dosage.shape, dosage.dtype),
-                    pltpu.VMEM(chunk.shape, chunk.dtype),
-                    pltpu.VMEM(chunk.shape, chunk.dtype),
-                    pltpu.SemaphoreType.DMA((3, BLOCKS)),
-                ],
-            )
-        else:
-            a, b = call(functools.partial(pick_kernel, samp, j), [chunk, chunk], flops, place, dosage)
+        a, b = call(functools.partial(pick_kernel, samp, j), [chunk, chunk], 4 * half * width * step, place, dosage)
         a = exchange(a, chain, 0)
         b = exchange(b, chain, 1)
         raw.append((a, b))
@@ -248,17 +242,18 @@
     )
     tile = scatter_sum(parts)
 
+    base = call(base_kernel, [f32(width, width)] * 2, 4 * half * width * width, place, sa, sb, own, *heads)
     nears, fars, totals = [], [], []
     for j in range(chunks):
         size = part + (2 * j + 1) * share
         last = j == chunks - 1
         results = [f32(samp // 2, size, step)] * 2 if last else [f32(size, step)] * samp
-        saved = [] if last else [bf16(local_rows, step), bf16(step, local_rows)]
+        saved = [] if last else [bf16(half, step), bf16(step, half)]
         kept = call(
             functools.partial(step_kernel, samp, j, len(results)),
             saved + results,
-            2 * local_rows * step * (width + (2 * j + 1) * step),
-            place, sa, sb, *raw[j], own, *nears, *fars,
+            2 * half * step * (width + (2 * j + 1) * step),
+            place, sa, sb, *raw[j], own, *base, *nears, *fars,
         )
         parts = kept[len(saved) :]
         if not last:

time: 141 us -> 144 us (1.021)
  waiting for transfers between devices: 49.3 us -> 62.9 us
  Pallas kernels: 27.6 us -> 20 us
  starting transfers between devices: 50.6 us -> 44.5 us
  local copies, waits for them, and re-layouts: 3.47 us -> 7.21 us
    ppermute x10 -> x14, waiting for transfers between devices: 29.5 us -> 45.5 us  [exchange(): lax.ppermute(array, 'chain', pairs)]
    ppermute x10 -> x14, starting transfers between devices: 38.6 us -> 30.4 us  [exchange(): lax.ppermute(array, 'chain', pairs)]
    pallas_call x10 -> x11, Pallas kernels: 27.6 us -> 20 us  [call(): pl.pallas_call(kernel, out_shape=out_shapes, in_specs=specs, out_specs=[v...]
    slice x0 -> x2, local copies, waits for them, and re-layouts: none -> 4.72 us  [body(): piece = dosage[low:high]]
    ppermute x12, starting transfers between devices: 6.19 us -> 7.91 us  [scatter_sum(): lax.ppermute(parts[d], 'samp', [(i, i ^ d) for i in range(samp)])]
    ppermute x1, waiting for transfers between devices: 4.73 us -> 3.01 us  [body(): lax.ppermute(kept[n, :part], 'samp', [(i, moved[i]) for i in range(samp)])]
    ppermute x12, waiting for transfers between devices: 15.1 us -> 13.4 us  [scatter_sum(): lax.ppermute(parts[d], 'samp', [(i, i ^ d) for i in range(samp)])]
    unnamed x10 -> x6, local copies, waits for them, and re-layouts: 3.17 us -> 2.19 us
  transfers between devices with their start and end apart: 27 -> 31, of which waited for: 10 -> 11; matrix products, arithmetic and copies ran while one was open for 1% -> 1% of each run, Pallas kernels for 15% -> 13%
where the time goes in v4:
time: 144 us; the launch traced here: 143 us
  waiting for transfers between devices  62.9 us (44%)
  starting transfers between devices  44.5 us (31%)
  Pallas kernels  20 us (14%)
  local copies, waits for them, and re-layouts  7.21 us (5%)
  blocking collectives  6.31 us (4%)
  other arithmetic  1.51 us (1%)
    ppermute x14, waiting for transfers between devices, exchange(): lax.ppermute(array, 'chain', pairs)  45.5 us
    ppermute x14, starting transfers between devices, exchange(): lax.ppermute(array, 'chain', pairs)  30.4 us
    pallas_call x11, Pallas kernels, call(): pl.pallas_call(kernel, out_shape=out_shapes, in_specs=specs, out_specs=[v...  20 us
    ppermute x12, waiting for transfers between devices, scatter_sum(): lax.ppermute(parts[d], 'samp', [(i, i ^ d) for i in range(samp)])  13.4 us
    ppermute x12, starting transfers between devices, scatter_sum(): lax.ppermute(parts[d], 'samp', [(i, i ^ d) for i in range(samp)])  7.91 us
    psum x1, blocking collectives, body(): lax.psum((jnp.sum(values, 0), jnp.sum(values * values, 0)), 'samp')  6.31 us
    slice x2, local copies, waits for them, and re-layouts, body(): piece = dosage[low:high]  4.72 us
    ppermute x1, waiting for transfers between devices, body(): lax.ppermute(kept[n, :part], 'samp', [(i, moved[i]) for i in range(samp)])  3.01 us
  transfers between devices with their start and end apart: 31, of which 11 were waited for; matrix products, arithmetic and copies ran while one was open for 1% of the time, Pallas kernels for 13%

profile of v4, /device:TPU:0, one launch (start us, length us, event | category | flops | bytes accessed | tf_op | source)
XLA Modules:
  0.0 143.4 jit_solution(10288421660620877074)
XLA Ops:
  0.0 2.0 %slice.24 = bf16[512,512]{1,0:T(8,128)(2,1)} slice(bf16[4096,512]{1,0:T(8,128)(2,1)} %values_ref.4), slice={[0:512], [0:512]} | slice | bytes 1048576 | tf_op jit(solution)/shard_map/slice | solution.py:213
  2.0 2.7 %slice.25 = bf16[1536,512]{1,0:T(8,128)(2,1)} slice(bf16[4096,512]{1,0:T(8,128)(2,1)} %values_ref.4), slice={[512:2048], [0:512]} | slice | bytes 3145728 | tf_op jit(solution)/shard_map/slice | solution.py:213
  5.5 5.8 %collective-permute-start.9 = (bf16[1536,512]{1,0:T(8,128)(2,1)}, bf16[1536,512]{1,0:T(8,128)(2,1)S(1)}, u32[]{:S(2)}, u32[]{:S(2)}) collective-permute-start(bf16[1536,512]{1,0:T(8,128)(2,1)} %slice.25), channel_id=1, source_target_pairs={{0,4},{4,0},{8,12},{12,8},{1,5},{5,1},{9,13},{13,9},{2,6},{6,2},{1... | collective-permute-start | bytes 4718600 | tf_op jit(solution)/shard_map/ppermute | solution.py:19
  14.7 6.3 %all-reduce = (f32[512]{0:T(512)S(1)}, f32[512]{0:T(512)S(1)}) all-reduce(f32[512]{0:T(512)S(1)} %get-tuple-element.84, f32[512]{0:T(512)S(1)} %get-tuple-element.83), channel_id=1, replica_groups=mesh['groups'=2,'chain'=4,'samp'=4] {'samp'}, use_global_device_ids=true, to_apply=%region_1.2 | all-reduce | flops 1024 | bytes 8192 | tf_op jit(solution)/shard_map/psum | solution.py:226
  21.3 2.5 %collective-permute-start.3 = (f32[4,512]{1,0:T(4,128)S(1)}, f32[4,512]{1,0:T(4,128)S(1)}, u32[]{:S(2)}, u32[]{:S(2)}) collective-permute-start(f32[4,512]{1,0:T(4,128)S(1)} %pad_maximum_fusion.1), channel_id=1, source_target_pairs={{0,4},{4,0},{8,12},{12,8},{1,5},{5,1},{9,13},{13,9},{2,6},{6,2},{1... | collective-permute-start | bytes 24584 | tf_op jit(solution)/shard_map/ppermute | solution.py:19
  23.9 33.2 %collective-permute-done.3.sa_ref = f32[4,512]{1,0:T(4,128)S(1)} collective-permute-done((f32[4,512]{1,0:T(4,128)S(1)}, f32[4,512]{1,0:T(4,128)S(1)}, u32[]{:S(2)}, u32[]{:S(2)}) %collective-permute-start.3) | collective-permute-done | bytes 8224 | tf_op jit(solution)/shard_map/ppermute | solution.py:19
  57.7 2.2 %copy-done.1 = bf16[4096,512]{1,0:T(8,128)(2,1)S(1)} copy-done((bf16[4096,512]{1,0:T(8,128)(2,1)S(1)}, bf16[4096,512]{1,0:T(8,128)(2,1)}, u32[]{:S(2)}) %copy-start.1) | copy-done | bytes 4194328
  61.2 3.5 %collective-permute-start.11 = (bf16[2048,128]{1,0:T(8,128)(2,1)S(1)}, bf16[2048,128]{1,0:T(8,128)(2,1)S(1)}, u32[]{:S(2)}, u32[]{:S(2)}) collective-permute-start(bf16[2048,128]{1,0:T(8,128)(2,1)S(1)} %get-tuple-element.57), channel_id=1, source_target_pairs={{0,4},{4,0},{8,12},{12,8},{1,5},{5,1},{9,13},{13,9},{2,6},{6,2},{1... | collective-permute-start | bytes 1572872 | tf_op jit(solution)/shard_map/ppermute | solution.py:19
  66.7 2.9 %collective-permute-start.13 = (bf16[2048,128]{1,0:T(8,128)(2,1)S(1)}, bf16[2048,128]{1,0:T(8,128)(2,1)S(1)}, u32[]{:S(2)}, u32[]{:S(2)}) collective-permute-start(bf16[2048,128]{1,0:T(8,128)(2,1)S(1)} %get-tuple-element.60), channel_id=1, source_target_pairs={{0,4},{4,0},{8,12},{12,8},{1,5},{5,1},{9,13},{13,9},{2,6},{6,2},{1... | collective-permute-start | bytes 1572872 | tf_op jit(solution)/shard_map/ppermute | solution.py:19
  69.6 7.9 %collective-permute-done.11.a_ref = bf16[2048,128]{1,0:T(8,128)(2,1)S(1)} collective-permute-done((bf16[2048,128]{1,0:T(8,128)(2,1)S(1)}, bf16[2048,128]{1,0:T(8,128)(2,1)S(1)}, u32[]{:S(2)}, u32[]{:S(2)}) %collective-permute-start.11) | collective-permute-done | bytes 524320 | tf_op jit(solution)/shard_map/ppermute | solution.py:19
  79.4 4.9 %collective-permute-start.15 = (bf16[2048,128]{1,0:T(8,128)(2,1)S(1)}, bf16[2048,128]{1,0:T(8,128)(2,1)S(1)}, u32[]{:S(2)}, u32[]{:S(2)}) collective-permute-start(bf16[2048,128]{1,0:T(8,128)(2,1)S(1)} %get-tuple-element.64), channel_id=1, source_target_pairs={{0,4},{4,0},{8,12},{12,8},{1,5},{5,1},{9,13},{13,9},{2,6},{6,2},{1... | collective-permute-start | bytes 1572872 | tf_op jit(solution)/shard_map/ppermute | solution.py:19
  84.3 4.4 %collective-permute-done.13.a_ref = bf16[2048,128]{1,0:T(8,128)(2,1)S(1)} collective-permute-done((bf16[2048,128]{1,0:T(8,128)(2,1)S(1)}, bf16[2048,128]{1,0:T(8,128)(2,1)S(1)}, u32[]{:S(2)}, u32[]{:S(2)}) %collective-permute-start.13) | collective-permute-done | bytes 524320 | tf_op jit(solution)/shard_map/ppermute | solution.py:19
  90.7 4.9 %collective-permute-start.5 = (bf16[2048,128]{1,0:T(8,128)(2,1)S(1)}, bf16[2048,128]{1,0:T(8,128)(2,1)S(1)}, u32[]{:S(2)}, u32[]{:S(2)}) collective-permute-start(bf16[2048,128]{1,0:T(8,128)(2,1)S(1)} %get-tuple-element.50), channel_id=1, source_target_pairs={{0,4},{4,0},{8,12},{12,8},{1,5},{5,1},{9,13},{13,9},{2,6},{6,2},{1... | collective-permute-start | bytes 1572872 | tf_op jit(solution)/shard_map/ppermute | solution.py:19
  96.4 3.0 %shard_map.37 = (bf16[512,4096]{1,0:T(8,128)(2,1)S(1)}, f32[128,512]{1,0:T(8,128)S(1)}, f32[128,512]{1,0:T(8,128)S(1)}, f32[128,512]{1,0:T(8,128)S(1)}, f32[128,512]{1,0:T(8,128)S(1)}) custom-call(s32[2]{0:T(128)S(1)} %pad_add_fusion.place_ref, bf16[4096,512]{1,0:T(8,128)(2,1)S(1)} %copy-done.1, f32[1,512]{1,0:T(1,128)S(1)} %bitcast.20, f32[1,512]{1,0:T(1,128)S(1)} %bitcast.18), custom_call_target="tpu_custom_call" | custom-call | flops 2147483648 | bytes 9441288 | tf_op jit(solution)/shard_map/pallas_call | solution.py:167
  99.4 3.8 %shard_map.39 = (f32[512,512]{1,0:T(8,128)S(1)}, f32[512,512]{1,0:T(8,128)S(1)}) custom-call(s32[2]{0:T(128)S(1)} %pad_add_fusion.place_ref, f32[4,512]{1,0:T(4,128)S(1)} %collective-permute-done.3.sa_ref, f32[4,512]{1,0:T(4,128)S(1)} %collective-permute-done.4.sb_ref, bf16[512,4096]{1,0:T(8,128)(2,1)S(1)} %get-tuple-element.52.own_ref, ...), custom_call_target="tpu_custom_call" | custom-call | flops 2147483648 | bytes 10502152 | tf_op jit(solution)/shard_map/pallas_call | solution.py:167
  104.8 1.7 %shard_map.43 = (bf16[2048,128]{1,0:T(8,128)(2,1)S(1)}, bf16[128,2048]{1,0:T(8,128)(2,1)S(1)}, f32[224,128]{1,0:T(8,128)S(1)}, f32[224,128]{1,0:T(8,128)S(1)}, f...) custom-call(s32[2]{0:T(128)S(1)} %pad_add_fusion.place_ref, f32[4,512]{1,0:T(4,128)S(1)} %collective-permute-done.3.sa_ref, ...), custom_call_target="tpu_custom_call" | custom-call | flops 469762048 | bytes 9912328 | tf_op jit(solution)/shard_map/pallas_call | solution.py:167
  108.4 2.0 %shard_map.45 = (bf16[2048,128]{1,0:T(8,128)(2,1)S(1)}, bf16[128,2048]{1,0:T(8,128)(2,1)S(1)}, f32[288,128]{1,0:T(8,128)S(1)}, f32[288,128]{1,0:T(8,128)S(1)}, f...) custom-call(s32[2]{0:T(128)S(1)} %pad_add_fusion.place_ref, f32[4,512]{1,0:T(4,128)S(1)} %collective-permute-done.3.sa_ref, ...), custom_call_target="tpu_custom_call" | custom-call | flops 603979776 | bytes 11091976 | tf_op jit(solution)/shard_map/pallas_call | solution.py:167
  111.0 2.1 %shard_map.46 = (f32[2,352,128]{2,1,0:T(8,128)S(1)}, f32[2,352,128]{2,1,0:T(8,128)S(1)}) custom-call(s32[2]{0:T(128)S(1)} %pad_add_fusion.place_ref, f32[4,512]{1,0:T(4,128)S(1)} %collective-permute-done.3.sa_ref, f32[4,512]{1,0:T(4,128)S(1)} %collective-permute-done.4.sb_ref, bf16[2048,128]{1,0:T(8,128)(2,1)S(1)} %collective-permute-done.5.a_ref, ...), custom_call_target="tpu_custom_call" | custom-call | flops 738197504 | bytes 11223048 | tf_op jit(solution)/shard_map/pallas_call | solution.py:167
  116.9 2.3 %collective-permute-done.23 = f32[224,128]{1,0:T(8,128)S(1)} collective-permute-done((f32[224,128]{1,0:T(8,128)S(1)}, f32[224,128]{1,0:T(8,128)S(1)}, u32[]{:S(2)}, u32[]{:S(2)}) %collective-permute-start.23) | collective-permute-done | bytes 114720 | tf_op jit(solution)/shard_map/ppermute | solution.py:200
  123.1 1.7 %collective-permute-done.26 = f32[288,128]{1,0:T(8,128)S(1)} collective-permute-done((f32[288,128]{1,0:T(8,128)S(1)}, f32[288,128]{1,0:T(8,128)S(1)}, u32[]{:S(2)}, u32[]{:S(2)}) %collective-permute-start.26) | collective-permute-done | bytes 147488 | tf_op jit(solution)/shard_map/ppermute | solution.py:200
  124.8 2.2 %collective-permute-done.27 = f32[288,128]{1,0:T(8,128)S(1)} collective-permute-done((f32[288,128]{1,0:T(8,128)S(1)}, f32[288,128]{1,0:T(8,128)S(1)}, u32[]{:S(2)}, u32[]{:S(2)}) %collective-permute-start.27) | collective-permute-done | bytes 147488 | tf_op jit(solution)/shard_map/ppermute | solution.py:200
  131.1 2.5 %collective-permute-done.1 = f32[128,512]{1,0:T(8,128)S(1)} collective-permute-done((f32[128,512]{1,0:T(8,128)S(1)}, f32[128,512]{1,0:T(8,128)S(1)}, u32[]{:S(2)}, u32[]{:S(2)}) %collective-permute-start.1) | collective-permute-done | bytes 262176 | tf_op jit(solution)/shard_map/ppermute | solution.py:200
  135.1 3.2 %collective-permute-done.2 = f32[128,512]{1,0:T(8,128)S(1)} collective-permute-done((f32[128,512]{1,0:T(8,128)S(1)}, f32[128,512]{1,0:T(8,128)S(1)}, u32[]{:S(2)}, u32[]{:S(2)}) %collective-permute-start.2) | collective-permute-done | bytes 262176 | tf_op jit(solution)/shard_map/ppermute | solution.py:200
  138.4 3.0 %collective-permute-done.18.other_ref = f32[128,128]{1,0:T(8,128)S(1)} collective-permute-done((f32[128,128]{1,0:T(8,128)S(1)}, f32[128,128]{1,0:T(8,128)S(1)}, u32[]{:S(2)}, u32[]{:S(2)}) %collective-permute-start.18) | collective-permute-done | bytes 65568 | tf_op jit(solution)/shard_map/ppermute | solution.py:273
  (78 shorter events, 31.9 us)
Async XLA Ops:
  4.7 85.9 %collective-permute-start.10 = (bf16[1536,512]{1,0:T(8,128)(2,1)}, bf16[1536,512]{1,0:T(8,128)(2,1)S(1)}, u32[]{:S(2)}, u32[]{:S(2)}) collective-permute-start(bf16[1536,512]{1,0:T(8,128)(2,1)} %slice.25), channel_id=1, source_target_pairs={{4,8},{8,4},{5,9},{9,5},{6,10},{10,6},{7,11},{11,7},{20,24},{24,20... | collective-permute-start | bytes 4718600 | tf_op jit(solution)/shard_map/ppermute | solution.py:19
  5.5 90.1 %collective-permute-start.9 = (bf16[1536,512]{1,0:T(8,128)(2,1)}, bf16[1536,512]{1,0:T(8,128)(2,1)S(1)}, u32[]{:S(2)}, u32[]{:S(2)}) collective-permute-start(bf16[1536,512]{1,0:T(8,128)(2,1)} %slice.25), channel_id=1, source_target_pairs={{0,4},{4,0},{8,12},{12,8},{1,5},{5,1},{9,13},{13,9},{2,6},{6,2},{1... | collective-permute-start | bytes 4718600 | tf_op jit(solution)/shard_map/ppermute | solution.py:19
  11.3 54.6 %collective-permute-start.7 = (bf16[512,512]{1,0:T(8,128)(2,1)}, bf16[512,512]{1,0:T(8,128)(2,1)}, u32[]{:S(2)}, u32[]{:S(2)}) collective-permute-start(bf16[512,512]{1,0:T(8,128)(2,1)} %slice.24), channel_id=1, source_target_pairs={{0,4},{4,0},{8,12},{12,8},{1,5},{5,1},{9,13},{13,9},{2,6},{6,2},{1... | collective-permute-start | bytes 1572872 | tf_op jit(solution)/shard_map/ppermute | solution.py:19
  11.4 55.3 %collective-permute-start.8 = (bf16[512,512]{1,0:T(8,128)(2,1)}, bf16[512,512]{1,0:T(8,128)(2,1)}, u32[]{:S(2)}, u32[]{:S(2)}) collective-permute-start(bf16[512,512]{1,0:T(8,128)(2,1)} %slice.24), channel_id=1, source_target_pairs={{4,8},{8,4},{5,9},{9,5},{6,10},{10,6},{7,11},{11,7},{20,24},{24,20... | collective-permute-start | bytes 1572872 | tf_op jit(solution)/shard_map/ppermute | solution.py:19
  21.3 35.8 %collective-permute-start.3 = (f32[4,512]{1,0:T(4,128)S(1)}, f32[4,512]{1,0:T(4,128)S(1)}, u32[]{:S(2)}, u32[]{:S(2)}) collective-permute-start(f32[4,512]{1,0:T(4,128)S(1)} %pad_maximum_fusion.1), channel_id=1, source_target_pairs={{0,4},{4,0},{8,12},{12,8},{1,5},{5,1},{9,13},{13,9},{2,6},{6,2},{1... | collective-permute-start | bytes 24584 | tf_op jit(solution)/shard_map/ppermute | solution.py:19
  61.2 16.3 %collective-permute-start.11 = (bf16[2048,128]{1,0:T(8,128)(2,1)S(1)}, bf16[2048,128]{1,0:T(8,128)(2,1)S(1)}, u32[]{:S(2)}, u32[]{:S(2)}) collective-permute-start(bf16[2048,128]{1,0:T(8,128)(2,1)S(1)} %get-tuple-element.57), channel_id=1, source_target_pairs={{0,4},{4,0},{8,12},{12,8},{1,5},{5,1},{9,13},{13,9},{2,6},{6,2},{1... | collective-permute-start | bytes 1572872 | tf_op jit(solution)/shard_map/ppermute | solution.py:19
  66.0 13.5 %collective-permute-start.12 = (bf16[2048,128]{1,0:T(8,128)(2,1)S(1)}, bf16[2048,128]{1,0:T(8,128)(2,1)S(1)}, u32[]{:S(2)}, u32[]{:S(2)}) collective-permute-start(bf16[2048,128]{1,0:T(8,128)(2,1)S(1)} %get-tuple-element.58), channel_id=1, source_target_pairs={{4,8},{8,4},{5,9},{9,5},{6,10},{10,6},{7,11},{11,7},{20,24},{24,20... | collective-permute-start | bytes 1572872 | tf_op jit(solution)/shard_map/ppermute | solution.py:19
  66.7 22.0 %collective-permute-start.13 = (bf16[2048,128]{1,0:T(8,128)(2,1)S(1)}, bf16[2048,128]{1,0:T(8,128)(2,1)S(1)}, u32[]{:S(2)}, u32[]{:S(2)}) collective-permute-start(bf16[2048,128]{1,0:T(8,128)(2,1)S(1)} %get-tuple-element.60), channel_id=1, source_target_pairs={{0,4},{4,0},{8,12},{12,8},{1,5},{5,1},{9,13},{13,9},{2,6},{6,2},{1... | collective-permute-start | bytes 1572872 | tf_op jit(solution)/shard_map/ppermute | solution.py:19
  77.5 27.2 %collective-permute-start.14 = (bf16[2048,128]{1,0:T(8,128)(2,1)S(1)}, bf16[2048,128]{1,0:T(8,128)(2,1)S(1)}, u32[]{:S(2)}, u32[]{:S(2)}) collective-permute-start(bf16[2048,128]{1,0:T(8,128)(2,1)S(1)} %get-tuple-element.61), channel_id=1, source_target_pairs={{4,8},{8,4},{5,9},{9,5},{6,10},{10,6},{7,11},{11,7},{20,24},{24,20... | collective-permute-start | bytes 1572872 | tf_op jit(solution)/shard_map/ppermute | solution.py:19
  79.4 27.0 %collective-permute-start.15 = (bf16[2048,128]{1,0:T(8,128)(2,1)S(1)}, bf16[2048,128]{1,0:T(8,128)(2,1)S(1)}, u32[]{:S(2)}, u32[]{:S(2)}) collective-permute-start(bf16[2048,128]{1,0:T(8,128)(2,1)S(1)} %get-tuple-element.64), channel_id=1, source_target_pairs={{0,4},{4,0},{8,12},{12,8},{1,5},{5,1},{9,13},{13,9},{2,6},{6,2},{1... | collective-permute-start | bytes 1572872 | tf_op jit(solution)/shard_map/ppermute | solution.py:19
  88.7 19.4 %collective-permute-start.16 = (bf16[2048,128]{1,0:T(8,128)(2,1)S(1)}, bf16[2048,128]{1,0:T(8,128)(2,1)S(1)}, u32[]{:S(2)}, u32[]{:S(2)}) collective-permute-start(bf16[2048,128]{1,0:T(8,128)(2,1)S(1)} %get-tuple-element.65), channel_id=1, source_target_pairs={{4,8},{8,4},{5,9},{9,5},{6,10},{10,6},{7,11},{11,7},{20,24},{24,20... | collective-permute-start | bytes 1572872 | tf_op jit(solution)/shard_map/ppermute | solution.py:19
  90.7 19.7 %collective-permute-start.5 = (bf16[2048,128]{1,0:T(8,128)(2,1)S(1)}, bf16[2048,128]{1,0:T(8,128)(2,1)S(1)}, u32[]{:S(2)}, u32[]{:S(2)}) collective-permute-start(bf16[2048,128]{1,0:T(8,128)(2,1)S(1)} %get-tuple-element.50), channel_id=1, source_target_pairs={{0,4},{4,0},{8,12},{12,8},{1,5},{5,1},{9,13},{13,9},{2,6},{6,2},{1... | collective-permute-start | bytes 1572872 | tf_op jit(solution)/shard_map/ppermute | solution.py:19
  95.6 15.2 %collective-permute-start.6 = (bf16[2048,128]{1,0:T(8,128)(2,1)S(1)}, bf16[2048,128]{1,0:T(8,128)(2,1)S(1)}, u32[]{:S(2)}, u32[]{:S(2)}) collective-permute-start(bf16[2048,128]{1,0:T(8,128)(2,1)S(1)} %get-tuple-element.51), channel_id=1, source_target_pairs={{4,8},{8,4},{5,9},{9,5},{6,10},{10,6},{7,11},{11,7},{20,24},{24,20... | collective-permute-start | bytes 1572872 | tf_op jit(solution)/shard_map/ppermute | solution.py:19
  104.7 8.4 %collective-permute-start.19 = (f32[160,128]{1,0:T(8,128)S(1)}, f32[160,128]{1,0:T(8,128)S(1)}, u32[]{:S(2)}, u32[]{:S(2)}) collective-permute-start(f32[160,128]{1,0:T(8,128)S(1)} %get-tuple-element.72), channel_id=1, source_target_pairs={{0,1},{1,0},{2,3},{3,2},{4,5},{5,4},{6,7},{7,6},{8,9},{9,8},{10,11... | collective-permute-start | bytes 245768 | tf_op jit(solution)/shard_map/ppermute | solution.py:200
  106.5 8.2 %collective-permute-start.20 = (f32[160,128]{1,0:T(8,128)S(1)}, f32[160,128]{1,0:T(8,128)S(1)}, u32[]{:S(2)}, u32[]{:S(2)}) collective-permute-start(f32[160,128]{1,0:T(8,128)S(1)} %get-tuple-element.73), channel_id=1, source_target_pairs={{0,2},{1,3},{2,0},{3,1},{4,6},{5,7},{6,4},{7,5},{8,10},{9,11},{10,... | collective-permute-start | bytes 245768 | tf_op jit(solution)/shard_map/ppermute | solution.py:200
  110.4 19.4 %collective-permute-start = (f32[128,512]{1,0:T(8,128)S(1)}, f32[128,512]{1,0:T(8,128)S(1)}, u32[]{:S(2)}, u32[]{:S(2)}) collective-permute-start(f32[128,512]{1,0:T(8,128)S(1)} %get-tuple-element.47), channel_id=1, source_target_pairs={{0,1},{1,0},{2,3},{3,2},{4,5},{5,4},{6,7},{7,6},{8,9},{9,8},{10,11... | collective-permute-start | bytes 786440 | tf_op jit(solution)/shard_map/ppermute | solution.py:200
  115.4 9.4 %collective-permute-start.26 = (f32[288,128]{1,0:T(8,128)S(1)}, f32[288,128]{1,0:T(8,128)S(1)}, u32[]{:S(2)}, u32[]{:S(2)}) collective-permute-start(f32[288,128]{1,0:T(8,128)S(1)} %get-tuple-element.81), channel_id=1, source_target_pairs={{0,2},{1,3},{2,0},{3,1},{4,6},{5,7},{6,4},{7,5},{8,10},{9,11},{10,... | collective-permute-start | bytes 442376 | tf_op jit(solution)/shard_map/ppermute | solution.py:200
  119.2 7.8 %collective-permute-start.27 = (f32[288,128]{1,0:T(8,128)S(1)}, f32[288,128]{1,0:T(8,128)S(1)}, u32[]{:S(2)}, u32[]{:S(2)}) collective-permute-start(f32[288,128]{1,0:T(8,128)S(1)} %get-tuple-element.82), channel_id=1, source_target_pairs={{0,3},{1,2},{2,1},{3,0},{4,7},{5,6},{6,5},{7,4},{8,11},{9,10},{10,... | collective-permute-start | bytes 442376 | tf_op jit(solution)/shard_map/ppermute | solution.py:200
  121.5 12.1 %collective-permute-start.1 = (f32[128,512]{1,0:T(8,128)S(1)}, f32[128,512]{1,0:T(8,128)S(1)}, u32[]{:S(2)}, u32[]{:S(2)}) collective-permute-start(f32[128,512]{1,0:T(8,128)S(1)} %get-tuple-element.48), channel_id=1, source_target_pairs={{0,2},{1,3},{2,0},{3,1},{4,6},{5,7},{6,4},{7,5},{8,10},{9,11},{10,... | collective-permute-start | bytes 786440 | tf_op jit(solution)/shard_map/ppermute | solution.py:200
  124.8 13.5 %collective-permute-start.2 = (f32[128,512]{1,0:T(8,128)S(1)}, f32[128,512]{1,0:T(8,128)S(1)}, u32[]{:S(2)}, u32[]{:S(2)}) collective-permute-start(f32[128,512]{1,0:T(8,128)S(1)} %get-tuple-element.49), channel_id=1, source_target_pairs={{0,3},{1,2},{2,1},{3,0},{4,7},{5,6},{6,5},{7,4},{8,11},{9,10},{10,... | collective-permute-start | bytes 786440 | tf_op jit(solution)/shard_map/ppermute | solution.py:200
  127.1 11.3 %collective-permute-start.28 = (f32[288,128]{1,0:T(8,128)S(1)}, f32[288,128]{1,0:T(8,128)S(1)}, u32[]{:S(2)}, u32[]{:S(2)}) collective-permute-start(f32[288,128]{1,0:T(8,128)S(1)} %pad_maximum_fusion), channel_id=1, source_target_pairs={{4,0},{8,4},{12,8},{5,1},{9,5},{13,9},{6,2},{10,6},{14,10},{7,3},{... | collective-permute-start | bytes 442376 | tf_op jit(solution)/shard_map/ppermute | solution.py:263
  128.5 13.0 %collective-permute-start.29 = (f32[224,128]{1,0:T(8,128)S(1)}, f32[224,128]{1,0:T(8,128)S(1)}, u32[]{:S(2)}, u32[]{:S(2)}) collective-permute-start(f32[224,128]{1,0:T(8,128)S(1)} %get-tuple-element.88), channel_id=1, source_target_pairs={{4,0},{5,1},{6,2},{7,3},{8,4},{9,5},{10,6},{11,7},{12,8},{13,9},{1... | collective-permute-start | bytes 344072 | tf_op jit(solution)/shard_map/ppermute | solution.py:271
  129.8 12.7 %collective-permute-start.30 = (f32[224,128]{1,0:T(8,128)S(1)}, f32[224,128]{1,0:T(8,128)S(1)}, u32[]{:S(2)}, u32[]{:S(2)}) collective-permute-start(f32[224,128]{1,0:T(8,128)S(1)} %get-tuple-element.87), channel_id=1, source_target_pairs={{4,2},{5,3},{6,0},{7,1},{8,6},{9,7},{10,4},{11,5},{12,10},{13,11},... | collective-permute-start | bytes 344072 | tf_op jit(solution)/shard_map/ppermute | solution.py:271
  133.6 7.8 %collective-permute-start.18 = (f32[128,128]{1,0:T(8,128)S(1)}, f32[128,128]{1,0:T(8,128)S(1)}, u32[]{:S(2)}, u32[]{:S(2)}) collective-permute-start(f32[128,128]{1,0:T(8,128)S(1)} %slice_bitcast_fusion.2), channel_id=1, source_target_pairs={{0,2},{1,3},{2,0},{3,1},{4,6},{5,7},{6,4},{7,5},{8,10},{9,11},{10,... | collective-permute-start | bytes 196616 | tf_op jit(solution)/shard_map/ppermute | solution.py:273
  (10 other events, 78.7 us)

commit v5 on v4

--- a/solution.py
+++ b/solution.py
@@ -15,7 +15,7 @@
 def exchange(array, devices, first):
     pairs = []
     for low in range(first, devices - 1, 2):
-        pairs += [(low, low + 1), (low + 1, low)]
+        pairs += [(low + 1, low)] if low + 2 == devices else [(low, low + 1), (low + 1, low)]
     return lax.ppermute(array, "chain", pairs) if pairs else jnp.zeros_like(array)
 
 
@@ -58,25 +58,35 @@
         b_ref[span, :] = both[:, LANES:]
 
 
-def final_kernel(samples, chunks, share, tile_ref, kept_ref, other_ref, early_ref, far0_ref, far1_ref, *rest):
+def final_kernel(samples, chunks, share, tile_ref, near_ref, other_ref, early_ref, far_ref, rest_ref, *rest):
     nears, out_ref = rest[:-1], rest[-1]
     part = tile_ref.shape[0]
     step = LANES
     scale = 1.0 / samples
     out_ref[0] = tile_ref[...] * scale
-    for j, near_ref in enumerate(nears):
-        out_ref[1, :, j * step : (j + 1) * step] = near_ref[:part, :] * scale
-    out_ref[1, :, len(nears) * step :] = (kept_ref[0, :part, :] + other_ref[...]) * scale
+    for j, done_ref in enumerate(nears):
+        out_ref[1, :, j * step : (j + 1) * step] = done_ref[:part, :] * scale
+    out_ref[1, :, len(nears) * step :] = (near_ref[0] + other_ref[...]) * scale
     at = 0
     for j in range(chunks):
-        names = [(i, j) for i in range(j)] + [(j, j)] + [(j, i) for i in range(j)]
         if j == chunks - 1:
             at = 0
-        for row, column in names:
+        for row, column in far_names(j):
             rows = slice(at, at + share)
-            piece = early_ref[rows, :] if j < chunks - 1 else far0_ref[rows, :] + far1_ref[rows, :]
+            piece = early_ref[rows, :] if j < chunks - 1 else far_ref[0, rows, :] + rest_ref[rows, :]
             out_ref[2, row * share : (row + 1) * share, column * step : (column + 1) * step] = piece * scale
             at += share
+
+
+def by_route(parts, me):
+    if len(parts) != 4:
+        return by_distance(parts, me)
+    chip, core = me // 2 == 1, me % 2 == 1
+    near = [jnp.where(core, parts[2 + n], parts[n]) for n in range(2)]
+    away = [jnp.where(core, parts[n], parts[2 + n]) for n in range(2)]
+    near = [jnp.where(chip, near[1 - n], near[n]) for n in range(2)]
+    away = [jnp.where(chip, away[1 - n], away[n]) for n in range(2)]
+    return [near[0], away[0], near[1], away[1]]
 
 
 def own_kernel(samp, place_ref, values_ref, mean_ref, scale_ref, own_ref, *outs):
@@ -89,9 +99,13 @@
         flat = z.T
         own_ref[:, span] = flat
         total = accumulate(total, [matmul(flat, z)])
-    parts = [total[0][t * part : (t + 1) * part] for t in range(samp)]
-    for out_ref, value in zip(outs, by_distance(parts, place_ref[1])):
-        out_ref[...] = value
+    store(outs, by_distance([total[0][t * part : (t + 1) * part] for t in range(samp)], place_ref[1]), 0)
+
+
+def store(outs, values, row):
+    for d, value in enumerate(values):
+        outs[d % 2][d // 2, row : row + value.shape[0], :] = value
+    return row + values[0].shape[0]
 
 
 def base_kernel(place_ref, sa_ref, sb_ref, own_ref, *rest):
@@ -114,9 +128,8 @@
     far_out[...] = total[1]
 
 
-def step_kernel(samp, j, results, place_ref, sa_ref, sb_ref, a_ref, b_ref, own_ref, base_near, base_far, *rest):
-    nears, fars = rest[:j], rest[j : 2 * j]
-    saved, outs = rest[2 * j : len(rest) - results], rest[len(rest) - results :]
+def step_kernel(samp, j, whole, place_ref, sa_ref, sb_ref, a_ref, b_ref, own_ref, base_near, base_far, *rest):
+    nears, fars, near_ref, saved, outs = rest[:j], rest[j : 2 * j], rest[2 * j], rest[2 * j + 1 : -2], rest[-2:]
     rows, step = a_ref.shape
     skip = own_ref.shape[1] - rows
     part, share = own_ref.shape[0] // samp, step // samp
@@ -131,31 +144,41 @@
         a, b = a_ref[span, :].astype(jnp.float32), b_ref[span, :].astype(jnp.float32)
         near = ((jnp.where(even, a, b) - after[0:1]) * after[1:2]).astype(jnp.bfloat16)
         far = ((jnp.where(even, b, a) - before[2:3]) * before[3:4]).astype(jnp.bfloat16).T
-        if saved:
-            saved[0][span, :] = near
-            saved[1][:, span] = far
-        terms = [matmul(own_ref[:, pl.ds(skip + k, DEPTH)], near)]
+        near_ref[span, :] = near
+        if whole:
+            saved[0][:, span] = far
+        terms = [matmul(own_ref[:, pl.ds(skip + k, DEPTH)], near)] if whole else []
         terms += [matmul(fars[i][:, span], near) for i in range(j)]
         terms += [matmul(far, jnp.concatenate([near] + [nears[i][span, :] for i in range(j)], 1))]
         total = accumulate(total, terms)
-    blocks = total[1:-1] + [total[-1][:, i * step : (i + 1) * step] for i in range(j + 1)]
-    names = [(i, j) for i in range(j)] + [(j, j)] + [(j, i) for i in range(j)]
-    parts = []
-    for t in range(samp):
-        parts.append([total[0][t * part : (t + 1) * part] + base_near[t * part : (t + 1) * part, cols]])
-        for block, (row, column) in zip(blocks, names):
-            first = t * part + row * share
-            base = base_far[first : first + share, column * step : (column + 1) * step]
-            parts[t].append(block[t * share : (t + 1) * share] + base)
-    parts = [by_distance([parts[t][n] for t in range(samp)], me) for n in range(len(blocks) + 1)]
-    if len(outs) != samp:
-        outs = [outs[d % 2].at[d // 2] for d in range(samp)]
-    for d, out_ref in enumerate(outs):
-        row = 0
-        for piece in parts:
-            size = piece[d].shape[0]
-            out_ref[row : row + size, :] = piece[d]
-            row += size
+    row = 0
+    if whole:
+        row = store(outs, near_parts(samp, total.pop(0), base_near, me, cols), row)
+    blocks = total[:-1] + [total[-1][:, i * step : (i + 1) * step] for i in range(j + 1)]
+    for block, (up, down) in zip(blocks, far_names(j)):
+        parts = []
+        for t in range(samp):
+            first = t * part + up * share
+            base = base_far[first : first + share, down * step : (down + 1) * step]
+            parts.append(block[t * share : (t + 1) * share] + base)
+        row = store(outs, by_distance(parts, me) if whole else by_route(parts, me), row)
+
+
+def near_parts(samp, tile, base_near, me, cols):
+    part = tile.shape[0] // samp
+    spans = [slice(t * part, (t + 1) * part) for t in range(samp)]
+    return by_distance([tile[span] + base_near[span, cols] for span in spans], me)
+
+
+def near_kernel(samp, j, place_ref, near_ref, own_ref, base_near, *outs):
+    rows, step = near_ref.shape
+    skip = own_ref.shape[1] - rows
+    tile = matmul(own_ref[:, pl.ds(skip, rows)], near_ref[...])
+    store(outs, near_parts(samp, tile, base_near, place_ref[1], pl.ds(j * step, step)), 0)
+
+
+def far_names(j):
+    return [(i, j) for i in range(j)] + [(j, j)] + [(j, i) for i in range(j)]
 
 
 def call(kernel, out_shapes, flops, *args, scalars=True):
@@ -194,10 +217,14 @@
         grid = vector.reshape(*lead, samp, chunks, share)
         return jnp.swapaxes(grid, -3, -2).reshape(*lead, width)
 
-    def scatter_sum(parts):
-        total = parts[0]
-        for d in range(1, samp):
-            total = total + lax.ppermute(parts[d], "samp", [(i, i ^ d) for i in range(samp)])
+    def swap(array, distance):
+        return lax.ppermute(array, "samp", [(i, i ^ distance) for i in range(samp)])
+
+    def scatter_sum(kept, sent):
+        kept = kept + swap(sent, 1)
+        total = kept[0]
+        for n in range(1, samp // 2):
+            total = total + swap(kept[n], 2 * n)
         return total
 
     def f32(*shape):
@@ -236,46 +263,55 @@
 
     own, *parts = call(
         functools.partial(own_kernel, samp),
-        [bf16(width, local_rows)] + [f32(part, width)] * samp,
+        [bf16(width, local_rows)] + [f32(samp // 2, part, width)] * 2,
         2 * local_rows * width * width,
         place, dosage, mean[None], scale[None],
     )
-    tile = scatter_sum(parts)
+    tile = scatter_sum(*parts)
 
     base = call(base_kernel, [f32(width, width)] * 2, 4 * half * width * width, place, sa, sb, own, *heads)
     nears, fars, totals = [], [], []
     for j in range(chunks):
-        size = part + (2 * j + 1) * share
+        blocks = (2 * j + 1) * share
         last = j == chunks - 1
-        results = [f32(samp // 2, size, step)] * 2 if last else [f32(size, step)] * samp
-        saved = [] if last else [bf16(half, step), bf16(step, half)]
-        kept = call(
-            functools.partial(step_kernel, samp, j, len(results)),
-            saved + results,
-            2 * half * step * (width + (2 * j + 1) * step),
+        near, *saved, kept, sent = call(
+            functools.partial(step_kernel, samp, j, not last),
+            [bf16(half, step)]
+            + ([] if last else [bf16(step, half)])
+            + [f32(samp // 2, blocks + (0 if last else part), step)] * 2,
+            2 * half * step * ((0 if last else width) + (2 * j + 1) * step),
             place, sa, sb, *raw[j], own, *base, *nears, *fars,
         )
-        parts = kept[len(saved) :]
         if not last:
-            nears.append(kept[0])
-            fars.append(kept[1])
-            totals.append(scatter_sum(parts))
+            nears.append(near)
+            fars += saved
+            totals.append(scatter_sum(kept, sent))
     early = lax.ppermute(
-        jnp.concatenate([total[part:] for total in totals]), "chain", [(i + 1, i) for i in range(chain - 1)]
+        jnp.concatenate([total[part:] for total in totals]), "chain", [(i + 1, i) for i in range(chain - 2)]
     )
-    kept = parts[0] + lax.ppermute(parts[1], "samp", [(i, i ^ 1) for i in range(samp)])
-    others, far = [], []
-    for n in range(samp // 2):
-        moved = [i ^ (2 * n) for i in range(samp)]
-        pairs = [((c + 1) * samp + i, c * samp + moved[i]) for c in range(chain - 1) for i in range(samp)]
-        far.append(lax.ppermute(kept[n, part:], ("chain", "samp"), pairs))
-        if n:
-            others.append(lax.ppermute(kept[n, :part], "samp", [(i, moved[i]) for i in range(samp)]))
+    kept = kept + swap(sent, 1)
+    near, sent = call(
+        functools.partial(near_kernel, samp, chunks - 1), [f32(samp // 2, part, step)] * 2, 2 * half * step * width,
+        place, near, own, base[0],
+    )
+    near = near + swap(sent, 1)
+
+    def down(array, moved):
+        pairs = [((c + 1) * samp + i, c * samp + moved(i)) for c in range(chain - 2) for i in range(samp)]
+        return lax.ppermute(array, ("chain", "samp"), pairs)
+
+    if samp == 4:
+        far = down(kept, lambda i: i % 2 * 2 + i // 2)
+        rest = swap(far[1], 1)
+    else:
+        rest = sum(down(kept[n], lambda i: i ^ (2 * n)) for n in range(1, samp // 2))
+        far = down(kept[:1], lambda i: i)
+    other = sum(swap(near[n], 2 * n) for n in range(1, samp // 2))
     (out,) = call(
         functools.partial(final_kernel, samples, chunks, share),
         [f32(3, part, width)],
         0,
-        tile, kept, sum(others), early, far[0], sum(far[1:]), *totals,
+        tile, near, other, early, far, rest, *totals,
         scalars=False,
     )
     return jnp.swapaxes(out, 0, 1)[None]

time: 144 us -> 140 us (0.972)
  waiting for transfers between devices: 62.9 us -> 42.2 us
  starting transfers between devices: 44.5 us -> 51.4 us
  local copies, waits for them, and re-layouts: 7.21 us -> 12.1 us
  other arithmetic: 1.51 us -> 4.77 us
    ppermute x14, waiting for transfers between devices: 45.5 us -> 22.1 us  [exchange(): lax.ppermute(array, 'chain', pairs)]
    ppermute x14, starting transfers between devices: 30.4 us -> 41.3 us  [exchange(): lax.ppermute(array, 'chain', pairs)]
    ppermute x1, waiting for transfers between devices: 0.01 us -> 5.25 us  [body(): lax.ppermute(jnp.concatenate([total[part:] for total in totals]), 'chain'...]
    unnamed x6 -> x16, local copies, waits for them, and re-layouts: 2.19 us -> 7.16 us
    ppermute x16 -> x13, starting transfers between devices: 12.8 us -> 8.82 us  [the longest x12 7.54 us: swap(): return lax.ppermute(array, 'samp', [(i, i ^ distance) for i in range(samp)])]
    ppermute x16 -> x13, waiting for transfers between devices: 17.4 us -> 14.9 us  [the longest x12 12.1 us: swap(): return lax.ppermute(array, 'samp', [(i, i ^ distance) for i in range(samp)])]
    reduce_sum x1, other arithmetic: 1.14 us -> 3.33 us  [body(): jnp.sum(values * values, 0)]
    pallas_call x11 -> x12, Pallas kernels: 20 us -> 20.6 us  [call(): pl.pallas_call(kernel, out_shape=out_shapes, in_specs=specs, out_specs=[v...]
  transfers between devices with their start and end apart: 31 -> 28, of which waited for: 11 -> 11; matrix products, arithmetic and copies ran while one was open for 1% -> 4% of each run, Pallas kernels for 13% -> 12%
where the time goes in v5:
time: 140 us; the launch traced here: 139 us
  starting transfers between devices  51.4 us (37%)
  waiting for transfers between devices  42.2 us (30%)
  Pallas kernels  20.6 us (15%)
  local copies, waits for them, and re-layouts  12.1 us (9%)
  blocking collectives  6.6 us (5%)
  other arithmetic  4.77 us (3%)
    ppermute x14, starting transfers between devices, exchange(): lax.ppermute(array, 'chain', pairs)  41.3 us
    ppermute x14, waiting for transfers between devices, exchange(): lax.ppermute(array, 'chain', pairs)  22.1 us
    pallas_call x12, Pallas kernels, call(): pl.pallas_call(kernel, out_shape=out_shapes, in_specs=specs, out_specs=[v...  20.6 us
    ppermute x12, waiting for transfers between devices, swap(): return lax.ppermute(array, 'samp', [(i, i ^ distance) for i in range(samp)])  12.1 us
    ppermute x12, starting transfers between devices, swap(): return lax.ppermute(array, 'samp', [(i, i ^ distance) for i in range(samp)])  7.54 us
    unnamed x16, local copies, waits for them, and re-layouts  7.16 us
    psum x1, blocking collectives, body(): lax.psum((jnp.sum(values, 0), jnp.sum(values * values, 0)), 'samp')  6.6 us
    ppermute x1, waiting for transfers between devices, body(): lax.ppermute(jnp.concatenate([total[part:] for total in totals]), 'chain'...  5.25 us
  transfers between devices with their start and end apart: 28, of which 11 were waited for; matrix products, arithmetic and copies ran while one was open for 4% of the time, Pallas kernels for 12%

profile of v5, /device:TPU:0, one launch (start us, length us, event | category | flops | bytes accessed | tf_op | source)
XLA Modules:
  0.0 138.8 jit_solution(5400432534791115625)
XLA Ops:
  1.9 2.7 %slice.46 = bf16[1536,512]{1,0:T(8,128)(2,1)} slice(bf16[4096,512]{1,0:T(8,128)(2,1)} %values_ref.4), slice={[512:2048], [0:512]} | slice | bytes 3145728 | tf_op jit(solution)/shard_map/slice | solution.py:240
  4.6 4.9 %collective-permute-start.8 = (bf16[1536,512]{1,0:T(8,128)(2,1)}, bf16[1536,512]{1,0:T(8,128)(2,1)S(1)}, u32[]{:S(2)}, u32[]{:S(2)}) collective-permute-start(bf16[1536,512]{1,0:T(8,128)(2,1)} %slice.46), channel_id=1, source_target_pairs={{0,4},{4,0},{12,8},{1,5},{5,1},{13,9},{2,6},{6,2},{14,10},{3,7},{7... | collective-permute-start | bytes 4718600 | tf_op jit(solution)/shard_map/ppermute | solution.py:19
  10.3 3.3 %fusion = (f32[512]{0:T(512)S(1)}, f32[512]{0:T(512)S(1)}) fusion(bf16[4096,512]{1,0:T(8,128)(2,1)} %values_ref.4), kind=kLoop, calls=%fused_computation.2 | loop fusion | flops 8387584 | bytes 4198400 | tf_op jit(solution)/shard_map/reduce_sum | solution.py:253
  14.3 6.6 %all-reduce = (f32[512]{0:T(512)S(1)}, f32[512]{0:T(512)S(1)}) all-reduce(f32[512]{0:T(512)S(1)} %get-tuple-element.74, f32[512]{0:T(512)S(1)} %get-tuple-element.73), channel_id=1, replica_groups=mesh['groups'=2,'chain'=4,'samp'=4] {'samp'}, use_global_device_ids=true, to_apply=%region_1.2 | all-reduce | flops 1024 | bytes 8192 | tf_op jit(solution)/shard_map/psum | solution.py:253
  21.0 2.2 %copy-done.2 = bf16[4096,512]{1,0:T(8,128)(2,1)S(1)} copy-done((bf16[4096,512]{1,0:T(8,128)(2,1)S(1)}, bf16[4096,512]{1,0:T(8,128)(2,1)}, u32[]{:S(2)}) %copy-start.2) | copy-done | bytes 4194328
  23.2 3.7 %shard_map.37 = (bf16[512,4096]{1,0:T(8,128)(2,1)S(1)}, f32[2,128,512]{2,1,0:T(8,128)S(1)}, f32[2,128,512]{2,1,0:T(8,128)}) custom-call(s32[2]{0:T(128)S(1)} %pad_add_fusion.place_ref, bf16[4096,512]{1,0:T(8,128)(2,1)S(1)} %copy-done.2, f32[1,512]{1,0:T(1,128)S(1)} %bitcast.41, f32[1,512]{1,0:T(1,128)S(1)} %bitcast.39), custom_call_target="tpu_custom_call" | custom-call | flops 2147483648 | bytes 9441288 | tf_op jit(solution)/shard_map/pallas_call | solution.py:190
  26.9 2.0 %copy-done = bf16[512,4096]{1,0:T(8,128)(2,1)} copy-done((bf16[512,4096]{1,0:T(8,128)(2,1)}, bf16[512,4096]{1,0:T(8,128)(2,1)S(1)}, u32[]{:S(2)}) %copy-start) | copy-done | bytes 4194328
  30.0 4.0 %collective-permute-start.2 = (f32[4,512]{1,0:T(4,128)S(1)}, f32[4,512]{1,0:T(4,128)S(1)}, u32[]{:S(2)}, u32[]{:S(2)}) collective-permute-start(f32[4,512]{1,0:T(4,128)S(1)} %pad_maximum_fusion.1), channel_id=1, source_target_pairs={{0,4},{4,0},{12,8},{1,5},{5,1},{13,9},{2,6},{6,2},{14,10},{3,7},{7... | collective-permute-start | bytes 24584 | tf_op jit(solution)/shard_map/ppermute | solution.py:19
  34.7 9.6 %collective-permute-done.2.sa_ref = f32[4,512]{1,0:T(4,128)S(1)} collective-permute-done((f32[4,512]{1,0:T(4,128)S(1)}, f32[4,512]{1,0:T(4,128)S(1)}, u32[]{:S(2)}, u32[]{:S(2)}) %collective-permute-start.2) | collective-permute-done | bytes 8224 | tf_op jit(solution)/shard_map/ppermute | solution.py:19
  44.3 3.6 %collective-permute-start.6 = (bf16[512,512]{1,0:T(8,128)(2,1)}, bf16[512,512]{1,0:T(8,128)(2,1)S(1)}, u32[]{:S(2)}, u32[]{:S(2)}) collective-permute-start(bf16[512,512]{1,0:T(8,128)(2,1)} %slice.45), channel_id=1, source_target_pairs={{0,4},{4,0},{12,8},{1,5},{5,1},{13,9},{2,6},{6,2},{14,10},{3,7},{7... | collective-permute-start | bytes 1572872 | tf_op jit(solution)/shard_map/ppermute | solution.py:19
  48.7 2.2 %copy-done.3 = bf16[4096,512]{1,0:T(8,128)(2,1)S(1)} copy-done((bf16[4096,512]{1,0:T(8,128)(2,1)S(1)}, bf16[4096,512]{1,0:T(8,128)(2,1)}, u32[]{:S(2)}) %copy-start.3) | copy-done | bytes 4194328
  52.1 4.1 %collective-permute-start.10 = (bf16[2048,128]{1,0:T(8,128)(2,1)S(1)}, bf16[2048,128]{1,0:T(8,128)(2,1)S(1)}, u32[]{:S(2)}, u32[]{:S(2)}) collective-permute-start(bf16[2048,128]{1,0:T(8,128)(2,1)S(1)} %get-tuple-element.50), channel_id=1, source_target_pairs={{0,4},{4,0},{12,8},{1,5},{5,1},{13,9},{2,6},{6,2},{14,10},{3,7},{7... | collective-permute-start | bytes 1572872 | tf_op jit(solution)/shard_map/ppermute | solution.py:19
  57.5 3.7 %collective-permute-done.6.rest_0_ = bf16[512,512]{1,0:T(8,128)(2,1)S(1)} collective-permute-done((bf16[512,512]{1,0:T(8,128)(2,1)}, bf16[512,512]{1,0:T(8,128)(2,1)S(1)}, u32[]{:S(2)}, u32[]{:S(2)}) %collective-permute-start.6) | collective-permute-done | bytes 524320 | tf_op jit(solution)/shard_map/ppermute | solution.py:19
  61.9 6.4 %collective-permute-start.12 = (bf16[2048,128]{1,0:T(8,128)(2,1)S(1)}, bf16[2048,128]{1,0:T(8,128)(2,1)S(1)}, u32[]{:S(2)}, u32[]{:S(2)}) collective-permute-start(bf16[2048,128]{1,0:T(8,128)(2,1)S(1)} %get-tuple-element.53), channel_id=1, source_target_pairs={{0,4},{4,0},{12,8},{1,5},{5,1},{13,9},{2,6},{6,2},{14,10},{3,7},{7... | collective-permute-start | bytes 1572872 | tf_op jit(solution)/shard_map/ppermute | solution.py:19
  68.3 4.1 %collective-permute-done.10.a_ref = bf16[2048,128]{1,0:T(8,128)(2,1)S(1)} collective-permute-done((bf16[2048,128]{1,0:T(8,128)(2,1)S(1)}, bf16[2048,128]{1,0:T(8,128)(2,1)S(1)}, u32[]{:S(2)}, u32[]{:S(2)}) %collective-permute-start.10) | collective-permute-done | bytes 524320 | tf_op jit(solution)/shard_map/ppermute | solution.py:19
  74.5 6.6 %collective-permute-start.14 = (bf16[2048,128]{1,0:T(8,128)(2,1)S(1)}, bf16[2048,128]{1,0:T(8,128)(2,1)S(1)}, u32[]{:S(2)}, u32[]{:S(2)}) collective-permute-start(bf16[2048,128]{1,0:T(8,128)(2,1)S(1)} %get-tuple-element.57), channel_id=1, source_target_pairs={{0,4},{4,0},{12,8},{1,5},{5,1},{13,9},{2,6},{6,2},{14,10},{3,7},{7... | collective-permute-start | bytes 1572872 | tf_op jit(solution)/shard_map/ppermute | solution.py:19
  81.1 2.5 %collective-permute-done.12.a_ref = bf16[2048,128]{1,0:T(8,128)(2,1)S(1)} collective-permute-done((bf16[2048,128]{1,0:T(8,128)(2,1)S(1)}, bf16[2048,128]{1,0:T(8,128)(2,1)S(1)}, u32[]{:S(2)}, u32[]{:S(2)}) %collective-permute-start.12) | collective-permute-done | bytes 524320 | tf_op jit(solution)/shard_map/ppermute | solution.py:19
  85.6 6.4 %collective-permute-start.4 = (bf16[2048,128]{1,0:T(8,128)(2,1)S(1)}, bf16[2048,128]{1,0:T(8,128)(2,1)S(1)}, u32[]{:S(2)}, u32[]{:S(2)}) collective-permute-start(bf16[2048,128]{1,0:T(8,128)(2,1)S(1)} %get-tuple-element.43), channel_id=1, source_target_pairs={{0,4},{4,0},{12,8},{1,5},{5,1},{13,9},{2,6},{6,2},{14,10},{3,7},{7... | collective-permute-start | bytes 1572872 | tf_op jit(solution)/shard_map/ppermute | solution.py:19
  94.1 3.1 %shard_map.39 = (f32[512,512]{1,0:T(8,128)S(1)}, f32[512,512]{1,0:T(8,128)S(1)}) custom-call(s32[2]{0:T(128)S(1)} %pad_add_fusion.place_ref, f32[4,512]{1,0:T(4,128)S(1)} %collective-permute-done.2.sa_ref, f32[4,512]{1,0:T(4,128)S(1)} %collective-permute-done.3.sb_ref, bf16[512,4096]{1,0:T(8,128)(2,1)S(1)} %copy-done.1, ...), custom_call_target="tpu_custom_call" | custom-call | flops 2147483648 | bytes 10502152 | tf_op jit(solution)/shard_map/pallas_call | solution.py:190
  102.3 2.1 %collective-permute-done.4.a_ref = bf16[2048,128]{1,0:T(8,128)(2,1)S(1)} collective-permute-done((bf16[2048,128]{1,0:T(8,128)(2,1)S(1)}, bf16[2048,128]{1,0:T(8,128)(2,1)S(1)}, u32[]{:S(2)}, u32[]{:S(2)}) %collective-permute-start.4) | collective-permute-done | bytes 524320 | tf_op jit(solution)/shard_map/ppermute | solution.py:19
  113.8 5.9 %collective-permute-done.19 = f32[160,128]{1,0:T(8,128)S(1)} collective-permute-done((f32[160,128]{1,0:T(8,128)S(1)}, f32[160,128]{1,0:T(8,128)S(1)}, u32[]{:S(2)}, u32[]{:S(2)}) %collective-permute-start.19) | collective-permute-done | bytes 81952 | tf_op jit(solution)/shard_map/ppermute | solution.py:221
  122.6 4.2 %collective-permute-done.23 = f32[288,128]{1,0:T(8,128)S(1)} collective-permute-done((f32[288,128]{1,0:T(8,128)S(1)}, f32[288,128]{1,0:T(8,128)S(1)}, u32[]{:S(2)}, u32[]{:S(2)}) %collective-permute-start.23) | collective-permute-done | bytes 147488 | tf_op jit(solution)/shard_map/ppermute | solution.py:221
  128.1 2.8 %collective-permute-done.26.far_ref = f32[2,224,128]{2,1,0:T(8,128)S(1)} collective-permute-done((f32[2,224,128]{2,1,0:T(8,128)S(1)}, f32[2,224,128]{2,1,0:T(8,128)S(1)}, u32[]{:S(2)}, u32[]{:S(2)}) %collective-permute-start.26) | collective-permute-done | bytes 229408 | tf_op jit(solution)/shard_map/ppermute | solution.py:301
  132.6 5.3 %collective-permute-done.24.early_ref = f32[288,128]{1,0:T(8,128)S(1)} collective-permute-done((f32[288,128]{1,0:T(8,128)S(1)}, f32[288,128]{1,0:T(8,128)S(1)}, u32[]{:S(2)}, u32[]{:S(2)}) %collective-permute-start.24) | collective-permute-done | bytes 147488 | tf_op jit(solution)/shard_map/ppermute | solution.py:289
  (92 shorter events, 35.6 us)
Async XLA Ops:
  4.6 81.0 %collective-permute-start.8 = (bf16[1536,512]{1,0:T(8,128)(2,1)}, bf16[1536,512]{1,0:T(8,128)(2,1)S(1)}, u32[]{:S(2)}, u32[]{:S(2)}) collective-permute-start(bf16[1536,512]{1,0:T(8,128)(2,1)} %slice.46), channel_id=1, source_target_pairs={{0,4},{4,0},{12,8},{1,5},{5,1},{13,9},{2,6},{6,2},{14,10},{3,7},{7... | collective-permute-start | bytes 4718600 | tf_op jit(solution)/shard_map/ppermute | solution.py:19
  9.5 82.5 %collective-permute-start.9 = (bf16[1536,512]{1,0:T(8,128)(2,1)}, bf16[1536,512]{1,0:T(8,128)(2,1)S(1)}, u32[]{:S(2)}, u32[]{:S(2)}) collective-permute-start(bf16[1536,512]{1,0:T(8,128)(2,1)} %slice.46), channel_id=1, source_target_pairs={{4,8},{8,4},{5,9},{9,5},{6,10},{10,6},{7,11},{11,7},{20,24},{24,20... | collective-permute-start | bytes 4718600 | tf_op jit(solution)/shard_map/ppermute | solution.py:19
  29.7 22.4 %collective-permute-start = (f32[2,128,512]{2,1,0:T(8,128)}, f32[2,128,512]{2,1,0:T(8,128)}, u32[]{:S(2)}, u32[]{:S(2)}) collective-permute-start(f32[2,128,512]{2,1,0:T(8,128)} %get-tuple-element.42), channel_id=1, source_target_pairs={{0,1},{1,0},{2,3},{3,2},{4,5},{5,4},{6,7},{7,6},{8,9},{9,8},{10,11... | collective-permute-start | bytes 1572872 | tf_op jit(solution)/shard_map/ppermute | solution.py:221
  30.0 14.3 %collective-permute-start.2 = (f32[4,512]{1,0:T(4,128)S(1)}, f32[4,512]{1,0:T(4,128)S(1)}, u32[]{:S(2)}, u32[]{:S(2)}) collective-permute-start(f32[4,512]{1,0:T(4,128)S(1)} %pad_maximum_fusion.1), channel_id=1, source_target_pairs={{0,4},{4,0},{12,8},{1,5},{5,1},{13,9},{2,6},{6,2},{14,10},{3,7},{7... | collective-permute-start | bytes 24584 | tf_op jit(solution)/shard_map/ppermute | solution.py:19
  34.0 13.9 %collective-permute-start.3 = (f32[4,512]{1,0:T(4,128)S(1)}, f32[4,512]{1,0:T(4,128)S(1)}, u32[]{:S(2)}, u32[]{:S(2)}) collective-permute-start(f32[4,512]{1,0:T(4,128)S(1)} %pad_maximum_fusion.1), channel_id=1, source_target_pairs={{4,8},{8,4},{5,9},{9,5},{6,10},{10,6},{7,11},{11,7},{20,24},{24,20... | collective-permute-start | bytes 24584 | tf_op jit(solution)/shard_map/ppermute | solution.py:19
  44.3 16.9 %collective-permute-start.6 = (bf16[512,512]{1,0:T(8,128)(2,1)}, bf16[512,512]{1,0:T(8,128)(2,1)S(1)}, u32[]{:S(2)}, u32[]{:S(2)}) collective-permute-start(bf16[512,512]{1,0:T(8,128)(2,1)} %slice.45), channel_id=1, source_target_pairs={{0,4},{4,0},{12,8},{1,5},{5,1},{13,9},{2,6},{6,2},{14,10},{3,7},{7... | collective-permute-start | bytes 1572872 | tf_op jit(solution)/shard_map/ppermute | solution.py:19
  48.0 13.9 %collective-permute-start.7 = (bf16[512,512]{1,0:T(8,128)(2,1)}, bf16[512,512]{1,0:T(8,128)(2,1)S(1)}, u32[]{:S(2)}, u32[]{:S(2)}) collective-permute-start(bf16[512,512]{1,0:T(8,128)(2,1)} %slice.45), channel_id=1, source_target_pairs={{4,8},{8,4},{5,9},{9,5},{6,10},{10,6},{7,11},{11,7},{20,24},{24,20... | collective-permute-start | bytes 1572872 | tf_op jit(solution)/shard_map/ppermute | solution.py:19
  52.1 20.3 %collective-permute-start.10 = (bf16[2048,128]{1,0:T(8,128)(2,1)S(1)}, bf16[2048,128]{1,0:T(8,128)(2,1)S(1)}, u32[]{:S(2)}, u32[]{:S(2)}) collective-permute-start(bf16[2048,128]{1,0:T(8,128)(2,1)S(1)} %get-tuple-element.50), channel_id=1, source_target_pairs={{0,4},{4,0},{12,8},{1,5},{5,1},{13,9},{2,6},{6,2},{14,10},{3,7},{7... | collective-permute-start | bytes 1572872 | tf_op jit(solution)/shard_map/ppermute | solution.py:19
  61.2 13.3 %collective-permute-start.11 = (bf16[2048,128]{1,0:T(8,128)(2,1)S(1)}, bf16[2048,128]{1,0:T(8,128)(2,1)S(1)}, u32[]{:S(2)}, u32[]{:S(2)}) collective-permute-start(bf16[2048,128]{1,0:T(8,128)(2,1)S(1)} %get-tuple-element.51), channel_id=1, source_target_pairs={{4,8},{8,4},{5,9},{9,5},{6,10},{10,6},{7,11},{11,7},{20,24},{24,20... | collective-permute-start | bytes 1572872 | tf_op jit(solution)/shard_map/ppermute | solution.py:19
  61.9 21.8 %collective-permute-start.12 = (bf16[2048,128]{1,0:T(8,128)(2,1)S(1)}, bf16[2048,128]{1,0:T(8,128)(2,1)S(1)}, u32[]{:S(2)}, u32[]{:S(2)}) collective-permute-start(bf16[2048,128]{1,0:T(8,128)(2,1)S(1)} %get-tuple-element.53), channel_id=1, source_target_pairs={{0,4},{4,0},{12,8},{1,5},{5,1},{13,9},{2,6},{6,2},{14,10},{3,7},{7... | collective-permute-start | bytes 1572872 | tf_op jit(solution)/shard_map/ppermute | solution.py:19
  72.4 26.3 %collective-permute-start.13 = (bf16[2048,128]{1,0:T(8,128)(2,1)S(1)}, bf16[2048,128]{1,0:T(8,128)(2,1)S(1)}, u32[]{:S(2)}, u32[]{:S(2)}) collective-permute-start(bf16[2048,128]{1,0:T(8,128)(2,1)S(1)} %get-tuple-element.54), channel_id=1, source_target_pairs={{4,8},{8,4},{5,9},{9,5},{6,10},{10,6},{7,11},{11,7},{20,24},{24,20... | collective-permute-start | bytes 1572872 | tf_op jit(solution)/shard_map/ppermute | solution.py:19
  74.5 25.8 %collective-permute-start.14 = (bf16[2048,128]{1,0:T(8,128)(2,1)S(1)}, bf16[2048,128]{1,0:T(8,128)(2,1)S(1)}, u32[]{:S(2)}, u32[]{:S(2)}) collective-permute-start(bf16[2048,128]{1,0:T(8,128)(2,1)S(1)} %get-tuple-element.57), channel_id=1, source_target_pairs={{0,4},{4,0},{12,8},{1,5},{5,1},{13,9},{2,6},{6,2},{14,10},{3,7},{7... | collective-permute-start | bytes 1572872 | tf_op jit(solution)/shard_map/ppermute | solution.py:19
  83.7 16.7 %collective-permute-start.15 = (bf16[2048,128]{1,0:T(8,128)(2,1)S(1)}, bf16[2048,128]{1,0:T(8,128)(2,1)S(1)}, u32[]{:S(2)}, u32[]{:S(2)}) collective-permute-start(bf16[2048,128]{1,0:T(8,128)(2,1)S(1)} %get-tuple-element.58), channel_id=1, source_target_pairs={{4,8},{8,4},{5,9},{9,5},{6,10},{10,6},{7,11},{11,7},{20,24},{24,20... | collective-permute-start | bytes 1572872 | tf_op jit(solution)/shard_map/ppermute | solution.py:19
  85.6 18.8 %collective-permute-start.4 = (bf16[2048,128]{1,0:T(8,128)(2,1)S(1)}, bf16[2048,128]{1,0:T(8,128)(2,1)S(1)}, u32[]{:S(2)}, u32[]{:S(2)}) collective-permute-start(bf16[2048,128]{1,0:T(8,128)(2,1)S(1)} %get-tuple-element.43), channel_id=1, source_target_pairs={{0,4},{4,0},{12,8},{1,5},{5,1},{13,9},{2,6},{6,2},{14,10},{3,7},{7... | collective-permute-start | bytes 1572872 | tf_op jit(solution)/shard_map/ppermute | solution.py:19
  92.1 12.3 %collective-permute-start.5 = (bf16[2048,128]{1,0:T(8,128)(2,1)S(1)}, bf16[2048,128]{1,0:T(8,128)(2,1)S(1)}, u32[]{:S(2)}, u32[]{:S(2)}) collective-permute-start(bf16[2048,128]{1,0:T(8,128)(2,1)S(1)} %get-tuple-element.44), channel_id=1, source_target_pairs={{4,8},{8,4},{5,9},{9,5},{6,10},{10,6},{7,11},{11,7},{20,24},{24,20... | collective-permute-start | bytes 1572872 | tf_op jit(solution)/shard_map/ppermute | solution.py:19
  107.3 24.4 %collective-permute-start.1 = (f32[128,512]{1,0:T(8,128)S(1)}, f32[128,512]{1,0:T(8,128)S(1)}, u32[]{:S(2)}, u32[]{:S(2)}) collective-permute-start(f32[128,512]{1,0:T(8,128)S(1)} %slice_bitcast_fusion), channel_id=1, source_target_pairs={{0,2},{1,3},{2,0},{3,1},{4,6},{5,7},{6,4},{7,5},{8,10},{9,11},{10,... | collective-permute-start | bytes 786440 | tf_op jit(solution)/shard_map/ppermute | solution.py:221
  108.7 12.3 %collective-permute-start.22 = (f32[2,288,128]{2,1,0:T(8,128)S(1)}, f32[2,288,128]{2,1,0:T(8,128)S(1)}, u32[]{:S(2)}, u32[]{:S(2)}) collective-permute-start(f32[2,288,128]{2,1,0:T(8,128)S(1)} %get-tuple-element.70), channel_id=1, source_target_pairs={{0,1},{1,0},{2,3},{3,2},{4,5},{5,4},{6,7},{7,6},{8,9},{9,8},{10,11... | collective-permute-start | bytes 884744 | tf_op jit(solution)/shard_map/ppermute | solution.py:221
  109.5 3.6 %collective-permute-start.25 = (f32[2,224,128]{2,1,0:T(8,128)S(1)}, f32[2,224,128]{2,1,0:T(8,128)S(1)}, u32[]{:S(2)}, u32[]{:S(2)}) collective-permute-start(f32[2,224,128]{2,1,0:T(8,128)S(1)} %get-tuple-element.72), channel_id=1, source_target_pairs={{0,1},{1,0},{2,3},{3,2},{4,5},{5,4},{6,7},{7,6},{8,9},{9,8},{10,11... | collective-permute-start | bytes 688136 | tf_op jit(solution)/shard_map/ppermute | solution.py:221
  110.9 20.8 %collective-permute-start.17 = (f32[128,128]{1,0:T(8,128)S(1)}, f32[128,128]{1,0:T(8,128)S(1)}, u32[]{:S(2)}, u32[]{:S(2)}) collective-permute-start(f32[128,128]{1,0:T(8,128)S(1)} %slice_bitcast_fusion.9), channel_id=1, source_target_pairs={{0,2},{1,3},{2,0},{3,1},{4,6},{5,7},{6,4},{7,5},{8,10},{9,11},{10,... | collective-permute-start | bytes 196616 | tf_op jit(solution)/shard_map/ppermute | solution.py:221
  111.6 8.1 %collective-permute-start.19 = (f32[160,128]{1,0:T(8,128)S(1)}, f32[160,128]{1,0:T(8,128)S(1)}, u32[]{:S(2)}, u32[]{:S(2)}) collective-permute-start(f32[160,128]{1,0:T(8,128)S(1)} %slice_bitcast_fusion.7), channel_id=1, source_target_pairs={{0,2},{1,3},{2,0},{3,1},{4,6},{5,7},{6,4},{7,5},{8,10},{9,11},{10,... | collective-permute-start | bytes 245768 | tf_op jit(solution)/shard_map/ppermute | solution.py:221
  113.1 9.5 %collective-permute-start.21 = (f32[224,128]{1,0:T(8,128)S(1)}, f32[224,128]{1,0:T(8,128)S(1)}, u32[]{:S(2)}, u32[]{:S(2)}) collective-permute-start(f32[224,128]{1,0:T(8,128)S(1)} %slice_bitcast_fusion.5), channel_id=1, source_target_pairs={{0,2},{1,3},{2,0},{3,1},{4,6},{5,7},{6,4},{7,5},{8,10},{9,11},{10,... | collective-permute-start | bytes 344072 | tf_op jit(solution)/shard_map/ppermute | solution.py:221
  119.7 11.2 %collective-permute-start.26 = (f32[2,224,128]{2,1,0:T(8,128)S(1)}, f32[2,224,128]{2,1,0:T(8,128)S(1)}, u32[]{:S(2)}, u32[]{:S(2)}) collective-permute-start(f32[2,224,128]{2,1,0:T(8,128)S(1)} %add.56), channel_id=1, source_target_pairs={{4,0},{5,2},{6,1},{7,3},{8,4},{9,6},{10,5},{11,7},{20,16},{21,18},... | collective-permute-start | bytes 688136 | tf_op jit(solution)/shard_map/ppermute | solution.py:301
  121.1 5.7 %collective-permute-start.23 = (f32[288,128]{1,0:T(8,128)S(1)}, f32[288,128]{1,0:T(8,128)S(1)}, u32[]{:S(2)}, u32[]{:S(2)}) collective-permute-start(f32[288,128]{1,0:T(8,128)S(1)} %slice_bitcast_fusion.2), channel_id=1, source_target_pairs={{0,2},{1,3},{2,0},{3,1},{4,6},{5,7},{6,4},{7,5},{8,10},{9,11},{10,... | collective-permute-start | bytes 442376 | tf_op jit(solution)/shard_map/ppermute | solution.py:221
  126.8 11.0 %collective-permute-start.24 = (f32[288,128]{1,0:T(8,128)S(1)}, f32[288,128]{1,0:T(8,128)S(1)}, u32[]{:S(2)}, u32[]{:S(2)}) collective-permute-start(f32[288,128]{1,0:T(8,128)S(1)} %pad_maximum_fusion), channel_id=1, source_target_pairs={{4,0},{8,4},{5,1},{9,5},{6,2},{10,6},{7,3},{11,7},{20,16},{24,20},... | collective-permute-start | bytes 442376 | tf_op jit(solution)/shard_map/ppermute | solution.py:289
  (12 other events, 100.9 us)

commit v6 on v5

--- a/solution.py
+++ b/solution.py
@@ -15,7 +15,7 @@
 def exchange(array, devices, first):
     pairs = []
     for low in range(first, devices - 1, 2):
-        pairs += [(low + 1, low)] if low + 2 == devices else [(low, low + 1), (low + 1, low)]
+        pairs += [(low, low + 1), (low + 1, low)]
     return lax.ppermute(array, "chain", pairs) if pairs else jnp.zeros_like(array)
 
 
@@ -58,7 +58,7 @@
         b_ref[span, :] = both[:, LANES:]
 
 
-def final_kernel(samples, chunks, share, tile_ref, near_ref, other_ref, early_ref, far_ref, rest_ref, *rest):
+def final_kernel(samples, chunks, share, tile_ref, near_ref, other_ref, early_ref, far0_ref, far1_ref, *rest):
     nears, out_ref = rest[:-1], rest[-1]
     part = tile_ref.shape[0]
     step = LANES
@@ -73,20 +73,9 @@
             at = 0
         for row, column in far_names(j):
             rows = slice(at, at + share)
-            piece = early_ref[rows, :] if j < chunks - 1 else far_ref[0, rows, :] + rest_ref[rows, :]
+            piece = early_ref[rows, :] if j < chunks - 1 else far0_ref[rows, :] + far1_ref[rows, :]
             out_ref[2, row * share : (row + 1) * share, column * step : (column + 1) * step] = piece * scale
             at += share
-
-
-def by_route(parts, me):
-    if len(parts) != 4:
-        return by_distance(parts, me)
-    chip, core = me // 2 == 1, me % 2 == 1
-    near = [jnp.where(core, parts[2 + n], parts[n]) for n in range(2)]
-    away = [jnp.where(core, parts[n], parts[2 + n]) for n in range(2)]
-    near = [jnp.where(chip, near[1 - n], near[n]) for n in range(2)]
-    away = [jnp.where(chip, away[1 - n], away[n]) for n in range(2)]
-    return [near[0], away[0], near[1], away[1]]
 
 
 def own_kernel(samp, place_ref, values_ref, mean_ref, scale_ref, own_ref, *outs):
@@ -161,7 +150,7 @@
             first = t * part + up * share
             base = base_far[first : first + share, down * step : (down + 1) * step]
             parts.append(block[t * share : (t + 1) * share] + base)
-        row = store(outs, by_distance(parts, me) if whole else by_route(parts, me), row)
+        row = store(outs, by_distance(parts, me), row)
 
 
 def near_parts(samp, tile, base_near, me, cols):
@@ -295,23 +284,17 @@
         place, near, own, base[0],
     )
     near = near + swap(sent, 1)
-
-    def down(array, moved):
-        pairs = [((c + 1) * samp + i, c * samp + moved(i)) for c in range(chain - 2) for i in range(samp)]
-        return lax.ppermute(array, ("chain", "samp"), pairs)
-
-    if samp == 4:
-        far = down(kept, lambda i: i % 2 * 2 + i // 2)
-        rest = swap(far[1], 1)
-    else:
-        rest = sum(down(kept[n], lambda i: i ^ (2 * n)) for n in range(1, samp // 2))
-        far = down(kept[:1], lambda i: i)
-    other = sum(swap(near[n], 2 * n) for n in range(1, samp // 2))
+    others, far = [], []
+    for n in range(samp // 2):
+        pairs = [((c + 1) * samp + i, c * samp + (i ^ (2 * n))) for c in range(chain - 2) for i in range(samp)]
+        far.append(lax.ppermute(kept[n], ("chain", "samp"), pairs))
+        if n:
+            others.append(swap(near[n], 2 * n))
     (out,) = call(
         functools.partial(final_kernel, samples, chunks, share),
         [f32(3, part, width)],
         0,
-        tile, near, other, early, far, rest, *totals,
+        tile, near, sum(others), early, far[0], sum(far[1:]), *totals,
         scalars=False,
     )
     return jnp.swapaxes(out, 0, 1)[None]

time: 140 us -> 140 us (level)
  waiting for transfers between devices: 42.2 us -> 48.6 us
  starting transfers between devices: 51.4 us -> 46 us
    ppermute x14, starting transfers between devices: 41.3 us -> 35.3 us  [exchange(): lax.ppermute(array, 'chain', pairs)]
    ppermute x1, waiting for transfers between devices: 5.25 us -> 8.42 us  [body(): lax.ppermute(jnp.concatenate([total[part:] for total in totals]), 'chain'...]
    ppermute x1 -> x2, waiting for transfers between devices: 2.75 us -> 5.08 us  [body(): far.append(lax.ppermute(kept[n], ('chain', 'samp'), pairs))]
    ppermute x14, waiting for transfers between devices: 22.1 us -> 24.4 us  [exchange(): lax.ppermute(array, 'chain', pairs)]
    ppermute x12 -> x11, waiting for transfers between devices: 12.1 us -> 10.7 us  [swap(): return lax.ppermute(array, 'samp', [(i, i ^ distance) for i in range(samp)])]
    ppermute x12 -> x11, starting transfers between devices: 7.54 us -> 6.79 us  [swap(): return lax.ppermute(array, 'samp', [(i, i ^ distance) for i in range(samp)])]
where the time goes in v6:
time: 140 us
  waiting for transfers between devices  48.6 us (35%)
  starting transfers between devices  46 us (33%)
  Pallas kernels  20.6 us (15%)
  local copies, waits for them, and re-layouts  12.1 us (9%)
  blocking collectives  6.6 us (5%)
  other arithmetic  4.78 us (3%)
    ppermute x14, starting transfers between devices, exchange(): lax.ppermute(array, 'chain', pairs)  35.3 us
    ppermute x14, waiting for transfers between devices, exchange(): lax.ppermute(array, 'chain', pairs)  24.4 us
    pallas_call x12, Pallas kernels, call(): pl.pallas_call(kernel, out_shape=out_shapes, in_specs=specs, out_specs=[v...  20.6 us
    ppermute x11, waiting for transfers between devices, swap(): return lax.ppermute(array, 'samp', [(i, i ^ distance) for i in range(samp)])  10.7 us
    ppermute x1, waiting for transfers between devices, body(): lax.ppermute(jnp.concatenate([total[part:] for total in totals]), 'chain'...  8.42 us
    unnamed x16, local copies, waits for them, and re-layouts  7.17 us
    ppermute x11, starting transfers between devices, swap(): return lax.ppermute(array, 'samp', [(i, i ^ distance) for i in range(samp)])  6.79 us
    psum x1, blocking collectives, body(): lax.psum((jnp.sum(values, 0), jnp.sum(values * values, 0)), 'samp')  6.6 us
  transfers between devices with their start and end apart: 28, of which 11 were waited for; matrix products, arithmetic and copies ran while one was open for 4% of the time, Pallas kernels for 12%

profile of v6, /device:TPU:0, one launch (start us, length us, event | category | flops | bytes accessed | tf_op | source)
XLA Modules:
  0.0 139.7 jit_solution(4827434641658146504)
XLA Ops:
  1.9 2.7 %slice.49 = bf16[1536,512]{1,0:T(8,128)(2,1)} slice(bf16[4096,512]{1,0:T(8,128)(2,1)} %values_ref.4), slice={[512:2048], [0:512]} | slice | bytes 3145728 | tf_op jit(solution)/shard_map/slice | solution.py:229
  4.6 3.1 %collective-permute-start.8 = (bf16[1536,512]{1,0:T(8,128)(2,1)}, bf16[1536,512]{1,0:T(8,128)(2,1)S(1)}, u32[]{:S(2)}, u32[]{:S(2)}) collective-permute-start(bf16[1536,512]{1,0:T(8,128)(2,1)} %slice.49), channel_id=1, source_target_pairs={{0,4},{4,0},{8,12},{12,8},{1,5},{5,1},{9,13},{13,9},{2,6},{6,2},{1... | collective-permute-start | bytes 4718600 | tf_op jit(solution)/shard_map/ppermute | solution.py:19
  8.4 3.3 %fusion = (f32[512]{0:T(512)S(1)}, f32[512]{0:T(512)S(1)}) fusion(bf16[4096,512]{1,0:T(8,128)(2,1)} %values_ref.4), kind=kLoop, calls=%fused_computation.2 | loop fusion | flops 8387584 | bytes 4198400 | tf_op jit(solution)/shard_map/reduce_sum | solution.py:242
  12.4 6.6 %all-reduce = (f32[512]{0:T(512)S(1)}, f32[512]{0:T(512)S(1)}) all-reduce(f32[512]{0:T(512)S(1)} %get-tuple-element.74, f32[512]{0:T(512)S(1)} %get-tuple-element.73), channel_id=1, replica_groups=mesh['groups'=2,'chain'=4,'samp'=4] {'samp'}, use_global_device_ids=true, to_apply=%region_1.2 | all-reduce | flops 1024 | bytes 8192 | tf_op jit(solution)/shard_map/psum | solution.py:242
  19.1 2.2 %copy-done.2 = bf16[4096,512]{1,0:T(8,128)(2,1)S(1)} copy-done((bf16[4096,512]{1,0:T(8,128)(2,1)S(1)}, bf16[4096,512]{1,0:T(8,128)(2,1)}, u32[]{:S(2)}) %copy-start.2) | copy-done | bytes 4194328
  21.3 3.7 %shard_map.37 = (bf16[512,4096]{1,0:T(8,128)(2,1)S(1)}, f32[2,128,512]{2,1,0:T(8,128)S(1)}, f32[2,128,512]{2,1,0:T(8,128)}) custom-call(s32[2]{0:T(128)S(1)} %pad_add_fusion.place_ref, bf16[4096,512]{1,0:T(8,128)(2,1)S(1)} %copy-done.2, f32[1,512]{1,0:T(1,128)S(1)} %bitcast.43, f32[1,512]{1,0:T(1,128)S(1)} %bitcast.41), custom_call_target="tpu_custom_call" | custom-call | flops 2147483648 | bytes 9441288 | tf_op jit(solution)/shard_map/pallas_call | solution.py:179
  25.0 2.0 %copy-done = bf16[512,4096]{1,0:T(8,128)(2,1)} copy-done((bf16[512,4096]{1,0:T(8,128)(2,1)}, bf16[512,4096]{1,0:T(8,128)(2,1)S(1)}, u32[]{:S(2)}) %copy-start) | copy-done | bytes 4194328
  28.1 4.1 %collective-permute-start.2 = (f32[4,512]{1,0:T(4,128)S(1)}, f32[4,512]{1,0:T(4,128)S(1)}, u32[]{:S(2)}, u32[]{:S(2)}) collective-permute-start(f32[4,512]{1,0:T(4,128)S(1)} %pad_maximum_fusion.1), channel_id=1, source_target_pairs={{0,4},{4,0},{8,12},{12,8},{1,5},{5,1},{9,13},{13,9},{2,6},{6,2},{1... | collective-permute-start | bytes 24584 | tf_op jit(solution)/shard_map/ppermute | solution.py:19
  32.8 9.6 %collective-permute-done.2.sa_ref = f32[4,512]{1,0:T(4,128)S(1)} collective-permute-done((f32[4,512]{1,0:T(4,128)S(1)}, f32[4,512]{1,0:T(4,128)S(1)}, u32[]{:S(2)}, u32[]{:S(2)}) %collective-permute-start.2) | collective-permute-done | bytes 8224 | tf_op jit(solution)/shard_map/ppermute | solution.py:19
  44.9 2.2 %copy-done.3 = bf16[4096,512]{1,0:T(8,128)(2,1)S(1)} copy-done((bf16[4096,512]{1,0:T(8,128)(2,1)S(1)}, bf16[4096,512]{1,0:T(8,128)(2,1)}, u32[]{:S(2)}) %copy-start.3) | copy-done | bytes 4194328
  48.3 6.0 %collective-permute-start.10 = (bf16[2048,128]{1,0:T(8,128)(2,1)S(1)}, bf16[2048,128]{1,0:T(8,128)(2,1)S(1)}, u32[]{:S(2)}, u32[]{:S(2)}) collective-permute-start(bf16[2048,128]{1,0:T(8,128)(2,1)S(1)} %get-tuple-element.50), channel_id=1, source_target_pairs={{0,4},{4,0},{8,12},{12,8},{1,5},{5,1},{9,13},{13,9},{2,6},{6,2},{1... | collective-permute-start | bytes 1572872 | tf_op jit(solution)/shard_map/ppermute | solution.py:19
  58.1 5.9 %collective-permute-start.12 = (bf16[2048,128]{1,0:T(8,128)(2,1)S(1)}, bf16[2048,128]{1,0:T(8,128)(2,1)S(1)}, u32[]{:S(2)}, u32[]{:S(2)}) collective-permute-start(bf16[2048,128]{1,0:T(8,128)(2,1)S(1)} %get-tuple-element.53), channel_id=1, source_target_pairs={{0,4},{4,0},{8,12},{12,8},{1,5},{5,1},{9,13},{13,9},{2,6},{6,2},{1... | collective-permute-start | bytes 1572872 | tf_op jit(solution)/shard_map/ppermute | solution.py:19
  64.1 4.6 %collective-permute-done.10.a_ref = bf16[2048,128]{1,0:T(8,128)(2,1)S(1)} collective-permute-done((bf16[2048,128]{1,0:T(8,128)(2,1)S(1)}, bf16[2048,128]{1,0:T(8,128)(2,1)S(1)}, u32[]{:S(2)}, u32[]{:S(2)}) %collective-permute-start.10) | collective-permute-done | bytes 524320 | tf_op jit(solution)/shard_map/ppermute | solution.py:19
  70.8 4.7 %collective-permute-start.14 = (bf16[2048,128]{1,0:T(8,128)(2,1)S(1)}, bf16[2048,128]{1,0:T(8,128)(2,1)S(1)}, u32[]{:S(2)}, u32[]{:S(2)}) collective-permute-start(bf16[2048,128]{1,0:T(8,128)(2,1)S(1)} %get-tuple-element.57), channel_id=1, source_target_pairs={{0,4},{4,0},{8,12},{12,8},{1,5},{5,1},{9,13},{13,9},{2,6},{6,2},{1... | collective-permute-start | bytes 1572872 | tf_op jit(solution)/shard_map/ppermute | solution.py:19
  75.5 4.4 %collective-permute-done.12.a_ref = bf16[2048,128]{1,0:T(8,128)(2,1)S(1)} collective-permute-done((bf16[2048,128]{1,0:T(8,128)(2,1)S(1)}, bf16[2048,128]{1,0:T(8,128)(2,1)S(1)}, u32[]{:S(2)}, u32[]{:S(2)}) %collective-permute-start.12) | collective-permute-done | bytes 524320 | tf_op jit(solution)/shard_map/ppermute | solution.py:19
  81.9 4.6 %collective-permute-start.4 = (bf16[2048,128]{1,0:T(8,128)(2,1)S(1)}, bf16[2048,128]{1,0:T(8,128)(2,1)S(1)}, u32[]{:S(2)}, u32[]{:S(2)}) collective-permute-start(bf16[2048,128]{1,0:T(8,128)(2,1)S(1)} %get-tuple-element.43), channel_id=1, source_target_pairs={{0,4},{4,0},{8,12},{12,8},{1,5},{5,1},{9,13},{13,9},{2,6},{6,2},{1... | collective-permute-start | bytes 1572872 | tf_op jit(solution)/shard_map/ppermute | solution.py:19
  88.5 3.1 %shard_map.39 = (f32[512,512]{1,0:T(8,128)S(1)}, f32[512,512]{1,0:T(8,128)S(1)}) custom-call(s32[2]{0:T(128)S(1)} %pad_add_fusion.place_ref, f32[4,512]{1,0:T(4,128)S(1)} %collective-permute-done.2.sa_ref, f32[4,512]{1,0:T(4,128)S(1)} %collective-permute-done.3.sb_ref, bf16[512,4096]{1,0:T(8,128)(2,1)S(1)} %copy-done.1, ...), custom_call_target="tpu_custom_call" | custom-call | flops 2147483648 | bytes 10502152 | tf_op jit(solution)/shard_map/pallas_call | solution.py:179
  94.7 1.9 %shard_map.45 = (bf16[2048,128]{1,0:T(8,128)(2,1)S(1)}, bf16[128,2048]{1,0:T(8,128)(2,1)S(1)}, f32[2,288,128]{2,1,0:T(8,128)S(1)}, f32[2,288,128]{2,1,0:T(8,128)S(1)}) custom-call(s32[2]{0:T(128)S(1)} %pad_add_fusion.place_ref, f32[4,512]{1,0:T(4,128)S(1)} %collective-permute-done.2.sa_ref, f32[4,512]{1,0:T(4,128)S(1)} %collective-permute-done.3.sb_ref, ...), custom_call_target="tpu_custom_call" | custom-call | flops 603979776 | bytes 11091976 | tf_op jit(solution)/shard_map/pallas_call | solution.py:179
  96.7 4.0 %collective-permute-done.4.a_ref = bf16[2048,128]{1,0:T(8,128)(2,1)S(1)} collective-permute-done((bf16[2048,128]{1,0:T(8,128)(2,1)S(1)}, bf16[2048,128]{1,0:T(8,128)(2,1)S(1)}, u32[]{:S(2)}, u32[]{:S(2)}) %collective-permute-start.4) | collective-permute-done | bytes 524320 | tf_op jit(solution)/shard_map/ppermute | solution.py:19
  110.1 5.9 %collective-permute-done.19 = f32[160,128]{1,0:T(8,128)S(1)} collective-permute-done((f32[160,128]{1,0:T(8,128)S(1)}, f32[160,128]{1,0:T(8,128)S(1)}, u32[]{:S(2)}, u32[]{:S(2)}) %collective-permute-start.19) | collective-permute-done | bytes 81952 | tf_op jit(solution)/shard_map/ppermute | solution.py:210
  120.1 3.7 %collective-permute-done.23 = f32[288,128]{1,0:T(8,128)S(1)} collective-permute-done((f32[288,128]{1,0:T(8,128)S(1)}, f32[288,128]{1,0:T(8,128)S(1)}, u32[]{:S(2)}, u32[]{:S(2)}) %collective-permute-start.23) | collective-permute-done | bytes 147488 | tf_op jit(solution)/shard_map/ppermute | solution.py:210
  125.3 2.5 %collective-permute-done.26.far0_ref = f32[224,128]{1,0:T(8,128)S(1)} collective-permute-done((f32[224,128]{1,0:T(8,128)S(1)}, f32[224,128]{1,0:T(8,128)S(1)}, u32[]{:S(2)}, u32[]{:S(2)}) %collective-permute-start.26) | collective-permute-done | bytes 114720 | tf_op jit(solution)/shard_map/ppermute | solution.py:290
  127.8 2.6 %collective-permute-done.27.far1_ref = f32[224,128]{1,0:T(8,128)S(1)} collective-permute-done((f32[224,128]{1,0:T(8,128)S(1)}, f32[224,128]{1,0:T(8,128)S(1)}, u32[]{:S(2)}, u32[]{:S(2)}) %collective-permute-start.27) | collective-permute-done | bytes 114720 | tf_op jit(solution)/shard_map/ppermute | solution.py:290
  130.4 8.4 %collective-permute-done.24.early_ref = f32[288,128]{1,0:T(8,128)S(1)} collective-permute-done((f32[288,128]{1,0:T(8,128)S(1)}, f32[288,128]{1,0:T(8,128)S(1)}, u32[]{:S(2)}, u32[]{:S(2)}) %collective-permute-start.24) | collective-permute-done | bytes 147488 | tf_op jit(solution)/shard_map/ppermute | solution.py:278
  (92 shorter events, 36.8 us)
Async XLA Ops:
  4.6 77.3 %collective-permute-start.8 = (bf16[1536,512]{1,0:T(8,128)(2,1)}, bf16[1536,512]{1,0:T(8,128)(2,1)S(1)}, u32[]{:S(2)}, u32[]{:S(2)}) collective-permute-start(bf16[1536,512]{1,0:T(8,128)(2,1)} %slice.49), channel_id=1, source_target_pairs={{0,4},{4,0},{8,12},{12,8},{1,5},{5,1},{9,13},{13,9},{2,6},{6,2},{1... | collective-permute-start | bytes 4718600 | tf_op jit(solution)/shard_map/ppermute | solution.py:19
  7.6 78.8 %collective-permute-start.9 = (bf16[1536,512]{1,0:T(8,128)(2,1)}, bf16[1536,512]{1,0:T(8,128)(2,1)S(1)}, u32[]{:S(2)}, u32[]{:S(2)}) collective-permute-start(bf16[1536,512]{1,0:T(8,128)(2,1)} %slice.49), channel_id=1, source_target_pairs={{4,8},{8,4},{5,9},{9,5},{6,10},{10,6},{7,11},{11,7},{20,24},{24,20... | collective-permute-start | bytes 4718600 | tf_op jit(solution)/shard_map/ppermute | solution.py:19
  27.8 20.5 %collective-permute-start = (f32[2,128,512]{2,1,0:T(8,128)}, f32[2,128,512]{2,1,0:T(8,128)}, u32[]{:S(2)}, u32[]{:S(2)}) collective-permute-start(f32[2,128,512]{2,1,0:T(8,128)} %get-tuple-element.42), channel_id=1, source_target_pairs={{0,1},{1,0},{2,3},{3,2},{4,5},{5,4},{6,7},{7,6},{8,9},{9,8},{10,11... | collective-permute-start | bytes 1572872 | tf_op jit(solution)/shard_map/ppermute | solution.py:210
  28.1 14.3 %collective-permute-start.2 = (f32[4,512]{1,0:T(4,128)S(1)}, f32[4,512]{1,0:T(4,128)S(1)}, u32[]{:S(2)}, u32[]{:S(2)}) collective-permute-start(f32[4,512]{1,0:T(4,128)S(1)} %pad_maximum_fusion.1), channel_id=1, source_target_pairs={{0,4},{4,0},{8,12},{12,8},{1,5},{5,1},{9,13},{13,9},{2,6},{6,2},{1... | collective-permute-start | bytes 24584 | tf_op jit(solution)/shard_map/ppermute | solution.py:19
  32.2 12.0 %collective-permute-start.3 = (f32[4,512]{1,0:T(4,128)S(1)}, f32[4,512]{1,0:T(4,128)S(1)}, u32[]{:S(2)}, u32[]{:S(2)}) collective-permute-start(f32[4,512]{1,0:T(4,128)S(1)} %pad_maximum_fusion.1), channel_id=1, source_target_pairs={{4,8},{8,4},{5,9},{9,5},{6,10},{10,6},{7,11},{11,7},{20,24},{24,20... | collective-permute-start | bytes 24584 | tf_op jit(solution)/shard_map/ppermute | solution.py:19
  42.4 15.0 %collective-permute-start.6 = (bf16[512,512]{1,0:T(8,128)(2,1)}, bf16[512,512]{1,0:T(8,128)(2,1)S(1)}, u32[]{:S(2)}, u32[]{:S(2)}) collective-permute-start(bf16[512,512]{1,0:T(8,128)(2,1)} %slice.48), channel_id=1, source_target_pairs={{0,4},{4,0},{8,12},{12,8},{1,5},{5,1},{9,13},{13,9},{2,6},{6,2},{1... | collective-permute-start | bytes 1572872 | tf_op jit(solution)/shard_map/ppermute | solution.py:19
  44.2 14.0 %collective-permute-start.7 = (bf16[512,512]{1,0:T(8,128)(2,1)}, bf16[512,512]{1,0:T(8,128)(2,1)S(1)}, u32[]{:S(2)}, u32[]{:S(2)}) collective-permute-start(bf16[512,512]{1,0:T(8,128)(2,1)} %slice.48), channel_id=1, source_target_pairs={{4,8},{8,4},{5,9},{9,5},{6,10},{10,6},{7,11},{11,7},{20,24},{24,20... | collective-permute-start | bytes 1572872 | tf_op jit(solution)/shard_map/ppermute | solution.py:19
  48.3 20.3 %collective-permute-start.10 = (bf16[2048,128]{1,0:T(8,128)(2,1)S(1)}, bf16[2048,128]{1,0:T(8,128)(2,1)S(1)}, u32[]{:S(2)}, u32[]{:S(2)}) collective-permute-start(bf16[2048,128]{1,0:T(8,128)(2,1)S(1)} %get-tuple-element.50), channel_id=1, source_target_pairs={{0,4},{4,0},{8,12},{12,8},{1,5},{5,1},{9,13},{13,9},{2,6},{6,2},{1... | collective-permute-start | bytes 1572872 | tf_op jit(solution)/shard_map/ppermute | solution.py:19
  57.4 13.3 %collective-permute-start.11 = (bf16[2048,128]{1,0:T(8,128)(2,1)S(1)}, bf16[2048,128]{1,0:T(8,128)(2,1)S(1)}, u32[]{:S(2)}, u32[]{:S(2)}) collective-permute-start(bf16[2048,128]{1,0:T(8,128)(2,1)S(1)} %get-tuple-element.51), channel_id=1, source_target_pairs={{4,8},{8,4},{5,9},{9,5},{6,10},{10,6},{7,11},{11,7},{20,24},{24,20... | collective-permute-start | bytes 1572872 | tf_op jit(solution)/shard_map/ppermute | solution.py:19
  58.1 21.8 %collective-permute-start.12 = (bf16[2048,128]{1,0:T(8,128)(2,1)S(1)}, bf16[2048,128]{1,0:T(8,128)(2,1)S(1)}, u32[]{:S(2)}, u32[]{:S(2)}) collective-permute-start(bf16[2048,128]{1,0:T(8,128)(2,1)S(1)} %get-tuple-element.53), channel_id=1, source_target_pairs={{0,4},{4,0},{8,12},{12,8},{1,5},{5,1},{9,13},{13,9},{2,6},{6,2},{1... | collective-permute-start | bytes 1572872 | tf_op jit(solution)/shard_map/ppermute | solution.py:19
  68.7 24.4 %collective-permute-start.13 = (bf16[2048,128]{1,0:T(8,128)(2,1)S(1)}, bf16[2048,128]{1,0:T(8,128)(2,1)S(1)}, u32[]{:S(2)}, u32[]{:S(2)}) collective-permute-start(bf16[2048,128]{1,0:T(8,128)(2,1)S(1)} %get-tuple-element.54), channel_id=1, source_target_pairs={{4,8},{8,4},{5,9},{9,5},{6,10},{10,6},{7,11},{11,7},{20,24},{24,20... | collective-permute-start | bytes 1572872 | tf_op jit(solution)/shard_map/ppermute | solution.py:19
  70.8 23.9 %collective-permute-start.14 = (bf16[2048,128]{1,0:T(8,128)(2,1)S(1)}, bf16[2048,128]{1,0:T(8,128)(2,1)S(1)}, u32[]{:S(2)}, u32[]{:S(2)}) collective-permute-start(bf16[2048,128]{1,0:T(8,128)(2,1)S(1)} %get-tuple-element.57), channel_id=1, source_target_pairs={{0,4},{4,0},{8,12},{12,8},{1,5},{5,1},{9,13},{13,9},{2,6},{6,2},{1... | collective-permute-start | bytes 1572872 | tf_op jit(solution)/shard_map/ppermute | solution.py:19
  79.9 14.8 %collective-permute-start.15 = (bf16[2048,128]{1,0:T(8,128)(2,1)S(1)}, bf16[2048,128]{1,0:T(8,128)(2,1)S(1)}, u32[]{:S(2)}, u32[]{:S(2)}) collective-permute-start(bf16[2048,128]{1,0:T(8,128)(2,1)S(1)} %get-tuple-element.58), channel_id=1, source_target_pairs={{4,8},{8,4},{5,9},{9,5},{6,10},{10,6},{7,11},{11,7},{20,24},{24,20... | collective-permute-start | bytes 1572872 | tf_op jit(solution)/shard_map/ppermute | solution.py:19
  81.9 18.8 %collective-permute-start.4 = (bf16[2048,128]{1,0:T(8,128)(2,1)S(1)}, bf16[2048,128]{1,0:T(8,128)(2,1)S(1)}, u32[]{:S(2)}, u32[]{:S(2)}) collective-permute-start(bf16[2048,128]{1,0:T(8,128)(2,1)S(1)} %get-tuple-element.43), channel_id=1, source_target_pairs={{0,4},{4,0},{8,12},{12,8},{1,5},{5,1},{9,13},{13,9},{2,6},{6,2},{1... | collective-permute-start | bytes 1572872 | tf_op jit(solution)/shard_map/ppermute | solution.py:19
  86.5 14.2 %collective-permute-start.5 = (bf16[2048,128]{1,0:T(8,128)(2,1)S(1)}, bf16[2048,128]{1,0:T(8,128)(2,1)S(1)}, u32[]{:S(2)}, u32[]{:S(2)}) collective-permute-start(bf16[2048,128]{1,0:T(8,128)(2,1)S(1)} %get-tuple-element.44), channel_id=1, source_target_pairs={{4,8},{8,4},{5,9},{9,5},{6,10},{10,6},{7,11},{11,7},{20,24},{24,20... | collective-permute-start | bytes 1572872 | tf_op jit(solution)/shard_map/ppermute | solution.py:19
  103.5 21.7 %collective-permute-start.1 = (f32[128,512]{1,0:T(8,128)S(1)}, f32[128,512]{1,0:T(8,128)S(1)}, u32[]{:S(2)}, u32[]{:S(2)}) collective-permute-start(f32[128,512]{1,0:T(8,128)S(1)} %slice_bitcast_fusion), channel_id=1, source_target_pairs={{0,2},{1,3},{2,0},{3,1},{4,6},{5,7},{6,4},{7,5},{8,10},{9,11},{10,... | collective-permute-start | bytes 786440 | tf_op jit(solution)/shard_map/ppermute | solution.py:210
  105.0 12.3 %collective-permute-start.22 = (f32[2,288,128]{2,1,0:T(8,128)S(1)}, f32[2,288,128]{2,1,0:T(8,128)S(1)}, u32[]{:S(2)}, u32[]{:S(2)}) collective-permute-start(f32[2,288,128]{2,1,0:T(8,128)S(1)} %get-tuple-element.70), channel_id=1, source_target_pairs={{0,1},{1,0},{2,3},{3,2},{4,5},{5,4},{6,7},{7,6},{8,9},{9,8},{10,11... | collective-permute-start | bytes 884744 | tf_op jit(solution)/shard_map/ppermute | solution.py:210
  107.1 18.1 %collective-permute-start.17 = (f32[128,128]{1,0:T(8,128)S(1)}, f32[128,128]{1,0:T(8,128)S(1)}, u32[]{:S(2)}, u32[]{:S(2)}) collective-permute-start(f32[128,128]{1,0:T(8,128)S(1)} %slice_bitcast_fusion.10), channel_id=1, source_target_pairs={{0,2},{1,3},{2,0},{3,1},{4,6},{5,7},{6,4},{7,5},{8,10},{9,11},{10,... | collective-permute-start | bytes 196616 | tf_op jit(solution)/shard_map/ppermute | solution.py:210
  107.8 8.1 %collective-permute-start.19 = (f32[160,128]{1,0:T(8,128)S(1)}, f32[160,128]{1,0:T(8,128)S(1)}, u32[]{:S(2)}, u32[]{:S(2)}) collective-permute-start(f32[160,128]{1,0:T(8,128)S(1)} %slice_bitcast_fusion.8), channel_id=1, source_target_pairs={{0,2},{1,3},{2,0},{3,1},{4,6},{5,7},{6,4},{7,5},{8,10},{9,11},{10,... | collective-permute-start | bytes 245768 | tf_op jit(solution)/shard_map/ppermute | solution.py:210
  109.3 9.3 %collective-permute-start.21 = (f32[224,128]{1,0:T(8,128)S(1)}, f32[224,128]{1,0:T(8,128)S(1)}, u32[]{:S(2)}, u32[]{:S(2)}) collective-permute-start(f32[224,128]{1,0:T(8,128)S(1)} %slice_bitcast_fusion.6), channel_id=1, source_target_pairs={{0,2},{1,3},{2,0},{3,1},{4,6},{5,7},{6,4},{7,5},{8,10},{9,11},{10,... | collective-permute-start | bytes 344072 | tf_op jit(solution)/shard_map/ppermute | solution.py:210
  115.9 11.8 %collective-permute-start.26 = (f32[224,128]{1,0:T(8,128)S(1)}, f32[224,128]{1,0:T(8,128)S(1)}, u32[]{:S(2)}, u32[]{:S(2)}) collective-permute-start(f32[224,128]{1,0:T(8,128)S(1)} %get-tuple-element.78), channel_id=1, source_target_pairs={{4,0},{5,1},{6,2},{7,3},{8,4},{9,5},{10,6},{11,7},{20,16},{21,17},... | collective-permute-start | bytes 344072 | tf_op jit(solution)/shard_map/ppermute | solution.py:290
  117.3 13.1 %collective-permute-start.27 = (f32[224,128]{1,0:T(8,128)S(1)}, f32[224,128]{1,0:T(8,128)S(1)}, u32[]{:S(2)}, u32[]{:S(2)}) collective-permute-start(f32[224,128]{1,0:T(8,128)S(1)} %get-tuple-element.77), channel_id=1, source_target_pairs={{4,2},{5,3},{6,0},{7,1},{8,6},{9,7},{10,4},{11,5},{20,18},{21,19},... | collective-permute-start | bytes 344072 | tf_op jit(solution)/shard_map/ppermute | solution.py:290
  118.6 5.2 %collective-permute-start.23 = (f32[288,128]{1,0:T(8,128)S(1)}, f32[288,128]{1,0:T(8,128)S(1)}, u32[]{:S(2)}, u32[]{:S(2)}) collective-permute-start(f32[288,128]{1,0:T(8,128)S(1)} %slice_bitcast_fusion.2), channel_id=1, source_target_pairs={{0,2},{1,3},{2,0},{3,1},{4,6},{5,7},{6,4},{7,5},{8,10},{9,11},{10,... | collective-permute-start | bytes 442376 | tf_op jit(solution)/shard_map/ppermute | solution.py:210
  123.9 14.9 %collective-permute-start.24 = (f32[288,128]{1,0:T(8,128)S(1)}, f32[288,128]{1,0:T(8,128)S(1)}, u32[]{:S(2)}, u32[]{:S(2)}) collective-permute-start(f32[288,128]{1,0:T(8,128)S(1)} %pad_maximum_fusion), channel_id=1, source_target_pairs={{4,0},{8,4},{5,1},{9,5},{6,2},{10,6},{7,3},{11,7},{20,16},{24,20},... | collective-permute-start | bytes 442376 | tf_op jit(solution)/shard_map/ppermute | solution.py:278
  (12 other events, 97.2 us)
